TPU v7x, 32 devices: a whole 2x2x4 slice. The times are simulated.
32 devices in a mesh: fsdp: 8 (over y, x, core), tp: 4 (over z).
Axes of the slice: x: 2, y: 2, z: 4, core: 2. Of those that a mesh axis runs over, the one named last changes fastest.
Arguments:
- residual: bfloat16 [8192, 2048], P(('fsdp', 'tp')), may hold values from -6 to 6
- query_weight: bfloat16 [2048, 2048], P('fsdp', 'tp'), may hold values from -0.125 to 0.125
- key_weight: bfloat16 [2048, 2048], P('fsdp', 'tp'), may hold values from -0.125 to 0.125
- value_weight: bfloat16 [2048, 2048], P('fsdp', 'tp'), may hold values from -0.125 to 0.125
- out_weight: bfloat16 [2048, 2048], P('tp', 'fsdp'), may hold values from -2 to 2
- query_gain: bfloat16 [16, 128], P('tp', 'fsdp'), may hold values from 0.5 to 1.5
- key_gain: bfloat16 [16, 128], P('tp', 'fsdp'), may hold values from 0.5 to 1.5
- attn_gain: bfloat16 [2048], P('fsdp'), may hold values from 0.5 to 1.5
- mlp_gain: bfloat16 [2048], P('fsdp'), may hold values from 0.5 to 1.5
- router_weight: bfloat16 [2048, 16], P('fsdp'), may hold values from -0.09375 to 0.09375
- gate_weight: bfloat16 [16, 2048, 1024], P(None, 'fsdp', 'tp'), may hold values from -0.125 to 0.125
- up_weight: bfloat16 [16, 2048, 1024], P(None, 'fsdp', 'tp'), may hold values from -0.125 to 0.125
- down_weight: bfloat16 [16, 1024, 2048], P(None, 'tp', 'fsdp'), may hold values from -1.5 to 1.5
- routes: int32 [8192, 8], P('fsdp'), may hold values from 0 to 15, all different within a row
- route_order: int32 [8, 8192], P('fsdp'), may hold values from 0 to 8191, each once within a row
- seg_ids: int32 [8192], P('fsdp'), may hold values from 0 to 8, as said below
- cotangent: bfloat16 [8192, 2048], P(('fsdp', 'tp')), may hold values from -6 to 6
Outputs:
- block_out: float32 [8192, 2048], P(('fsdp', 'tp'))
- grad_input: float32 [8192, 2048], P(('fsdp', 'tp'))
- grad_query: float32 [2048, 2048], P('fsdp', 'tp')
- grad_key: float32 [2048, 2048], P('fsdp', 'tp')
- grad_value: float32 [2048, 2048], P('fsdp', 'tp')
- grad_out_proj: float32 [2048, 2048], P('tp', 'fsdp')
- grad_query_gain: float32 [16, 128], P('tp', 'fsdp')
- grad_key_gain: float32 [16, 128], P('tp', 'fsdp')
- grad_attn_gain: float32 [2048], P('fsdp')
- grad_mlp_gain: float32 [2048], P('fsdp')
- grad_router: float32 [2048, 16], P('fsdp')
- grad_gate: float32 [16, 2048, 1024], P(None, 'fsdp', 'tp')
- grad_up: float32 [16, 2048, 1024], P(None, 'fsdp', 'tp')
- grad_down: float32 [16, 1024, 2048], P(None, 'tp', 'fsdp')
Inputs may be any that keep to these rules, and one draw needn't show every extreme that they name: `routes`: each row names 8 different experts. `route_order`: each row is a permutation of the 8192 pairs of one block; pair p is token p // 8 of the block with its route p % 8. `seg_ids`: the first half of the blocks hold prompts (all 0); block g + 4 holds the 8 continuations of prompt g with ids 1 to 8 in order, each of 64 to 192 tokens, one exactly 192.
All inputs are finite; a program needn't handle non-finite values.
Results may differ from a plain program's by a relative error of at most 0.017.
Values may be sent and summed in bfloat16 or wider, within the bound.
No kernel may reach another device: no remote copies, remote signals or barrier semaphores. Data moves between devices by JAX's collectives and lax.ppermute only.
A program may use at most 256 MiB of HBM per device.

v0:
```python
import math

import jax
import jax.numpy as jnp
from jax import lax
from jax.sharding import PartitionSpec as P

HEAD_DIM = 128
TOPK = 8
EXPERTS = 16
TOK_DEV = 1024
CONTS = 8
CAP = 512


EPS = 1e-05
NEG = -1e30
HIGH = lax.Precision.HIGHEST


def passed_along(value, axis, steps):
    count = lax.axis_size(axis)
    first, last = (max(0, -steps), min(count, count - steps))
    return lax.ppermute(value, axis, [(source, source + steps) for source in range(first, last)])


def norm_scale(values):
    return lax.rsqrt(jnp.mean(values * values, axis=-1, keepdims=True) + EPS)


def rope_angles(seg_block):
    row_count = seg_block.shape[0]
    labels = jnp.arange(CONTS + 1, dtype=jnp.int32)
    member = (seg_block[:, None] == labels[None, :]).astype(jnp.int32)
    counts = jnp.sum(member, axis=0)
    starts = jnp.cumsum(counts) - counts
    seg_start = jnp.sum(member * starts[None, :], axis=1)
    offset = TOK_DEV * (seg_block != 0).astype(jnp.int32)
    places = jnp.arange(row_count, dtype=jnp.int32) - seg_start + offset
    half_dim = HEAD_DIM // 2
    frequency = jnp.exp(
        jnp.arange(half_dim, dtype=jnp.float32) * (-2.0 * math.log(10000.0) / HEAD_DIM)
    )
    angles = places.astype(jnp.float32)[:, None] * frequency[None, :]
    return (jnp.cos(angles), jnp.sin(angles))


def rotate(values, cosines, sines):
    row_count = values.shape[0]
    by_head = values.reshape(row_count, -1, HEAD_DIM)
    half_dim = HEAD_DIM // 2
    first_half = by_head[..., :half_dim]
    second_half = by_head[..., half_dim:]
    cos_wide = cosines[:, None, :]
    sin_wide = sines[:, None, :]
    turned = jnp.concatenate(
        [
            first_half * cos_wide - second_half * sin_wide,
            second_half * cos_wide + first_half * sin_wide,
        ],
        axis=-1,
    )
    return turned.reshape(row_count, -1)


def unrotate(values, cosines, sines):
    row_count = values.shape[0]
    by_head = values.reshape(row_count, -1, HEAD_DIM)
    half_dim = HEAD_DIM // 2
    first_half = by_head[..., :half_dim]
    second_half = by_head[..., half_dim:]
    cos_wide = cosines[:, None, :]
    sin_wide = sines[:, None, :]
    turned = jnp.concatenate(
        [
            first_half * cos_wide + second_half * sin_wide,
            second_half * cos_wide - first_half * sin_wide,
        ],
        axis=-1,
    )
    return turned.reshape(row_count, -1)


def route_tables(block_routes, block_order):
    expert_count = EXPERTS
    pair_expert = block_routes.reshape(-1)
    placed = pair_expert[block_order]
    member = (placed[:, None] == jnp.arange(expert_count, dtype=jnp.int32)[None, :]).astype(
        jnp.int32
    )
    pair_rank = jnp.sum(member * jnp.cumsum(member, axis=0), axis=1) - 1
    target = jnp.where(pair_rank < CAP, placed * CAP + pair_rank, expert_count * CAP)
    slot_of_pair = jnp.zeros_like(pair_expert).at[block_order].set(target)
    token_of_slot = (
        jnp.full((expert_count * CAP + 1,), block_routes.shape[0], jnp.int32)
        .at[target]
        .set(block_order // TOPK)
    )
    return (slot_of_pair, token_of_slot[: expert_count * CAP], target)


def rows_gather(values):
    return lax.all_gather(values, "tp", axis=0, tiled=True)


def rows_scatter(values):
    return lax.psum_scatter(values, "tp", scatter_dimension=0, tiled=True)


def head_totals(first_sum, second_sum):
    return lax.psum((first_sum, second_sum), "tp")


def visible_block(seg_rows, row_ids, seg_all):
    columns = jnp.arange(seg_all.shape[0], dtype=jnp.int32)
    own_keys = (seg_all[None, :] == seg_rows[:, None]) & (columns[None, :] <= row_ids[:, None])
    prompt_keys = jnp.broadcast_to((seg_rows != 0)[:, None], own_keys.shape)
    return jnp.concatenate([prompt_keys, own_keys], axis=1)


def block_scores(query_blk, key_head, seg_rows, row_ids, seg_all):
    raw_scores = lax.dot_general(
        query_blk, key_head, (((1,), (1,)), ((), ())), preferred_element_type=jnp.float32
    )
    raw_scores = raw_scores * HEAD_DIM ** (-0.5)
    return jnp.where(visible_block(seg_rows, row_ids, seg_all), raw_scores, NEG)


def head_forward(query_head, key_head, value_head, seg_all, block_rows):
    row_count = query_head.shape[0]
    block_count = row_count // block_rows
    block_inputs = (
        query_head.reshape(block_count, block_rows, -1),
        seg_all.reshape(block_count, block_rows),
        jnp.arange(row_count, dtype=jnp.int32).reshape(block_count, block_rows),
    )

    def one_block(block_items):
        query_blk, seg_rows, row_ids = block_items
        scores = block_scores(query_blk, key_head, seg_rows, row_ids, seg_all)
        row_peak = jnp.max(scores, axis=-1, keepdims=True)
        exp_scores = jnp.exp(scores - row_peak)
        row_total = jnp.sum(exp_scores, axis=-1, keepdims=True)
        attn_probs = exp_scores / row_total
        attended = jnp.dot(
            attn_probs.astype(jnp.bfloat16), value_head, preferred_element_type=jnp.float32
        )
        return (attended.astype(jnp.bfloat16), (row_peak + jnp.log(row_total))[:, 0])

    attended, log_total = lax.map(one_block, block_inputs)
    return (attended.reshape(row_count, -1), log_total.reshape(row_count))


def head_backward(query_head, key_head, value_head, grad_head, log_total, seg_all, block_rows):
    row_count = query_head.shape[0]
    block_count = row_count // block_rows
    block_inputs = (
        query_head.reshape(block_count, block_rows, -1),
        grad_head.reshape(block_count, block_rows, -1),
        log_total.reshape(block_count, block_rows),
        seg_all.reshape(block_count, block_rows),
        jnp.arange(row_count, dtype=jnp.int32).reshape(block_count, block_rows),
    )
    score_scale = HEAD_DIM ** (-0.5)

    def one_block(loop_state, block_items):
        key_grad, value_grad = loop_state
        query_blk, grad_blk, total_blk, seg_rows, row_ids = block_items
        scores = block_scores(query_blk, key_head, seg_rows, row_ids, seg_all)
        attn_probs = jnp.exp(scores - total_blk[:, None])
        grad_probs = lax.dot_general(
            grad_blk, value_head, (((1,), (1,)), ((), ())), preferred_element_type=jnp.float32
        )
        grad_scores = (
            attn_probs * (grad_probs - jnp.sum(attn_probs * grad_probs, axis=-1, keepdims=True))
        ).astype(jnp.bfloat16)
        query_grad = (
            jnp.dot(grad_scores, key_head, preferred_element_type=jnp.float32) * score_scale
        )
        key_grad = (
            key_grad
            + lax.dot_general(
                grad_scores, query_blk, (((0,), (0,)), ((), ())), preferred_element_type=jnp.float32
            )
            * score_scale
        )
        value_grad = value_grad + lax.dot_general(
            attn_probs.astype(jnp.bfloat16),
            grad_blk,
            (((0,), (0,)), ((), ())),
            preferred_element_type=jnp.float32,
        )
        return ((key_grad, value_grad), query_grad)

    zero_keys = jnp.zeros(key_head.shape, jnp.float32)
    (key_grad, value_grad), query_grad = lax.scan(one_block, (zero_keys, zero_keys), block_inputs)
    return (query_grad.reshape(row_count, -1), key_grad, value_grad)


def on_device(
    residual,
    query_weight,
    key_weight,
    value_weight,
    out_weight,
    query_gain,
    key_gain,
    attn_gain,
    mlp_gain,
    router_weight,
    gate_weight,
    up_weight,
    down_weight,
    routes,
    route_order,
    seg_ids,
    cotangent,
):
    fetched = (
        lax.all_gather(query_weight, "fsdp", axis=0, tiled=True),
        lax.all_gather(key_weight, "fsdp", axis=0, tiled=True),
        lax.all_gather(value_weight, "fsdp", axis=0, tiled=True),
        lax.all_gather(out_weight, "fsdp", axis=1, tiled=True),
        lax.all_gather(query_gain, "fsdp", axis=1, tiled=True),
        lax.all_gather(key_gain, "fsdp", axis=1, tiled=True),
        lax.all_gather(attn_gain, "fsdp", axis=0, tiled=True),
        lax.all_gather(mlp_gain, "fsdp", axis=0, tiled=True),
        lax.all_gather(router_weight, "fsdp", axis=0, tiled=True),
    )
    (
        query_mat,
        key_mat,
        value_mat,
        out_mat,
        query_gains,
        key_gains,
        attn_gains,
        mlp_gains,
        router_mat,
    ) = fetched
    model_dim = residual.shape[1]
    tok_count = seg_ids.shape[0]
    head_local = query_mat.shape[1] // HEAD_DIM
    block_rows = min(512, tok_count)
    half_axis = lax.axis_size("fsdp") // 2
    stream = residual.astype(jnp.float32)
    norm_first = norm_scale(stream)
    attn_gain_f = attn_gains.astype(jnp.float32)
    normed = (stream * norm_first * attn_gain_f).astype(jnp.bfloat16)
    normed_all = rows_gather(normed)
    query_raw = jnp.dot(normed_all, query_mat, preferred_element_type=jnp.float32)
    key_raw = jnp.dot(normed_all, key_mat, preferred_element_type=jnp.float32)
    value_raw = jnp.dot(normed_all, value_mat, preferred_element_type=jnp.float32)
    query_total, key_total = head_totals(
        jnp.sum(query_raw * query_raw, axis=1), jnp.sum(key_raw * key_raw, axis=1)
    )
    norm_query = lax.rsqrt(query_total / model_dim + EPS)[:, None]
    norm_key = lax.rsqrt(key_total / model_dim + EPS)[:, None]
    query_gain_f = query_gains.astype(jnp.float32).reshape(-1)
    key_gain_f = key_gains.astype(jnp.float32).reshape(-1)
    cosines, sines = rope_angles(seg_ids)
    query_rot = rotate(query_raw * norm_query * query_gain_f, cosines, sines).astype(jnp.bfloat16)
    key_rot = rotate(key_raw * norm_key * key_gain_f, cosines, sines).astype(jnp.bfloat16)
    value_low = value_raw.astype(jnp.bfloat16)
    remote = passed_along(jnp.stack([key_rot, value_low]), "fsdp", half_axis)
    keys_all = jnp.concatenate([remote[0], key_rot], axis=0)
    values_all = jnp.concatenate([remote[1], value_low], axis=0)
    attended_parts = []
    total_parts = []
    for head_num in range(head_local):
        first_col = head_num * HEAD_DIM
        last_col = first_col + HEAD_DIM
        attended_head, total_head = head_forward(
            query_rot[:, first_col:last_col],
            keys_all[:, first_col:last_col],
            values_all[:, first_col:last_col],
            seg_ids,
            block_rows,
        )
        attended_parts.append(attended_head)
        total_parts.append(total_head)
    attended = jnp.concatenate(attended_parts, axis=1)
    attn_part = jnp.dot(attended, out_mat, preferred_element_type=jnp.float32)
    after_attn = stream + rows_scatter(attn_part)
    norm_second = norm_scale(after_attn)
    mlp_gain_f = mlp_gains.astype(jnp.float32)
    normed_mlp = (after_attn * norm_second * mlp_gain_f).astype(jnp.bfloat16)
    mlp_all, upstream = (
        lax.all_gather(normed_mlp, "tp", axis=0, tiled=True),
        lax.all_gather(cotangent, "tp", axis=0, tiled=True),
    )
    expert_count = gate_weight.shape[0]
    logits = jnp.dot(mlp_all, router_mat, preferred_element_type=jnp.float32)
    row_peak = jnp.max(logits, axis=-1, keepdims=True)
    exp_logits = jnp.exp(logits - row_peak)
    router_probs = exp_logits / jnp.sum(exp_logits, axis=-1, keepdims=True)
    route_hot = (
        routes[:, :, None] == jnp.arange(expert_count, dtype=jnp.int32)[None, None, :]
    ).astype(jnp.float32)
    gate_vals = jnp.sum(route_hot * router_probs[:, None, :], axis=2)
    order_row = route_order[0]
    slot_of_pair, token_of_slot, target = route_tables(routes, order_row)
    gate_of_slot = (
        jnp.zeros((expert_count * CAP + 1,), jnp.float32)
        .at[target]
        .set(gate_vals.reshape(-1)[order_row])[: expert_count * CAP]
    )
    mlp_pad = jnp.concatenate([mlp_all, jnp.zeros((1, model_dim), jnp.bfloat16)], axis=0)
    upstream_pad = jnp.concatenate([upstream, jnp.zeros((1, model_dim), jnp.bfloat16)], axis=0)
    group_size = 1
    loop_count = expert_count // group_size
    slot_span = group_size * CAP

    def fetch_weights(step_index):
        first_expert = step_index * group_size
        gate_part = lax.dynamic_slice_in_dim(gate_weight, first_expert, group_size, 0)
        up_part = lax.dynamic_slice_in_dim(up_weight, first_expert, group_size, 0)
        down_part = lax.dynamic_slice_in_dim(down_weight, first_expert, group_size, 0)
        return (
            lax.all_gather(gate_part, "fsdp", axis=1, tiled=True),
            lax.all_gather(up_part, "fsdp", axis=1, tiled=True),
            lax.all_gather(down_part, "fsdp", axis=2, tiled=True),
        )

    def slot_inputs(step_index):
        slot_rows = lax.dynamic_slice_in_dim(token_of_slot, step_index * slot_span, slot_span, 0)
        dispatched = jnp.take(mlp_pad, slot_rows, axis=0).reshape(group_size, CAP, model_dim)
        slot_gates = lax.dynamic_slice_in_dim(gate_of_slot, step_index * slot_span, slot_span, 0)
        upstream_rows = jnp.take(upstream_pad, slot_rows, axis=0).astype(jnp.float32)
        return (slot_rows, dispatched, slot_gates, upstream_rows)

    def forward_step(step_index, loop_state):
        mix_acc, grad_slot, saved_gate, saved_up, held_gate, held_up, held_down = loop_state
        gate_full, up_full, down_full = fetch_weights(step_index)
        slot_rows, dispatched, slot_gates, upstream_rows = slot_inputs(step_index)
        gate_hidden = jnp.einsum(
            "ecd,edf->ecf", dispatched, gate_full, preferred_element_type=jnp.float32
        )
        up_hidden = jnp.einsum(
            "ecd,edf->ecf", dispatched, up_full, preferred_element_type=jnp.float32
        )
        sigmoid_g = 1.0 / (1.0 + jnp.exp(-gate_hidden))
        activation = (gate_hidden * sigmoid_g * up_hidden).astype(jnp.bfloat16)
        expert_out = jnp.einsum(
            "ecf,efd->ecd", activation, down_full, preferred_element_type=jnp.float32
        ).reshape(slot_span, model_dim)
        mix_acc = mix_acc.at[slot_rows].add(expert_out * slot_gates[:, None])
        grad_slot = lax.dynamic_update_slice_in_dim(
            grad_slot, jnp.sum(expert_out * upstream_rows, axis=1), step_index * slot_span, 0
        )
        return (mix_acc, grad_slot, saved_gate, saved_up, held_gate, held_up, held_down)

    saved_shape = (1, 1)
    held_in_shape = (1, 1, 1)
    held_out_shape = (1, 1, 1)
    forward_state = (
        jnp.zeros((tok_count + 1, model_dim), jnp.float32),
        jnp.zeros((expert_count * CAP,), jnp.float32),
        jnp.zeros(saved_shape, jnp.float32),
        jnp.zeros(saved_shape, jnp.float32),
        jnp.zeros(held_in_shape, jnp.bfloat16),
        jnp.zeros(held_in_shape, jnp.bfloat16),
        jnp.zeros(held_out_shape, jnp.bfloat16),
    )
    mix_acc, grad_slot, saved_gate, saved_up, held_gate, held_up, held_down = lax.fori_loop(
        0, loop_count, forward_step, forward_state
    )
    block_out = after_attn + rows_scatter(mix_acc[:tok_count])
    grad_pairs = jnp.concatenate([grad_slot, jnp.zeros((1,), jnp.float32)])[slot_of_pair].reshape(
        tok_count, -1
    )
    grad_probs = jnp.sum(route_hot * grad_pairs[:, :, None], axis=1)
    grad_logits = router_probs * (
        grad_probs - jnp.sum(router_probs * grad_probs, axis=-1, keepdims=True)
    )
    router_term = lax.dot_general(
        mlp_all.astype(jnp.float32), grad_logits, (((0,), (0,)), ((), ())), precision=HIGH
    )
    router_back = lax.dot_general(
        grad_logits, router_mat.astype(jnp.float32), (((1,), (1,)), ((), ())), precision=HIGH
    )

    def backward_step(step_index, loop_state):
        grad_acc, gate_grads, up_grads, down_grads = loop_state
        first_expert = step_index * group_size
        gate_full, up_full, down_full = fetch_weights(step_index)
        slot_rows, dispatched, slot_gates, upstream_rows = slot_inputs(step_index)
        gate_hidden = jnp.einsum(
            "ecd,edf->ecf", dispatched, gate_full, preferred_element_type=jnp.float32
        )
        up_hidden = jnp.einsum(
            "ecd,edf->ecf", dispatched, up_full, preferred_element_type=jnp.float32
        )
        sigmoid_g = 1.0 / (1.0 + jnp.exp(-gate_hidden))
        swish_g = gate_hidden * sigmoid_g
        activation = (swish_g * up_hidden).astype(jnp.bfloat16)
        grad_out = (
            (upstream_rows * slot_gates[:, None])
            .reshape(group_size, CAP, model_dim)
            .astype(jnp.bfloat16)
        )
        grad_act = jnp.einsum(
            "ecd,efd->ecf", grad_out, down_full, preferred_element_type=jnp.float32
        )
        grad_gate_h = (
            grad_act * up_hidden * (sigmoid_g + gate_hidden * sigmoid_g * (1.0 - sigmoid_g))
        ).astype(jnp.bfloat16)
        grad_up_h = (grad_act * swish_g).astype(jnp.bfloat16)
        down_term = jnp.einsum(
            "ecf,ecd->efd", activation, grad_out, preferred_element_type=jnp.float32
        )
        gate_term = jnp.einsum(
            "ecd,ecf->edf", dispatched, grad_gate_h, preferred_element_type=jnp.float32
        )
        up_term = jnp.einsum(
            "ecd,ecf->edf", dispatched, grad_up_h, preferred_element_type=jnp.float32
        )
        grad_disp = jnp.einsum(
            "ecf,edf->ecd", grad_gate_h, gate_full, preferred_element_type=jnp.float32
        )
        grad_disp = grad_disp + jnp.einsum(
            "ecf,edf->ecd", grad_up_h, up_full, preferred_element_type=jnp.float32
        )
        grad_acc = grad_acc.at[slot_rows].add(grad_disp.reshape(slot_span, model_dim))
        gate_share, up_share, down_share = (
            lax.psum_scatter(gate_term, "fsdp", scatter_dimension=1, tiled=True),
            lax.psum_scatter(up_term, "fsdp", scatter_dimension=1, tiled=True),
            lax.psum_scatter(down_term, "fsdp", scatter_dimension=2, tiled=True),
        )
        gate_grads = lax.dynamic_update_slice_in_dim(gate_grads, gate_share, first_expert, 0)
        up_grads = lax.dynamic_update_slice_in_dim(up_grads, up_share, first_expert, 0)
        down_grads = lax.dynamic_update_slice_in_dim(down_grads, down_share, first_expert, 0)
        return (grad_acc, gate_grads, up_grads, down_grads)

    backward_state = (
        jnp.concatenate([router_back, jnp.zeros((1, model_dim), jnp.float32)], axis=0),
        jnp.zeros(gate_weight.shape, jnp.float32),
        jnp.zeros(up_weight.shape, jnp.float32),
        jnp.zeros(down_weight.shape, jnp.float32),
    )
    grad_acc, grad_gate, grad_up, grad_down = lax.fori_loop(
        0, loop_count, backward_step, backward_state
    )
    grad_normed_mlp = rows_scatter(grad_acc[:tok_count])
    hat_two = after_attn * norm_second
    scaled_two = grad_normed_mlp * mlp_gain_f
    mlp_gain_part = jnp.sum(grad_normed_mlp * hat_two, axis=0)
    grad_after = cotangent.astype(jnp.float32) + norm_second * (
        scaled_two - hat_two * jnp.mean(scaled_two * hat_two, axis=-1, keepdims=True)
    )
    grad_attn_all = rows_gather(grad_after.astype(jnp.bfloat16))
    grad_attended = lax.dot_general(
        grad_attn_all, out_mat, (((1,), (1,)), ((), ())), preferred_element_type=jnp.float32
    ).astype(jnp.bfloat16)
    out_term = lax.dot_general(
        attended, grad_attn_all, (((0,), (0,)), ((), ())), preferred_element_type=jnp.float32
    )
    query_grads = []
    key_grads = []
    value_grads = []
    for head_num in range(head_local):
        first_col = head_num * HEAD_DIM
        last_col = first_col + HEAD_DIM
        query_grad, key_grad, value_grad = head_backward(
            query_rot[:, first_col:last_col],
            keys_all[:, first_col:last_col],
            values_all[:, first_col:last_col],
            grad_attended[:, first_col:last_col],
            total_parts[head_num],
            seg_ids,
            block_rows,
        )
        query_grads.append(query_grad)
        key_grads.append(key_grad)
        value_grads.append(value_grad)
    grad_query_rot = jnp.concatenate(query_grads, axis=1)
    key_grad_all = jnp.concatenate(key_grads, axis=1)
    value_grad_all = jnp.concatenate(value_grads, axis=1)
    returned = passed_along(
        jnp.stack([key_grad_all[:tok_count], value_grad_all[:tok_count]]), "fsdp", -half_axis
    )
    grad_key_rot = key_grad_all[tok_count:] + returned[0]
    grad_value_raw = (value_grad_all[tok_count:] + returned[1]).astype(jnp.bfloat16)
    grad_query_normed = unrotate(grad_query_rot, cosines, sines)
    grad_key_normed = unrotate(grad_key_rot, cosines, sines)
    query_gain_part = jnp.sum(grad_query_normed * query_raw * norm_query, axis=0)
    key_gain_part = jnp.sum(grad_key_normed * key_raw * norm_key, axis=0)
    scaled_query = grad_query_normed * query_gain_f
    scaled_key = grad_key_normed * key_gain_f
    query_dot, key_dot = head_totals(
        jnp.sum(scaled_query * query_raw, axis=1), jnp.sum(scaled_key * key_raw, axis=1)
    )
    grad_query_raw = (
        norm_query * scaled_query - query_raw * norm_query**3 * query_dot[:, None] / model_dim
    ).astype(jnp.bfloat16)
    grad_key_raw = (
        norm_key * scaled_key - key_raw * norm_key**3 * key_dot[:, None] / model_dim
    ).astype(jnp.bfloat16)
    query_term = lax.dot_general(
        normed_all, grad_query_raw, (((0,), (0,)), ((), ())), preferred_element_type=jnp.float32
    )
    key_term = lax.dot_general(
        normed_all, grad_key_raw, (((0,), (0,)), ((), ())), preferred_element_type=jnp.float32
    )
    value_term = lax.dot_general(
        normed_all, grad_value_raw, (((0,), (0,)), ((), ())), preferred_element_type=jnp.float32
    )
    grad_normed_part = lax.dot_general(
        grad_query_raw, query_mat, (((1,), (1,)), ((), ())), preferred_element_type=jnp.float32
    )
    grad_normed_part = grad_normed_part + lax.dot_general(
        grad_key_raw, key_mat, (((1,), (1,)), ((), ())), preferred_element_type=jnp.float32
    )
    grad_normed_part = grad_normed_part + lax.dot_general(
        grad_value_raw, value_mat, (((1,), (1,)), ((), ())), preferred_element_type=jnp.float32
    )
    grad_normed = rows_scatter(grad_normed_part)
    hat_one = stream * norm_first
    scaled_one = grad_normed * attn_gain_f
    attn_gain_part = jnp.sum(grad_normed * hat_one, axis=0)
    grad_input = grad_after + norm_first * (
        scaled_one - hat_one * jnp.mean(scaled_one * hat_one, axis=-1, keepdims=True)
    )
    shares = (
        lax.psum_scatter(query_term, "fsdp", scatter_dimension=0, tiled=True),
        lax.psum_scatter(key_term, "fsdp", scatter_dimension=0, tiled=True),
        lax.psum_scatter(value_term, "fsdp", scatter_dimension=0, tiled=True),
        lax.psum_scatter(out_term, "fsdp", scatter_dimension=1, tiled=True),
        lax.psum_scatter(
            query_gain_part.reshape(head_local, HEAD_DIM), "fsdp", scatter_dimension=1, tiled=True
        ),
        lax.psum_scatter(
            key_gain_part.reshape(head_local, HEAD_DIM), "fsdp", scatter_dimension=1, tiled=True
        ),
        lax.psum_scatter(attn_gain_part, "fsdp", scatter_dimension=0, tiled=True),
        lax.psum_scatter(mlp_gain_part, "fsdp", scatter_dimension=0, tiled=True),
        lax.psum_scatter(router_term, "fsdp", scatter_dimension=0, tiled=True),
    )
    (
        grad_query,
        grad_key,
        grad_value,
        grad_out_proj,
        grad_query_gain,
        grad_key_gain,
        attn_share,
        mlp_share,
        router_share,
    ) = shares
    grad_attn_gain, grad_mlp_gain, grad_router = lax.psum(
        (attn_share, mlp_share, router_share), "tp"
    )
    return (
        block_out,
        grad_input,
        grad_query,
        grad_key,
        grad_value,
        grad_out_proj,
        grad_query_gain,
        grad_key_gain,
        grad_attn_gain,
        grad_mlp_gain,
        grad_router,
        grad_gate,
        grad_up,
        grad_down,
    )


def solution(mesh):
    in_specs = (
        P(("fsdp", "tp"), None),
        P("fsdp", "tp"),
        P("fsdp", "tp"),
        P("fsdp", "tp"),
        P("tp", "fsdp"),
        P("tp", "fsdp"),
        P("tp", "fsdp"),
        P("fsdp"),
        P("fsdp"),
        P("fsdp", None),
        P(None, "fsdp", "tp"),
        P(None, "fsdp", "tp"),
        P(None, "tp", "fsdp"),
        P("fsdp", None),
        P("fsdp", None),
        P("fsdp"),
        P(("fsdp", "tp"), None),
    )
    out_specs = (
        P(("fsdp", "tp"), None),
        P(("fsdp", "tp"), None),
        P("fsdp", "tp"),
        P("fsdp", "tp"),
        P("fsdp", "tp"),
        P("tp", "fsdp"),
        P("tp", "fsdp"),
        P("tp", "fsdp"),
        P("fsdp"),
        P("fsdp"),
        P("fsdp", None),
        P(None, "fsdp", "tp"),
        P(None, "fsdp", "tp"),
        P(None, "tp", "fsdp"),
    )
    return jax.shard_map(
        on_device, mesh=mesh, in_specs=in_specs, out_specs=out_specs, check_vma=False
    )
```

profile of v0, /device:TPU:0, one launch (start us, length us, event | category | flops | bytes accessed | tf_op | source)
XLA Modules:
  0.0 6952.4 jit_solution(2564470680469832785)
XLA Ops:
  40.5 82.9 %all-gather.19.cloned.1.call-done = bf16[1024,2048]{1,0:T(8,128)(2,1)} async-done(((bf16[256,2048]{1,0:T(8,128)(2,1)}), bf16[1024,2048]{1,0:T(8,128)(2,1)}) %all-gather.19.cloned.1.call-update) | async-done | bytes 4194320 | tf_op jit(solution)/shard_map/all_gather | solution.py:103
  193.1 56.0 all-gather.1
  349.6 135.7 %reduce-scatter.19.cloned.1.call-done = f32[256,2048]{1,0:T(8,128)} async-done(((f32[1024,2048]{1,0:T(8,128)}), f32[256,2048]{1,0:T(8,128)}) %reduce-scatter.19.cloned.1.call-update) | async-done | bytes 2097168 | tf_op jit(solution)/shard_map/reduce_scatter | solution.py:107
  490.4 45.7 gather_fusion.4
  653.4 45.5 gather_fusion.5
  738.7 1601.2 %while.146 = (s32[]{:T(128)}, f32[1025,2048]{1,0:T(8,128)}, f32[8192]{0:T(1024)S(1)}, s32[8192]{0:T(1024)S(1)}, bf16[1025,2048]{1,0:T(8,128)(2,1)}, /*index=5*/b...) while((s32[]{:T(128)}, f32[1025,2048]{1,0:T(8,128)}, ...), condition=%wide.region_37.39_spmd, body=%wide.region_34.38_spmd.sunk | while | flops 1619791360 | bytes 47091520 | solution.py:365
  2339.9 45.5 gather_fusion.6
  2393.6 3438.0 %while.147 = (s32[]{:T(128)}, f32[1025,2048]{1,0:T(8,128)}, f32[16,256,256]{2,1,0:T(8,128)}, f32[16,256,256]{2,1,0:T(8,128)}, f32[16,256,256]{2,1,0:T(8,128)}, /...) while((s32[]{:T(128)}, f32[1025,2048]{1,0:T(8,128)}, ...), condition=%wide.region_47.49_spmd, body=%wide.region_42.48_spmd.sunk | while | flops 4312010752 | bytes 113412136 | solution.py:441
  2563.8 43.2 reduce-scatter.45.cloned.1.call-done
  2778.6 43.2 reduce-scatter.45.cloned.1.call-done
  3208.6 43.2 reduce-scatter.45.cloned.1.call-done
  4282.3 43.2 reduce-scatter.45.cloned.1.call-done
  4497.5 43.2 reduce-scatter.45.cloned.1.call-done
  4712.0 43.2 reduce-scatter.45.cloned.1.call-done
  4926.9 43.2 reduce-scatter.45.cloned.1.call-done
  5839.5 144.6 %reduce-scatter.23.cloned.1.call-done = f32[256,2048]{1,0:T(8,128)} async-done(((f32[1024,2048]{1,0:T(8,128)}), f32[256,2048]{1,0:T(8,128)}) %reduce-scatter.23.cloned.1.call-update) | async-done | bytes 2097168 | tf_op jit(solution)/shard_map/reduce_scatter | solution.py:107
  5989.4 81.5 %all-gather.33.cloned.1.call-done = bf16[1024,2048]{1,0:T(8,128)(2,1)} async-done(((bf16[256,2048]{1,0:T(8,128)(2,1)}), bf16[1024,2048]{1,0:T(8,128)(2,1)}) %all-gather.33.cloned.1.call-update) | async-done | bytes 4194320 | tf_op jit(solution)/shard_map/all_gather | solution.py:103
  6217.0 89.0 %collective-permute-done.1 = f32[2,1024,512]{2,1,0:T(8,128)} collective-permute-done((f32[2,1024,512]{2,1,0:T(8,128)}, f32[2,1024,512]{2,1,0:T(8,128)}, u32[]{:S(2)}, u32[]{:S(2)}) %collective-permute-start.1) | collective-permute-done | bytes 4194336 | tf_op jit(solution)/shard_map/ppermute | solution.py:24
  6397.5 140.4 %reduce-scatter.25.cloned.1.call-done = f32[256,2048]{1,0:T(8,128)} async-done(((f32[1024,2048]{1,0:T(8,128)}), f32[256,2048]{1,0:T(8,128)}) %reduce-scatter.25.cloned.1.call-update) | async-done | bytes 2097168 | tf_op jit(solution)/shard_map/reduce_scatter | solution.py:107
  6595.7 127.1 %reduce-scatter.21.cloned.1.call-done = f32[256,2048]{1,0:T(8,128)} async-done(((f32[1024,2048]{1,0:T(8,128)}), f32[256,2048]{1,0:T(8,128)}) %reduce-scatter.21.cloned.1.call-update) | async-done | bytes 2097168 | tf_op jit(solution)/shard_map/reduce_scatter | solution.py:107
  6729.1 50.2 reduce-scatter.33.cloned.1.call-done
  6779.3 55.3 reduce-scatter.29.cloned.1.call-done
  6834.6 55.7 reduce-scatter.27.cloned.1.call-done
  6890.3 55.1 reduce-scatter.31.cloned.1.call-done
  (1736 shorter events, 5598.6 us)
Async XLA Ops:
  23.7 128.2 %all-gather.23.cloned.1.call-start = ((), (), s32[]{:S(2)}) async-start(), calls=%async_computation.16 | async-start | bytes 2359296 | tf_op jit(solution)/shard_map/all_gather | solution.py:221
  24.4 157.1 %all-gather.25.cloned.1.call-start = ((), (), s32[]{:S(2)}) async-start(), calls=%async_computation.17 | async-start | bytes 2359296 | tf_op jit(solution)/shard_map/all_gather | solution.py:222
  25.0 306.3 %all-gather.27.cloned.1.call-start = ((), (), s32[]{:S(2)}) async-start(), calls=%async_computation.18 | async-start | bytes 2359296 | tf_op jit(solution)/shard_map/all_gather | solution.py:223
  193.0 292.3 %reduce-scatter.19.cloned.1.call-start = ((), (), s32[]{:S(2)}) async-start(), calls=%async_computation.19 | async-start | bytes 10485760 | tf_op jit(solution)/shard_map/reduce_scatter | solution.py:107
  339.2 273.3 %all-gather.31.cloned.1.call-start = ((), (), s32[]{:S(2)}) async-start(), calls=%async_computation.21 | async-start | bytes 5242880 | tf_op jit(solution)/shard_map/all_gather | solution.py:290
  340.0 309.4 %all-gather.29.cloned.1.call-start = ((), (), s32[]{:S(2)}) async-start(), calls=%async_computation.20 | async-start | bytes 5242880 | tf_op jit(solution)/shard_map/all_gather | solution.py:289
  2480.1 127.0 %reduce-scatter.45.cloned.1.call-start = ((), (), s32[]{:S(2)}) async-start(), calls=%async_computation.41 | async-start | bytes 2359296 | tf_op jit(solution)/shard_map/while/body/eval_jaxpr/reduce_scatter | solution.py:428
  3124.8 127.0 %reduce-scatter.45.cloned.1.call-start = ((), (), s32[]{:S(2)}) async-start(), calls=%async_computation.41 | async-start | bytes 2359296 | tf_op jit(solution)/shard_map/while/body/eval_jaxpr/reduce_scatter | solution.py:428
  3340.0 126.9 %reduce-scatter.45.cloned.1.call-start = ((), (), s32[]{:S(2)}) async-start(), calls=%async_computation.41 | async-start | bytes 2359296 | tf_op jit(solution)/shard_map/while/body/eval_jaxpr/reduce_scatter | solution.py:428
  3554.7 126.9 %reduce-scatter.45.cloned.1.call-start = ((), (), s32[]{:S(2)}) async-start(), calls=%async_computation.41 | async-start | bytes 2359296 | tf_op jit(solution)/shard_map/while/body/eval_jaxpr/reduce_scatter | solution.py:428
  4413.9 126.9 %reduce-scatter.45.cloned.1.call-start = ((), (), s32[]{:S(2)}) async-start(), calls=%async_computation.41 | async-start | bytes 2359296 | tf_op jit(solution)/shard_map/while/body/eval_jaxpr/reduce_scatter | solution.py:428
  5058.3 126.9 %reduce-scatter.45.cloned.1.call-start = ((), (), s32[]{:S(2)}) async-start(), calls=%async_computation.41 | async-start | bytes 2359296 | tf_op jit(solution)/shard_map/while/body/eval_jaxpr/reduce_scatter | solution.py:428
  5273.0 126.9 %reduce-scatter.45.cloned.1.call-start = ((), (), s32[]{:S(2)}) async-start(), calls=%async_computation.41 | async-start | bytes 2359296 | tf_op jit(solution)/shard_map/while/body/eval_jaxpr/reduce_scatter | solution.py:428
  5702.6 126.9 %reduce-scatter.45.cloned.1.call-start = ((), (), s32[]{:S(2)}) async-start(), calls=%async_computation.41 | async-start | bytes 2359296 | tf_op jit(solution)/shard_map/while/body/eval_jaxpr/reduce_scatter | solution.py:428
  5831.5 152.5 %reduce-scatter.23.cloned.1.call-start = ((), (), s32[]{:S(2)}) async-start(), calls=%async_computation.23 | async-start | bytes 10485760 | tf_op jit(solution)/shard_map/reduce_scatter | solution.py:107
  5839.4 231.4 %all-gather.33.cloned.1.call-start = ((), (), s32[]{:S(2)}) async-start(), calls=%async_computation.24 | async-start | bytes 5242880 | tf_op jit(solution)/shard_map/all_gather | solution.py:103
  5989.2 405.5 %reduce-scatter.39.cloned.1.call-start = ((), (), s32[]{:S(2)}) async-start(), calls=%async_computation.32 | async-start | bytes 73728
  6338.5 199.4 %reduce-scatter.25.cloned.1.call-start = ((), (), s32[]{:S(2)}) async-start(), calls=%async_computation.25 | async-start | bytes 10485760 | tf_op jit(solution)/shard_map/reduce_scatter | solution.py:107
  6351.3 224.2 %reduce-scatter.35.cloned.1.call-start = ((), (), s32[]{:S(2)}) async-start(), calls=%async_computation.30 | async-start | bytes 147456 | tf_op jit(solution)/shard_map/reduce_scatter | solution.py:537
  6356.8 366.0 %reduce-scatter.21.cloned.1.call-start = ((), (), s32[]{:S(2)}) async-start(), calls=%async_computation.22 | async-start | bytes 10485760 | tf_op jit(solution)/shard_map/reduce_scatter | solution.py:107
  6364.7 414.6 %reduce-scatter.33.cloned.1.call-start = ((), (), s32[]{:S(2)}) async-start(), calls=%async_computation.29 | async-start | bytes 4718592 | tf_op jit(solution)/shard_map/reduce_scatter | solution.py:528
  6372.4 462.2 %reduce-scatter.29.cloned.1.call-start = ((), (), s32[]{:S(2)}) async-start(), calls=%async_computation.27 | async-start | bytes 4718592 | tf_op jit(solution)/shard_map/reduce_scatter | solution.py:526
  6379.4 510.9 %reduce-scatter.27.cloned.1.call-start = ((), (), s32[]{:S(2)}) async-start(), calls=%async_computation.26 | async-start | bytes 4718592 | tf_op jit(solution)/shard_map/reduce_scatter | solution.py:525
  6386.1 559.3 %reduce-scatter.31.cloned.1.call-start = ((), (), s32[]{:S(2)}) async-start(), calls=%async_computation.28 | async-start | bytes 4718592 | tf_op jit(solution)/shard_map/reduce_scatter | solution.py:527
  (351 other events, 15443.0 us)
Sparse Core Ops, SparseCore 0:
  42.7 80.7 all-gather.18
  339.3 146.0 reduce-scatter.18
  486.9 81.4 all-gather.30
  570.0 79.2 all-gather.28
  2691.2 41.2 reduce-scatter.40
  2906.2 41.2 reduce-scatter.40
  2995.4 41.2 reduce-scatter.44
  3336.3 41.2 reduce-scatter.40
  3425.6 41.2 reduce-scatter.44
  3551.0 41.2 reduce-scatter.40
  3765.9 41.2 reduce-scatter.40
  4195.0 41.2 reduce-scatter.40
  4410.2 41.2 reduce-scatter.40
  4839.6 41.2 reduce-scatter.40
  5054.6 41.2 reduce-scatter.40
  5143.9 41.2 reduce-scatter.44
  5839.6 144.4 reduce-scatter.22
  5989.3 81.4 all-gather.32
  6393.3 144.4 reduce-scatter.24
  6578.0 144.7 reduce-scatter.20
  6727.1 52.1 reduce-scatter.32
  6783.3 51.2 reduce-scatter.28
  6838.9 51.3 reduce-scatter.26
  6894.1 51.2 reduce-scatter.30
  (139 shorter events, 3946.3 us)
where the time goes:
time: 6970 us; the launch traced here: 6950 us
  waiting for transfers between devices  4360 us (63%)
  local copies, waits for them, and re-layouts  1090 us (16%)
  matrix products  718 us (10%)
  other arithmetic  593 us (9%)
  blocking collectives  159 us (2%)
    all_gather x32, waiting for transfers between devices, fetch_weights(): lax.all_gather(down_part, 'fsdp', axis=2, tiled=True)  742 us
    reduce_scatter x16, waiting for transfers between devices, backward_step(): lax.psum_scatter(down_term, 'fsdp', scatter_dimension=2, tiled=True)  690 us
    reduce_scatter x16, waiting for transfers between devices, backward_step(): lax.psum_scatter(up_term, 'fsdp', scatter_dimension=1, tiled=True)  685 us
    reduce_scatter x4, waiting for transfers between devices, rows_scatter(): return lax.psum_scatter(values, 'tp', scatter_dimension=0, tiled=True)  548 us
    all_gather x32, waiting for transfers between devices, fetch_weights(): lax.all_gather(up_part, 'fsdp', axis=1, tiled=True)  503 us
    all_gather x32, waiting for transfers between devices, fetch_weights(): lax.all_gather(gate_part, 'fsdp', axis=1, tiled=True)  468 us
    scatter-add x16, other arithmetic, backward_step(): grad_acc.at[slot_rows].add(grad_disp.reshape(slot_span, model_dim))  269 us
    scatter-add x16, other arithmetic, forward_step(): mix_acc = mix_acc.at[slot_rows].add(expert_out * slot_gates[:, None])  248 us
  transfers between devices with their start and end apart: 165, of which 160 were waited for; matrix products, arithmetic and copies ran while one was open for 22% of the time, Pallas kernels for 0%

commit v1 on v0

v1 whole, which is shorter than its diff:
```python
import functools
import math

import jax
import jax.numpy as jnp
from jax import lax
from jax.experimental import pallas as pl
from jax.experimental.pallas import tpu as pltpu
from jax.sharding import PartitionSpec as P

HEAD_DIM = 128
CONTS = 8
CAP = 512
EPS = 1e-05
NEG = -1e30
QT = 256
BF = jnp.bfloat16
F32 = jnp.float32
NT = (((1,), (1,)), ((), ()))
TN = (((0,), (0,)), ((), ()))


def dot(a, b, dims=(((1,), (0,)), ((), ()))):
    return lax.dot_general(a, b, dims, preferred_element_type=F32)


def params(count=1):
    return pltpu.CompilerParams(
        dimension_semantics=("arbitrary",) * count, vmem_limit_bytes=56 << 20
    )


def cost(flops, nbytes, trans=0):
    return pl.CostEstimate(flops=int(flops), bytes_accessed=int(nbytes), transcendentals=int(trans))


def across(value, axis, pairs):
    return lax.ppermute(value, axis, pairs)


def swap_core(value):
    count = lax.axis_size("fsdp")
    return lax.ppermute(value, "fsdp", [(i, i ^ 1) for i in range(count)])


def swap_chip(value, bit):
    count = lax.axis_size("fsdp")
    return lax.ppermute(value, "fsdp", [(i, i ^ (2 * bit)) for i in range(count)])


def chip_bits():
    chips = lax.axis_size("fsdp") // 2
    return [1 << b for b in range(chips.bit_length() - 1)]


def spread(piece, bits):
    held = {0: piece}
    for bit in bits:
        held.update({r ^ bit: swap_chip(v, bit) for r, v in list(held.items())})
    return [held[r] for r in range(len(held))]


def collect(parts, bits):
    held = dict(enumerate(parts))
    for bit in bits:
        for r in [r for r in held if r & bit]:
            got = swap_chip(held.pop(r).astype(BF), bit)
            held[r ^ bit] = held[r ^ bit].astype(F32) + got.astype(F32)
    return held[0]


def line_gather(value):
    count = lax.axis_size("tp")
    place = lax.axis_index("tp")
    up, down = [value], [value]
    for s in range(1, count):
        up.append(lax.ppermute(up[-1], "tp", [(i, i + 1) for i in range(s - 1, count - 1)]))
        down.append(lax.ppermute(down[-1], "tp", [(i + 1, i) for i in range(count - s)]))
    return [value] + [jnp.where(place + d < count, down[d], up[count - d]) for d in range(1, count)]


def line_scatter(parts):
    count = lax.axis_size("tp")
    up = down = None
    for s in range(count - 1, 0, -1):
        send_up, send_down = parts[s].astype(F32), parts[count - s].astype(F32)
        if up is not None:
            send_up, send_down = send_up + up.astype(F32), send_down + down.astype(F32)
        up = lax.ppermute(send_up.astype(BF), "tp", [(i, i + 1) for i in range(count - s)])
        down = lax.ppermute(send_down.astype(BF), "tp", [(i + 1, i) for i in range(s - 1, count - 1)])
    return parts[0].astype(F32) + up.astype(F32) + down.astype(F32)


def total_tp(value):
    count = lax.axis_size("tp")
    out = value
    for s in range(1, count):
        out = out + lax.ppermute(value, "tp", [(i, (i + s) % count) for i in range(count)])
    return out


def to_rel(value, axis):
    chips = lax.axis_size("fsdp") // 2
    own = lax.axis_index("fsdp") // 2
    width = value.shape[axis] // chips
    return jnp.concatenate(
        [lax.dynamic_slice_in_dim(value, (own ^ r) * width, width, axis) for r in range(chips)], axis
    )


def rows_abs(pieces):
    count = len(pieces)
    place = lax.axis_index("tp")
    rows = pieces[0].shape[0]
    out = jnp.zeros((count * rows,) + pieces[0].shape[1:], pieces[0].dtype)
    for d, piece in enumerate(pieces):
        out = lax.dynamic_update_slice_in_dim(out, piece, ((place + d) % count) * rows, 0)
    return out


def rows_rel(value):
    count = lax.axis_size("tp")
    place = lax.axis_index("tp")
    rows = value.shape[0] // count
    return jnp.concatenate(
        [lax.dynamic_slice_in_dim(value, ((place + d) % count) * rows, rows, 0) for d in range(count)], 0
    )


def keep_kernel(pos_ref, keep_ref):
    pos = pos_ref[...]
    bound = jnp.zeros((1, pos.shape[1]), jnp.int32)
    for b in range(13, -1, -1):
        trial = bound + (1 << b)
        count = jnp.sum((pos <= trial).astype(F32), axis=0, keepdims=True)
        bound = jnp.where(count <= CAP, trial, bound)
    keep_ref[...] = (pos <= bound).astype(F32)


def kept_pairs(routes, order_row, experts):
    pairs = order_row.shape[0]
    tokens = routes.shape[0]
    step = jnp.arange(pairs, dtype=jnp.int32)
    high = (order_row[:, None] // 128 == jnp.arange(pairs // 128, dtype=jnp.int32)[None, :]).astype(BF)
    low = (order_row[:, None] % 128 == jnp.arange(128, dtype=jnp.int32)[None, :]).astype(BF)
    step_high = (step // 64).astype(BF)[:, None]
    step_low = (step % 64).astype(BF)[:, None]
    table = 64.0 * dot(high * step_high, low, TN) + dot(high * step_low, low, TN)
    place = table.astype(jnp.int32).reshape(tokens, -1) + 1
    hot = routes[:, :, None] == jnp.arange(experts, dtype=jnp.int32)[None, None, :]
    pos = jnp.sum(jnp.where(hot, place[:, :, None], 0), axis=1)
    pos = jnp.where(pos == 0, 1 << 20, pos)
    return pl.pallas_call(
        keep_kernel, out_shape=jax.ShapeDtypeStruct((tokens, experts), F32), name="keep"
    )(pos)


def turn_kernel(q_ref, k_ref, v_ref, norm_ref, cos_ref, sin_ref, gain_ref, q_out, k_out, v_out):
    cos, sin = cos_ref[...], sin_ref[...]
    for slot, (raw, out) in enumerate(((q_ref, q_out), (k_ref, k_out))):
        x = raw[...] * norm_ref[:, slot : slot + 1] * gain_ref[slot]
        out[...] = (x * cos + pltpu.roll(x, HEAD_DIM // 2, 1) * sin).astype(BF)
    v_out[...] = v_ref[...].astype(BF)


def turn(raw, norms, cos, sin, gains):
    rows = raw.shape[0]
    heads = raw.shape[1] // (3 * HEAD_DIM)
    part = lambda j: pl.BlockSpec((rows, HEAD_DIM), lambda h: (0, j * heads + h))
    whole = lambda shape: pl.BlockSpec(shape, lambda h: (0,) * len(shape))
    return pl.pallas_call(
        turn_kernel,
        grid=(heads,),
        in_specs=[
            part(0),
            part(1),
            part(2),
            whole(norms.shape),
            whole(cos.shape),
            whole(sin.shape),
            pl.BlockSpec((2, 1, HEAD_DIM), lambda h: (0, 0, h)),
        ],
        out_specs=[part(0)] * 3,
        out_shape=[jax.ShapeDtypeStruct((rows, heads * HEAD_DIM), BF)] * 3,
        compiler_params=params(),
        cost_estimate=cost(10 * raw.size, 6 * raw.size),
        name="turn",
    )(raw, raw, raw, norms, cos, sin, gains)


def turn_back_kernel(
    dq_ref, dk_ref, dkr_ref, q_ref, k_ref, norm_ref, cos_ref, sin_ref, gain_ref, uq_out, uk_out, dots_out, part_out
):
    cos, sin = cos_ref[...], sin_ref[...]
    grads = (dq_ref[...], dk_ref[...] + dkr_ref[...].astype(F32))
    lane = lax.broadcasted_iota(jnp.int32, dots_out.shape, 1)

    @pl.when(pl.program_id(0) == 0)
    def _():
        dots_out[...] = jnp.zeros_like(dots_out)

    for slot, (grad, raw, out) in enumerate(zip(grads, (q_ref, k_ref), (uq_out, uk_out))):
        back = grad * cos - pltpu.roll(grad, HEAD_DIM // 2, 1) * sin
        x = raw[...]
        part_out[slot] = jnp.sum(back * x * norm_ref[:, slot : slot + 1], axis=0, keepdims=True)
        u = back * gain_ref[slot]
        out[...] = u
        dots_out[...] += jnp.where(lane == slot, jnp.sum(u * x, axis=1, keepdims=True), 0.0)


def turn_back(dq, dk, dk_more, raw, norms, cos, sin, gains):
    rows = raw.shape[0]
    heads = raw.shape[1] // (3 * HEAD_DIM)
    part = lambda j: pl.BlockSpec((rows, HEAD_DIM), lambda h: (0, j * heads + h))
    whole = lambda shape: pl.BlockSpec(shape, lambda h: (0,) * len(shape))
    gain_spec = pl.BlockSpec((2, 1, HEAD_DIM), lambda h: (0, 0, h))
    wide = jax.ShapeDtypeStruct((rows, heads * HEAD_DIM), F32)
    return pl.pallas_call(
        turn_back_kernel,
        grid=(heads,),
        in_specs=[
            part(0),
            part(0),
            part(0),
            part(0),
            part(1),
            whole(norms.shape),
            whole(cos.shape),
            whole(sin.shape),
            gain_spec,
        ],
        out_specs=[part(0), part(0), whole((rows, 2)), gain_spec],
        out_shape=[
            wide,
            wide,
            jax.ShapeDtypeStruct((rows, 2), F32),
            jax.ShapeDtypeStruct((2, 1, heads * HEAD_DIM), F32),
        ],
        compiler_params=params(),
        cost_estimate=cost(10 * raw.size, 8 * raw.size),
        name="turn_back",
    )(dq, dk, dk_more, raw, raw, norms, cos, sin, gains)


def own_mask(seg_col, seg_row, first_row, row_count, first_key, key_count):
    rows = lax.broadcasted_iota(jnp.int32, (row_count, key_count), 0) + first_row
    keys = lax.broadcasted_iota(jnp.int32, (row_count, key_count), 1) + first_key
    same = seg_col[first_row : first_row + row_count, :] == seg_row[:, first_key : first_key + key_count]
    return same & (keys <= rows)


SCALE = HEAD_DIM ** (-0.5)


def tile_probs(q_tile, k_ref, seg_col, seg_row, first_row, first_key, keys, kr):
    own = dot(q_tile, k_ref[first_key : first_key + keys, :], NT)
    own = jnp.where(own_mask(seg_col, seg_row, first_row, QT, first_key, keys), own, NEG)
    peak = jnp.max(own, axis=1, keepdims=True)
    far = None
    if kr is not None:
        far = dot(q_tile, kr[...], NT)
        peak = jnp.maximum(peak, jnp.max(far, axis=1, keepdims=True))
        far = jnp.exp((far - peak) * SCALE)
    own = jnp.exp((own - peak) * SCALE)
    total = jnp.sum(own, axis=1, keepdims=True)
    if far is not None:
        total = total + jnp.sum(far, axis=1, keepdims=True)
    inverse = 1.0 / total
    return own * inverse, (None if far is None else far * inverse)


def attend_kernel(cont_ref, q_ref, k_ref, v_ref, kr_ref, vr_ref, col_ref, row_ref, out_ref):
    rows = q_ref.shape[0]

    def run(far):
        for first in range(0, rows, QT):
            start = max(0, first - QT) if far else 0
            keys = first + QT - start
            own, other = tile_probs(
                q_ref[first : first + QT, :], k_ref, col_ref, row_ref, first, start, keys, kr_ref if far else None
            )
            out = dot(own.astype(BF), v_ref[start : start + keys, :])
            if far:
                out = out + dot(other.astype(BF), vr_ref[...])
            out_ref[first : first + QT, :] = out.astype(BF)

    pl.when(cont_ref[0] == 0)(lambda: run(False))
    pl.when(cont_ref[0] != 0)(lambda: run(True))


def attend_specs(rows, count):
    head = pl.BlockSpec((rows, HEAD_DIM), lambda h, c: (0, h))
    return [head] * count + [
        pl.BlockSpec((rows, 1), lambda h, c: (0, 0)),
        pl.BlockSpec((1, rows), lambda h, c: (0, 0)),
    ], head


def attend(cont, q, k, v, kr, vr, seg_col, seg_row):
    rows, width = q.shape
    specs, head = attend_specs(rows, 5)
    return pl.pallas_call(
        attend_kernel,
        grid_spec=pltpu.PrefetchScalarGridSpec(
            num_scalar_prefetch=1, grid=(width // HEAD_DIM,), in_specs=specs, out_specs=head
        ),
        out_shape=jax.ShapeDtypeStruct((rows, width), BF),
        compiler_params=params(),
        cost_estimate=cost(6 * rows * rows * width, 12 * rows * width, rows * rows * 6),
        name="attend",
    )(cont, q, k, v, kr, vr, seg_col, seg_row)


def attend_back_kernel(
    cont_ref, q_ref, k_ref, v_ref, kr_ref, vr_ref, do_ref, col_ref, row_ref, dq_ref, dk_ref, dv_ref, dkr_ref, dvr_ref, far_dk, far_dv
):
    rows = q_ref.shape[0]
    dk_ref[...] = jnp.zeros_like(dk_ref)
    dv_ref[...] = jnp.zeros_like(dv_ref)

    def run(far):
        if far:
            far_dk[...] = jnp.zeros_like(far_dk)
            far_dv[...] = jnp.zeros_like(far_dv)
        for first in range(0, rows, QT):
            start = max(0, first - QT) if far else 0
            keys = first + QT - start
            here = slice(start, start + keys)
            q_tile = q_ref[first : first + QT, :]
            do_tile = do_ref[first : first + QT, :]
            own, other = tile_probs(q_tile, k_ref, col_ref, row_ref, first, start, keys, kr_ref if far else None)
            grad = dot(do_tile, v_ref[here, :], NT)
            mean = jnp.sum(own * grad, axis=1, keepdims=True)
            if far:
                grad_far = dot(do_tile, vr_ref[...], NT)
                mean = mean + jnp.sum(other * grad_far, axis=1, keepdims=True)
            slope = (own * (grad - mean)).astype(BF)
            dq = dot(slope, k_ref[here, :])
            dk_ref[here, :] += dot(slope, q_tile, TN) * SCALE
            dv_ref[here, :] += dot(own.astype(BF), do_tile, TN)
            if far:
                slope = (other * (grad_far - mean)).astype(BF)
                dq = dq + dot(slope, kr_ref[...])
                far_dk[...] += dot(slope, q_tile, TN) * SCALE
                far_dv[...] += dot(other.astype(BF), do_tile, TN)
            dq_ref[first : first + QT, :] = dq * SCALE
        if far:
            dkr_ref[...] = far_dk[...].astype(BF)
            dvr_ref[...] = far_dv[...].astype(BF)
        else:
            dkr_ref[...] = jnp.zeros_like(dkr_ref)
            dvr_ref[...] = jnp.zeros_like(dvr_ref)

    pl.when(cont_ref[0] == 0)(lambda: run(False))
    pl.when(cont_ref[0] != 0)(lambda: run(True))


def attend_back(cont, q, k, v, kr, vr, do, seg_col, seg_row):
    rows, width = q.shape
    specs, head = attend_specs(rows, 6)
    wide = jax.ShapeDtypeStruct((rows, width), F32)
    low = jax.ShapeDtypeStruct((rows, width), BF)
    return pl.pallas_call(
        attend_back_kernel,
        grid_spec=pltpu.PrefetchScalarGridSpec(
            num_scalar_prefetch=1,
            grid=(width // HEAD_DIM,),
            in_specs=specs,
            out_specs=[head] * 5,
            scratch_shapes=[pltpu.VMEM((rows, HEAD_DIM), F32)] * 2,
        ),
        out_shape=[wide, wide, wide, low, low],
        compiler_params=params(),
        cost_estimate=cost(15 * rows * rows * width, 30 * rows * width, rows * rows * 6),
        name="attend_back",
    )(cont, q, k, v, kr, vr, do, seg_col, seg_row)


def hidden_kernel(x_ref, c_ref, g_ref, u_ref, d_ref, w_ref, act_out, dg_out, du_out, s_out):
    expert = pl.program_id(0)
    gate = dot(x_ref[...], g_ref[...])
    up = dot(x_ref[...], u_ref[...])
    back = dot(c_ref[...], d_ref[...])
    lane = lax.broadcasted_iota(jnp.int32, s_out.shape, 1)
    weight = jnp.sum(jnp.where(lane == expert, w_ref[...], 0.0), axis=1, keepdims=True)
    sig = 1.0 / (1.0 + jnp.exp(-gate))
    swish = gate * sig
    act = swish * up
    act_out[...] = (act * weight).astype(BF)
    s = jnp.sum(act * back, axis=1, keepdims=True)
    back = back * weight
    dg_out[...] = (back * up * (sig + swish * (1.0 - sig))).astype(BF)
    du_out[...] = (back * swish).astype(BF)

    @pl.when(expert == 0)
    def _():
        s_out[...] = jnp.zeros_like(s_out)

    s_out[...] = jnp.where(lane == expert, s, s_out[...])


def hidden(x, c, wg, wu, wd, weight):
    rows, dim = x.shape
    experts = weight.shape[1]
    span = wg.shape[1] // experts
    full = pl.BlockSpec((rows, dim), lambda e: (0, 0))
    mat = pl.BlockSpec((dim, span), lambda e: (0, e))
    out = pl.BlockSpec((rows, span), lambda e: (0, e))
    small = pl.BlockSpec((rows, experts), lambda e: (0, 0))
    wide = jax.ShapeDtypeStruct((rows, experts * span), BF)
    return pl.pallas_call(
        hidden_kernel,
        grid=(experts,),
        in_specs=[full, full, mat, mat, mat, small],
        out_specs=[out, out, out, small],
        out_shape=[wide, wide, wide, jax.ShapeDtypeStruct((rows, experts), F32)],
        compiler_params=params(),
        cost_estimate=cost(6 * rows * dim * experts * span, 2 * (2 * rows * dim + 6 * dim * experts * span)),
        name="hidden",
    )(x, c, wg, wu, wd, weight)


def mix_kernel(*refs):
    count = (len(refs) - 1) // 2
    total = None
    for j in range(count):
        term = dot(refs[2 * j][...], refs[2 * j + 1][...], NT)
        total = term if total is None else total + term
    refs[-1][...] = total.astype(refs[-1].dtype)


def mix(pairs, dtype, tile=512):
    rows, cols = pairs[0][0].shape[0], pairs[0][1].shape[0]
    specs, flat, flops, nbytes = [], [], 0, 0
    for a, b in pairs:
        specs += [pl.BlockSpec(a.shape, lambda j: (0, 0)), pl.BlockSpec((tile, b.shape[1]), lambda j: (j, 0))]
        flat += [a, b]
        flops += 2 * rows * cols * a.shape[1]
        nbytes += 2 * (a.size + b.size)
    return pl.pallas_call(
        mix_kernel,
        grid=(cols // tile,),
        in_specs=specs,
        out_specs=pl.BlockSpec((rows, tile), lambda j: (0, j)),
        out_shape=jax.ShapeDtypeStruct((rows, cols), dtype),
        compiler_params=params(),
        cost_estimate=cost(flops, nbytes + 4 * rows * cols),
        name="mix",
    )(*flat)


def angles(seg_block):
    row_count = seg_block.shape[0]
    labels = jnp.arange(CONTS + 1, dtype=jnp.int32)
    member = (seg_block[:, None] == labels[None, :]).astype(jnp.int32)
    counts = jnp.sum(member, axis=0)
    starts = jnp.sum(jnp.where(labels[:, None] > labels[None, :], counts[None, :], 0), axis=1)
    seg_start = jnp.sum(member * starts[None, :], axis=1)
    offset = row_count * (seg_block != 0).astype(jnp.int32)
    places = jnp.arange(row_count, dtype=jnp.int32) - seg_start + offset
    half = HEAD_DIM // 2
    column = jnp.arange(HEAD_DIM, dtype=jnp.int32)
    frequency = jnp.exp((column % half).astype(F32) * (-2.0 * math.log(10000.0) / HEAD_DIM))
    angle = places.astype(F32)[:, None] * frequency[None, :]
    sign = jnp.where(column < half, -1.0, 1.0).astype(F32)
    return jnp.cos(angle), jnp.sin(angle) * sign[None, :]


def inverse_norm(values):
    return lax.rsqrt(jnp.mean(values * values, axis=-1, keepdims=True) + EPS)


def on_device(
    residual,
    query_weight,
    key_weight,
    value_weight,
    out_weight,
    query_gain,
    key_gain,
    attn_gain,
    mlp_gain,
    router_weight,
    gate_weight,
    up_weight,
    down_weight,
    routes,
    route_order,
    seg_ids,
    cotangent,
):
    fsdp, tp = lax.axis_size("fsdp"), lax.axis_size("tp")
    place = lax.axis_index("fsdp")
    core = place % 2
    dim = residual.shape[1]
    piece = dim // fsdp
    tokens = seg_ids.shape[0]
    experts, _, span = gate_weight.shape
    local = experts // 2
    cols = query_weight.shape[1]
    bits = chip_bits()
    back_bits = bits[::-1]
    cut = piece // 2

    a_gain = attn_gain.astype(F32)[:, None]
    m_gain = mlp_gain.astype(F32)[:, None]

    stream = to_rel(residual, 1).astype(F32)
    norm_first = inverse_norm(stream)
    hat_one = stream * norm_first
    normed = rows_abs(line_gather(hat_one.astype(BF)))

    attn_pack = jnp.concatenate(
        [
            (query_weight.astype(F32) * a_gain).astype(BF),
            (key_weight.astype(F32) * a_gain).astype(BF),
            (value_weight.astype(F32) * a_gain).astype(BF),
            out_weight.T,
            jnp.pad((router_weight.astype(F32) * m_gain).astype(BF), ((0, 0), (0, 128 - experts))),
        ],
        axis=1,
    )
    first_half = spread(attn_pack[:cut], bits)
    second_half = spread(attn_pack[cut:], back_bits)
    mine = jnp.stack([jnp.stack([a, b]) for a, b in zip(first_half, second_half)])
    theirs = swap_core(mine)
    pair = jnp.where(core == 0, jnp.stack([mine, theirs], 1), jnp.stack([theirs, mine], 1))
    attn_mat = pair.reshape(dim, -1)
    qkv_mat = attn_mat[:, : 3 * cols]
    out_mat = attn_mat[:, 3 * cols : 4 * cols]
    router_mat = attn_mat[:, 4 * cols :]
    gains = lax.all_gather(jnp.stack([query_gain, key_gain]), "fsdp", axis=2, tiled=True)
    gains = gains.astype(F32).reshape(2, 1, cols)

    def by_rows(weight):
        return weight.transpose(1, 0, 2).reshape(piece, experts, span)

    moe_pack = jnp.stack(
        [
            by_rows((gate_weight.astype(F32) * m_gain[None]).astype(BF)),
            by_rows((up_weight.astype(F32) * m_gain[None]).astype(BF)),
            down_weight.transpose(2, 0, 1),
        ]
    )
    keep_half = lax.dynamic_slice_in_dim(moe_pack, core * local, local, 2).reshape(3, piece, local * span)
    give_half = lax.dynamic_slice_in_dim(moe_pack, (1 - core) * local, local, 2).reshape(3, piece, local * span)
    got_half = swap_core(give_half)
    rows_low = jnp.where(core == 0, keep_half, got_half)
    rows_high = jnp.where(core == 0, got_half, keep_half)

    raw = dot(normed, qkv_mat)
    totals = total_tp(
        jnp.stack([jnp.sum(raw[:, :cols] ** 2, axis=1), jnp.sum(raw[:, cols : 2 * cols] ** 2, axis=1)])
    )
    norms = lax.rsqrt(totals / dim + EPS).T
    cos, sin = angles(seg_ids)
    query_rot, key_rot, value_low = turn(raw, norms, cos, sin, gains)
    half = fsdp // 2
    remote = lax.ppermute(jnp.stack([key_rot, value_low]), "fsdp", [(i, i + half) for i in range(half)])
    cont = (place >= half).astype(jnp.int32).reshape(1)
    seg_col, seg_row = seg_ids[:, None], seg_ids[None, :]

    low_parts = spread(rows_low, bits)
    high_parts = spread(rows_high, back_bits)
    mats = []
    for j in range(3):
        mats.append(jnp.concatenate([p[j] for lo, hi in zip(low_parts, high_parts) for p in (lo, hi)], axis=0))
    gate_mat, up_mat, down_mat = mats

    attended = attend(cont, query_rot, key_rot, value_low, remote[0], remote[1], seg_col, seg_row)
    attn_part = dot(attended, out_mat, NT)
    share = tokens // tp
    parts = rows_rel(attn_part)
    after_attn = stream + line_scatter([parts[d * share : (d + 1) * share] for d in range(tp)])
    norm_second = inverse_norm(after_attn)
    hat_two = after_attn * norm_second

    up_rel = to_rel(cotangent, 1)
    upstream = jnp.concatenate(line_gather(up_rel), axis=0)
    upstream_far = swap_core(upstream)
    mlp_own = jnp.concatenate(line_gather(hat_two.astype(BF)), axis=0)
    mlp_far = swap_core(mlp_own)
    keep = rows_rel(kept_pairs(routes, route_order[0], experts))
    keep_far = swap_core(keep)

    def routed(x, kept):
        logits = dot(x, router_mat)[:, :experts]
        peak = jnp.max(logits, axis=-1, keepdims=True)
        grown = jnp.exp(logits - peak)
        probs = grown / jnp.sum(grown, axis=-1, keepdims=True)
        weight = lax.dynamic_slice_in_dim(probs * kept, core * local, local, 1)
        return probs, weight

    probs_far, weight_far = routed(mlp_far, keep_far)
    probs_own, weight_own = routed(mlp_own, keep)
    act_far, dg_far, du_far, s_far = hidden(mlp_far, upstream_far, gate_mat, up_mat, down_mat, weight_far)
    act_own, dg_own, du_own, s_own = hidden(mlp_own, upstream, gate_mat, up_mat, down_mat, weight_own)

    def logits_back(s, kept, probs):
        zero = jnp.zeros_like(s)
        wide = jnp.where(core == 0, jnp.concatenate([s, zero], 1), jnp.concatenate([zero, s], 1)) * kept
        grad = probs * (wide - jnp.sum(probs * wide, axis=-1, keepdims=True))
        return jnp.pad(grad, ((0, 0), (0, 128 - experts))).astype(BF)

    gl_far = logits_back(s_far, keep_far, probs_far)
    gl_own = logits_back(s_own, keep, probs_own)
    back_far = mix([(dg_far, gate_mat), (du_far, up_mat), (gl_far, router_mat)], BF)
    back_got = swap_core(back_far)
    back_own = mix([(dg_own, gate_mat), (du_own, up_mat), (gl_own, router_mat)], F32)
    back_sum = back_own + back_got.astype(F32)
    grad_scaled = line_scatter([back_sum[d * share : (d + 1) * share] for d in range(tp)])

    out_far = mix([(act_far, down_mat)], BF)
    out_got = swap_core(out_far)
    out_own = mix([(act_own, down_mat)], F32)
    out_sum = out_own + out_got.astype(F32)

    wide_x = jnp.concatenate([mlp_own, mlp_far], axis=0)
    wide_c = jnp.concatenate([upstream, upstream_far], axis=0)
    act = jnp.concatenate([act_own, act_far], axis=0)
    dg = jnp.concatenate([dg_own, dg_far], axis=0)
    du = jnp.concatenate([du_own, du_far], axis=0)
    chips = fsdp // 2
    width = dim // chips
    half_cols = local * span // 2
    terms = []
    for left, right in ((wide_x, dg), (wide_x, du), (wide_c, act)):
        sums = []
        for h, order in ((0, back_bits), (1, bits)):
            pieces = [
                dot(
                    left[:, r * width : (r + 1) * width],
                    right[:, h * half_cols : (h + 1) * half_cols],
                    TN,
                ).astype(BF)
                for r in range(chips)
            ]
            sums.append(collect(pieces, order))
        terms.append(jnp.concatenate(sums, axis=1))
    moe_grad = jnp.stack(terms).reshape(3, 2, piece, local, span)
    mine = lax.dynamic_index_in_dim(moe_grad, core, 1, keepdims=False)
    others = swap_core(lax.dynamic_index_in_dim(moe_grad, 1 - core, 1, keepdims=False).astype(BF)).astype(F32)
    moe_grad = jnp.where(
        core == 0, jnp.concatenate([mine, others], 2), jnp.concatenate([others, mine], 2)
    )
    grad_gate = moe_grad[0].transpose(1, 0, 2) * m_gain[None]
    grad_up = moe_grad[1].transpose(1, 0, 2) * m_gain[None]
    grad_down = moe_grad[2].transpose(1, 2, 0)

    router_term = dot(wide_x, jnp.concatenate([gl_own, gl_far], axis=0), TN)[:, :experts]
    mlp_gain_part = jnp.sum(grad_scaled * hat_two, axis=0)
    grad_after = up_rel.astype(F32) + norm_second * (
        grad_scaled - hat_two * jnp.mean(grad_scaled * hat_two, axis=-1, keepdims=True)
    )
    grad_attn = rows_abs(line_gather(grad_after.astype(BF)))

    block_rel = after_attn + line_scatter([out_sum[d * share : (d + 1) * share] for d in range(tp)])
    block_out = to_rel(block_rel, 1)

    grad_attended = dot(grad_attn, out_mat).astype(BF)
    dq, dk, dv, dk_far, dv_far = attend_back(
        cont, query_rot, key_rot, value_low, remote[0], remote[1], grad_attended, seg_col, seg_row
    )
    returned = lax.ppermute(jnp.stack([dk_far, dv_far]), "fsdp", [(i + half, i) for i in range(half)])
    grad_value = (dv + returned[1].astype(F32)).astype(BF)
    u_query, u_key, dots, gain_parts = turn_back(dq, dk, returned[0], raw, norms, cos, sin, gains)
    dots = total_tp(dots.T).T

    def raw_back(u, x, j):
        n = norms[:, j : j + 1]
        return (n * u - x * (n * n * n * dots[:, j : j + 1] / dim)).astype(BF)

    grad_raw = jnp.concatenate(
        [raw_back(u_query, raw[:, :cols], 0), raw_back(u_key, raw[:, cols : 2 * cols], 1), grad_value], axis=1
    )
    normed_part = dot(grad_raw, qkv_mat, NT)
    parts = rows_rel(normed_part)
    grad_hat = line_scatter([parts[d * share : (d + 1) * share] for d in range(tp)])
    attn_gain_part = jnp.sum(normed_part * normed.astype(F32), axis=0)
    grad_input = to_rel(
        grad_after + norm_first * (grad_hat - hat_one * jnp.mean(grad_hat * hat_one, axis=-1, keepdims=True)), 1
    )

    def by_core(x, which):
        return lax.dynamic_index_in_dim(x.reshape(x.shape[0], chips, 2, piece), which, 2, keepdims=False).reshape(
            x.shape[0], -1
        )

    def weight_back(left, right):
        away = swap_core(dot(by_core(left, 1 - core), right, TN).astype(BF))
        both = (dot(by_core(left, core), right, TN) + away.astype(F32)).astype(BF)
        middle = right.shape[1] // 2
        rows = [both[r * piece : (r + 1) * piece] for r in range(chips)]
        return jnp.concatenate(
            [collect([r[:, :middle] for r in rows], back_bits), collect([r[:, middle:] for r in rows], bits)], axis=1
        )

    grad_out_proj = weight_back(grad_attn, attended).T
    grad_qkv = weight_back(normed, grad_raw) * a_gain

    small = to_rel(jnp.concatenate([mlp_gain_part[:, None], router_term], axis=1), 0)
    small = lax.psum(lax.psum_scatter(small, "fsdp", scatter_dimension=0, tiled=True), "tp")
    grad_mlp_gain = small[:, 0] / m_gain[:, 0]
    grad_router = small[:, 1:] * m_gain
    last = lax.psum_scatter(to_rel(attn_gain_part, 0), "fsdp", scatter_dimension=0, tiled=True)
    grad_attn_gain = lax.psum(last, "tp") / a_gain[:, 0]
    gain_grads = lax.psum_scatter(
        gain_parts.reshape(2, cols // HEAD_DIM, HEAD_DIM), "fsdp", scatter_dimension=2, tiled=True
    )
    return (
        block_out,
        grad_input,
        grad_qkv[:, :cols],
        grad_qkv[:, cols : 2 * cols],
        grad_qkv[:, 2 * cols :],
        grad_out_proj,
        gain_grads[0],
        gain_grads[1],
        grad_attn_gain,
        grad_mlp_gain,
        grad_router,
        grad_gate,
        grad_up,
        grad_down,
    )


def solution(mesh):
    rows = P(("fsdp", "tp"), None)
    in_specs = (
        rows,
        P("fsdp", "tp"),
        P("fsdp", "tp"),
        P("fsdp", "tp"),
        P("tp", "fsdp"),
        P("tp", "fsdp"),
        P("tp", "fsdp"),
        P("fsdp"),
        P("fsdp"),
        P("fsdp", None),
        P(None, "fsdp", "tp"),
        P(None, "fsdp", "tp"),
        P(None, "tp", "fsdp"),
        P("fsdp", None),
        P("fsdp", None),
        P("fsdp"),
        rows,
    )
    out_specs = (
        rows,
        rows,
        P("fsdp", "tp"),
        P("fsdp", "tp"),
        P("fsdp", "tp"),
        P("tp", "fsdp"),
        P("tp", "fsdp"),
        P("tp", "fsdp"),
        P("fsdp"),
        P("fsdp"),
        P("fsdp", None),
        P(None, "fsdp", "tp"),
        P(None, "fsdp", "tp"),
        P(None, "tp", "fsdp"),
    )
    return jax.shard_map(on_device, mesh=mesh, in_specs=in_specs, out_specs=out_specs, check_vma=False)
```

time: 6970 us -> 1650 us (0.24)
  waiting for transfers between devices: 4360 us -> 540 us
  local copies, waits for them, and re-layouts: 1090 us -> 267 us
  matrix products: 718 us -> 153 us
  other arithmetic: 593 us -> 214 us
  Pallas kernels: 0 us -> 199 us
  starting transfers between devices: 12.6 us -> 190 us
  blocking collectives: 159 us -> 57.4 us
    reduce_scatter x57 -> x1, waiting for transfers between devices: 2320 us -> 0.01 us  [on_device(): lax.psum_scatter(small, 'fsdp', scatter_dimension=0, tiled=True)]
    all_gather x104 -> x0, waiting for transfers between devices: 1940 us -> none  [the longest x32 742 us: fetch_weights(): lax.all_gather(down_part, 'fsdp', axis=2, tiled=True)]
    gather x67 -> x0, local copies, waits for them, and re-layouts: 621 us -> none  [the longest x32 242 us: slot_inputs(): jnp.take(mlp_pad, slot_rows, axis=0).reshape(group_size, CAP, model_dim)]
    dot_general x231 -> x37, matrix products: 718 us -> 153 us  [dot(): return lax.dot_general(a, b, dims, preferred_element_type=F32)]
    scatter-add x32 -> x0, other arithmetic: 517 us -> none  [the longest x16 269 us: backward_step(): grad_acc.at[slot_rows].add(grad_disp.reshape(slot_span, model_dim))]
    ppermute x2 -> x108, waiting for transfers between devices: 89.1 us -> 512 us  [the longest x42 221 us: swap_chip(): return lax.ppermute(value, 'fsdp', [(i, i ^ 2 * bit) for i in range(count)])]
    pallas_call x0 -> x11, Pallas kernels: none -> 199 us  [the longest x4 79.2 us: mix(): pl.pallas_call(mix_kernel, grid=(cols // tile,), in_specs=specs, out_spec...]
    ppermute x2 -> x108, starting transfers between devices: 6.22 us -> 189 us  [the longest x42 68.2 us: swap_chip(): return lax.ppermute(value, 'fsdp', [(i, i ^ 2 * bit) for i in range(count)])]
  transfers between devices with their start and end apart: 165 -> 110, of which waited for: 160 -> 40; matrix products, arithmetic and copies ran while one was open for 22% -> 29% of each run, Pallas kernels for 0% -> 6%
where the time goes in v1:
time: 1650 us; the launch traced here: 1640 us
  waiting for transfers between devices  540 us (33%)
  local copies, waits for them, and re-layouts  267 us (16%)
  other arithmetic  214 us (13%)
  Pallas kernels  199 us (12%)
  starting transfers between devices  190 us (12%)
  matrix products  153 us (9%)
  blocking collectives  57.4 us (3%)
  between operations  17.2 us (1%)
    ppermute x42, waiting for transfers between devices, swap_chip(): return lax.ppermute(value, 'fsdp', [(i, i ^ 2 * bit) for i in range(count)])  221 us
    dot_general x37, matrix products, dot(): return lax.dot_general(a, b, dims, preferred_element_type=F32)  153 us
    ppermute x12, waiting for transfers between devices, line_gather(): lax.ppermute(down[-1], 'tp', [(i + 1, i) for i in range(count - s)])  136 us
    unnamed x319, local copies, waits for them, and re-layouts  134 us
    pallas_call x4, Pallas kernels, mix(): pl.pallas_call(mix_kernel, grid=(cols // tile,), in_specs=specs, out_spec...  79.2 us
    ppermute x6, waiting for transfers between devices, total_tp(): lax.ppermute(value, 'tp', [(i, (i + s) % count) for i in range(count)])  74.1 us
    pallas_call x2, Pallas kernels, hidden(): pl.pallas_call(hidden_kernel, grid=(experts,), in_specs=[full, full, mat,...  70.5 us
    ppermute x42, starting transfers between devices, swap_chip(): return lax.ppermute(value, 'fsdp', [(i, i ^ 2 * bit) for i in range(count)])  68.2 us
  transfers between devices with their start and end apart: 110, of which 40 were waited for; matrix products, arithmetic and copies ran while one was open for 29% of the time, Pallas kernels for 6%

profile of v1, /device:TPU:0, one launch (start us, length us, event | category | flops | bytes accessed | tf_op | source)
XLA Modules:
  0.0 1637.6 jit_solution(14384412490941433993)
XLA Ops:
  28.4 15.9 collective-permute-done.9
  65.3 24.3 %collective-permute-done = bf16[256,2048]{1,0:T(8,128)(2,1)} collective-permute-done((bf16[256,2048]{1,0:T(8,128)(2,1)S(1)}, bf16[256,2048]{1,0:T(8,128)(2,1)}, u32[]{:S(2)}, u32[]{:S(2)}) %collective-permute-start) | collective-permute-done | bytes 1048608 | tf_op jit(solution)/shard_map/ppermute | solution.py:78
  124.6 36.7 %collective-permute-done.5 = bf16[256,2048]{1,0:T(8,128)(2,1)S(1)} collective-permute-done((bf16[256,2048]{1,0:T(8,128)(2,1)}, bf16[256,2048]{1,0:T(8,128)(2,1)S(1)}, u32[]{:S(2)}, u32[]{:S(2)}) %collective-permute-start.5) | collective-permute-done | bytes 1048608 | tf_op jit(solution)/shard_map/ppermute | solution.py:78
  230.3 18.8 %collective-permute-done.14 = f32[2,1024]{0,1:T(8,128)} collective-permute-done((f32[2,1024]{0,1:T(8,128)S(1)}, f32[2,1024]{0,1:T(8,128)}, u32[]{:S(2)}, u32[]{:S(2)}) %collective-permute-start.14) | collective-permute-done | bytes 8224 | tf_op jit(solution)/shard_map/ppermute | solution.py:98
  289.8 19.5 %collective-permute-done.16 = bf16[2,1024,512]{2,1,0:T(8,128)(2,1)} collective-permute-done((bf16[2,1024,512]{2,1,0:T(8,128)(2,1)}, bf16[2,1024,512]{2,1,0:T(8,128)(2,1)}, u32[]{:S(2)}, u32[]{:S(2)}) %collective-permute-start.16) | collective-permute-done | bytes 2097184 | tf_op jit(solution)/shard_map/ppermute | solution.py:559
  374.8 14.5 collective-permute-done.18
  407.0 17.6 %collective-permute-done.36 = bf16[3,256,2048]{2,1,0:T(8,128)(2,1)} collective-permute-done((bf16[3,256,2048]{2,1,0:T(8,128)(2,1)S(1)}, bf16[3,256,2048]{2,1,0:T(8,128)(2,1)}, u32[]{:S(2)}, u32[]{:S(2)}) %collective-permute-start.36) | collective-permute-done | bytes 3145760 | tf_op jit(solution)/shard_map/ppermute | solution.py:48
  456.7 35.4 %collective-permute-done.37 = bf16[3,256,2048]{2,1,0:T(8,128)(2,1)} collective-permute-done((bf16[3,256,2048]{2,1,0:T(8,128)(2,1)S(1)}, bf16[3,256,2048]{2,1,0:T(8,128)(2,1)}, u32[]{:S(2)}, u32[]{:S(2)}) %collective-permute-start.37) | collective-permute-done | bytes 3145760 | tf_op jit(solution)/shard_map/ppermute | solution.py:48
  526.9 36.0 %collective-permute-done.40 = bf16[3,256,2048]{2,1,0:T(8,128)(2,1)} collective-permute-done((bf16[3,256,2048]{2,1,0:T(8,128)(2,1)}, bf16[3,256,2048]{2,1,0:T(8,128)(2,1)}, u32[]{:S(2)}, u32[]{:S(2)}) %collective-permute-start.40) | collective-permute-done | bytes 3145760 | tf_op jit(solution)/shard_map/ppermute | solution.py:48
  572.5 22.2 %collective-permute-done.28 = bf16[256,2048]{1,0:T(8,128)(2,1)S(1)} collective-permute-done((bf16[256,2048]{1,0:T(8,128)(2,1)S(1)}, bf16[256,2048]{1,0:T(8,128)(2,1)S(1)}, u32[]{:S(2)}, u32[]{:S(2)}) %collective-permute-start.28) | collective-permute-done | bytes 1048608 | tf_op jit(solution)/shard_map/ppermute | solution.py:78
  605.2 35.3 %hidden.2 = (bf16[1024,2048]{1,0:T(8,128)(2,1)}, bf16[1024,2048]{1,0:T(8,128)(2,1)}, bf16[1024,2048]{1,0:T(8,128)(2,1)}, f32[1024,8]{1,0:T(8,128)}) custom-call(bf16[1024,2048]{1,0:T(8,128)(2,1)} %pad_maximum_fusion.3.x_ref, bf16[1024,2048]{1,0:T(8,128)(2,1)} %copy-done.43, bf16[2048,2048]{1,0:T(8,128)(2,1)} %get-tuple-element.207.g_ref.refs_1_, ...), custom_call_target="tpu_custom_call" | custom-call | flops 25769803776 | bytes 58720256 | tf_op jit(solution)/shard_map/hidden/pallas_call | solution.py:411
  656.5 13.7 mix.4
  670.2 26.2 %mix.6 = f32[1024,2048]{1,0:T(8,128)} custom-call(bf16[1024,2048]{1,0:T(8,128)(2,1)} %get-tuple-element.39.refs_0_, bf16[2048,2048]{1,0:T(8,128)(2,1)} %get-tuple-element.207.g_ref.refs_1_, bf16[1024,2048]{1,0:T(8,128)(2,1)} %get-tuple-element.40.refs_2_, bf16[2048,2048]{1,0:T(8,128)(2,1)} %get-tuple-element.206.u_ref.refs_3_, ...), custom_call_target="tpu_custom_call" | custom-call | flops 17716740096 | bytes 34340864 | tf_op jit(solution)/shard_map/mix/pallas_call | solution.py:440
  701.0 35.2 %hidden.3 = (bf16[1024,2048]{1,0:T(8,128)(2,1)}, bf16[1024,2048]{1,0:T(8,128)(2,1)}, bf16[1024,2048]{1,0:T(8,128)(2,1)}, f32[1024,8]{1,0:T(8,128)}) custom-call(bf16[1024,2048]{1,0:T(8,128)(2,1)} %copy-done.44, bf16[1024,2048]{1,0:T(8,128)(2,1)} %copy-done.42, bf16[2048,2048]{1,0:T(8,128)(2,1)} %get-tuple-element.207.g_ref.refs_1_, ...), custom_call_target="tpu_custom_call" | custom-call | flops 25769803776 | bytes 58720256 | tf_op jit(solution)/shard_map/hidden/pallas_call | solution.py:411
  736.2 13.9 mix.5
  833.9 25.5 %mix.7 = bf16[1024,2048]{1,0:T(8,128)(2,1)} custom-call(bf16[1024,2048]{1,0:T(8,128)(2,1)} %get-tuple-element.42.refs_0_, bf16[2048,2048]{1,0:T(8,128)(2,1)} %get-tuple-element.207.g_ref.refs_1_, bf16[1024,2048]{1,0:T(8,128)(2,1)} %get-tuple-element.43.refs_2_, bf16[2048,2048]{1,0:T(8,128)(2,1)} %get-tuple-element.206.u_ref.refs_3_, ...), custom_call_target="tpu_custom_call" | custom-call | flops 17716740096 | bytes 34340864 | tf_op jit(solution)/shard_map/mix/pallas_call | solution.py:440
  920.6 16.8 %collective-permute-done.93 = bf16[512,1024]{1,0:T(8,128)(2,1)S(1)} collective-permute-done((bf16[512,1024]{1,0:T(8,128)(2,1)S(1)}, bf16[512,1024]{1,0:T(8,128)(2,1)S(1)}, u32[]{:S(2)}, u32[]{:S(2)}) %collective-permute-start.93) | collective-permute-done | bytes 1048608 | tf_op jit(solution)/shard_map/ppermute | solution.py:48
  971.4 15.6 collective-permute-done.106
  1051.2 15.1 collective-permute-done.97
  1250.5 23.4 %collective-permute-done.64 = bf16[256,2048]{1,0:T(8,128)(2,1)S(1)} collective-permute-done((bf16[256,2048]{1,0:T(8,128)(2,1)}, bf16[256,2048]{1,0:T(8,128)(2,1)S(1)}, u32[]{:S(2)}, u32[]{:S(2)}) %collective-permute-start.64) | collective-permute-done | bytes 1048608 | tf_op jit(solution)/shard_map/ppermute | solution.py:78
  1289.0 17.6 %attend_back.1 = (f32[1024,512]{1,0:T(8,128)}, f32[1024,512]{1,0:T(8,128)}, f32[1024,512]{1,0:T(8,128)}, bf16[1024,512]{1,0:T(8,128)(2,1)}, bf16[1024,512]{1,0:T(8,128)(2,1)}) custom-call(s32[1]{0:T(128)} %bitcast.cont_ref, bf16[1024,512]{1,0:T(8,128)(2,1)} %get-tuple-element.34.q_ref, bf16[1024,512]{1,0:T(8,128)(2,1)} %get-tuple-element.35.k_ref, ...), custom_call_target="tpu_custom_call" | custom-call | flops 8053063680 | bytes 15728640 | tf_op jit(solution)/shard_map/attend_back/pallas_call | solution.py:363
  1393.7 33.7 %collective-permute-done.67 = f32[2,1024]{0,1:T(8,128)S(1)} collective-permute-done((f32[2,1024]{0,1:T(8,128)}, f32[2,1024]{0,1:T(8,128)S(1)}, u32[]{:S(2)}, u32[]{:S(2)}) %collective-permute-start.67) | collective-permute-done | bytes 8224 | tf_op jit(solution)/shard_map/ppermute | solution.py:98
  1494.8 28.2 %reduce-scatter.7.cloned.1.call-done = f32[16,8]{1,0:T(8,128)} async-done(((f32[128,8]{1,0:T(8,128)}), f32[16,8]{1,0:T(8,128)}) %reduce-scatter.7.cloned.1.call-update) | async-done | bytes 528
  1560.6 35.5 %all-reduce.8 = (f32[256]{0:T(256)S(1)}, f32[256,17]{0,1:T(8,128)}) all-reduce(f32[256]{0:T(256)S(1)} %dynamic-slice.1, f32[256,17]{0,1:T(8,128)} %reduce-scatter.5.cloned.1.call-done), channel_id=1, replica_groups=mesh['fsdp'=8,'tp'=4] {'tp'}, use_global_device_ids=true, to_apply=%region_19.20 | all-reduce | flops 4608 | bytes 36864 | tf_op jit(solution)/shard_map/psum | solution.py:706
  (757 shorter events, 1044.1 us)
Async XLA Ops:
  7.2 1515.9 %reduce-scatter.7.cloned.1.call-start = ((), (), s32[]{:S(2)}) async-start(), calls=%async_computation.3 | async-start | bytes 73728
  62.0 100.6 %collective-permute-start.12 = (bf16[4,2,128,2176]{2,3,1,0:T(8,128)(2,1)}, bf16[4,2,128,2176]{2,3,1,0:T(8,128)(2,1)}, u32[]{:S(2)}, u32[]{:S(2)}) collective-permute-start(bf16[4,2,128,2176]{2,3,1,0:T(8,128)(2,1)} %get-tuple-element.194), channel_id=1, source_target_pairs={{0,4},{4,0},{8,12},{12,8},{16,20},{20,16},{24,28},{28,24},{1,5},{5... | collective-permute-start | bytes 13369352 | tf_op jit(solution)/shard_map/ppermute | solution.py:43
  94.3 194.2 %collective-permute-start.29 = (bf16[256,2048]{1,0:T(8,128)(2,1)}, bf16[256,2048]{1,0:T(8,128)(2,1)}, u32[]{:S(2)}, u32[]{:S(2)}) collective-permute-start(bf16[256,2048]{1,0:T(8,128)(2,1)} %get-tuple-element.254), channel_id=1, source_target_pairs={{1,0},{2,1},{3,2},{5,4},{6,5},{7,6},{9,8},{10,9},{11,10},{13,12},{... | collective-permute-start | bytes 3145736 | tf_op jit(solution)/shard_map/ppermute | solution.py:78
  95.7 191.1 %collective-permute-start.30 = (bf16[256,2048]{1,0:T(8,128)(2,1)}, bf16[256,2048]{1,0:T(8,128)(2,1)}, u32[]{:S(2)}, u32[]{:S(2)}) collective-permute-start(bf16[256,2048]{1,0:T(8,128)(2,1)} %get-tuple-element.254), channel_id=1, source_target_pairs={{0,1},{1,2},{2,3},{4,5},{5,6},{6,7},{8,9},{9,10},{10,11},{12,13},{... | collective-permute-start | bytes 3145736 | tf_op jit(solution)/shard_map/ppermute | solution.py:77
  279.2 71.7 %collective-permute-start.35 = (bf16[3,256,2048]{2,1,0:T(8,128)(2,1)}, bf16[3,256,2048]{2,1,0:T(8,128)(2,1)}, u32[]{:S(2)}, u32[]{:S(2)}) collective-permute-start(bf16[3,256,2048]{2,1,0:T(8,128)(2,1)} %copy.207), channel_id=1, source_target_pairs={{0,4},{4,0},{8,12},{12,8},{16,20},{20,16},{24,28},{28,24},{1,5},{5... | collective-permute-start | bytes 9437192 | tf_op jit(solution)/shard_map/ppermute | solution.py:43
  286.8 61.9 %collective-permute-start.31 = (bf16[256,2048]{1,0:T(8,128)(2,1)}, bf16[256,2048]{1,0:T(8,128)(2,1)}, u32[]{:S(2)}, u32[]{:S(2)}) collective-permute-start(bf16[256,2048]{1,0:T(8,128)(2,1)} %collective-permute-done.30), channel_id=1, source_target_pairs={{1,2},{2,3},{5,6},{6,7},{9,10},{10,11},{13,14},{14,15},{17,18},{18... | collective-permute-start | bytes 3145736 | tf_op jit(solution)/shard_map/ppermute | solution.py:77
  288.5 61.1 %collective-permute-start.33 = (bf16[256,2048]{1,0:T(8,128)(2,1)}, bf16[256,2048]{1,0:T(8,128)(2,1)}, u32[]{:S(2)}, u32[]{:S(2)}) collective-permute-start(bf16[256,2048]{1,0:T(8,128)(2,1)} %collective-permute-done.29), channel_id=1, source_target_pairs={{1,0},{2,1},{5,4},{6,5},{9,8},{10,9},{13,12},{14,13},{17,16},{18,1... | collective-permute-start | bytes 3145736 | tf_op jit(solution)/shard_map/ppermute | solution.py:78
  353.4 71.2 %collective-permute-start.36 = (bf16[3,256,2048]{2,1,0:T(8,128)(2,1)S(1)}, bf16[3,256,2048]{2,1,0:T(8,128)(2,1)}, u32[]{:S(2)}, u32[]{:S(2)}) collective-permute-start(bf16[3,256,2048]{2,1,0:T(8,128)(2,1)S(1)} %get-tuple-element.190), channel_id=1, source_target_pairs={{0,8},{4,12},{8,0},{12,4},{16,24},{20,28},{24,16},{28,20},{1,9},{5... | collective-permute-start | bytes 9437192 | tf_op jit(solution)/shard_map/ppermute | solution.py:48
  354.0 78.5 %collective-permute-start.39 = (bf16[3,256,2048]{2,1,0:T(8,128)(2,1)S(1)}, bf16[3,256,2048]{2,1,0:T(8,128)(2,1)S(1)}, u32[]{:S(2)}, u32[]{:S(2)}) collective-permute-start(bf16[3,256,2048]{2,1,0:T(8,128)(2,1)S(1)} %get-tuple-element.189), channel_id=1, source_target_pairs={{0,16},{4,20},{8,24},{12,28},{16,0},{20,4},{24,8},{28,12},{1,17},{... | collective-permute-start | bytes 9437192 | tf_op jit(solution)/shard_map/ppermute | solution.py:48
  392.3 99.7 %collective-permute-start.37 = (bf16[3,256,2048]{2,1,0:T(8,128)(2,1)S(1)}, bf16[3,256,2048]{2,1,0:T(8,128)(2,1)}, u32[]{:S(2)}, u32[]{:S(2)}) collective-permute-start(bf16[3,256,2048]{2,1,0:T(8,128)(2,1)S(1)} %get-tuple-element.189), channel_id=1, source_target_pairs={{0,8},{4,12},{8,0},{12,4},{16,24},{20,28},{24,16},{28,20},{1,9},{5... | collective-permute-start | bytes 9437192 | tf_op jit(solution)/shard_map/ppermute | solution.py:48
  402.3 115.4 %collective-permute-start.43 = (bf16[1024,2048]{1,0:T(8,128)(2,1)S(1)}, bf16[1024,2048]{1,0:T(8,128)(2,1)S(1)}, u32[]{:S(2)}, u32[]{:S(2)}) collective-permute-start(bf16[1024,2048]{1,0:T(8,128)(2,1)S(1)} %pad_maximum_fusion.4.c_ref), channel_id=1, source_target_pairs={{0,4},{4,0},{8,12},{12,8},{16,20},{20,16},{24,28},{28,24},{1,5},{5... | collective-permute-start | bytes 12582920 | tf_op jit(solution)/shard_map/ppermute | solution.py:43
  402.4 101.7 %collective-permute-start.38 = (bf16[3,256,2048]{2,1,0:T(8,128)(2,1)S(1)}, bf16[3,256,2048]{2,1,0:T(8,128)(2,1)S(1)}, u32[]{:S(2)}, u32[]{:S(2)}) collective-permute-start(bf16[3,256,2048]{2,1,0:T(8,128)(2,1)S(1)} %get-tuple-element.190), channel_id=1, source_target_pairs={{0,16},{4,20},{8,24},{12,28},{16,0},{20,4},{24,8},{28,12},{1,17},{... | collective-permute-start | bytes 9437192 | tf_op jit(solution)/shard_map/ppermute | solution.py:48
  451.0 111.8 %collective-permute-start.40 = (bf16[3,256,2048]{2,1,0:T(8,128)(2,1)}, bf16[3,256,2048]{2,1,0:T(8,128)(2,1)}, u32[]{:S(2)}, u32[]{:S(2)}) collective-permute-start(bf16[3,256,2048]{2,1,0:T(8,128)(2,1)} %collective-permute-done.36), channel_id=1, source_target_pairs={{0,16},{4,20},{8,24},{12,28},{16,0},{20,4},{24,8},{28,12},{1,17},{... | collective-permute-start | bytes 9437192 | tf_op jit(solution)/shard_map/ppermute | solution.py:48
  455.2 111.3 %collective-permute-start.41 = (bf16[3,256,2048]{2,1,0:T(8,128)(2,1)S(1)}, bf16[3,256,2048]{2,1,0:T(8,128)(2,1)}, u32[]{:S(2)}, u32[]{:S(2)}) collective-permute-start(bf16[3,256,2048]{2,1,0:T(8,128)(2,1)S(1)} %collective-permute-done.39), channel_id=1, source_target_pairs={{0,8},{4,12},{8,0},{12,4},{16,24},{20,28},{24,16},{28,20},{1,9},{5... | collective-permute-start | bytes 9437192 | tf_op jit(solution)/shard_map/ppermute | solution.py:48
  517.7 182.2 %collective-permute-start.44 = (f32[1024,16]{1,0:T(8,128)S(1)}, f32[1024,16]{1,0:T(8,128)S(1)}, u32[]{:S(2)}, u32[]{:S(2)}) collective-permute-start(f32[1024,16]{1,0:T(8,128)S(1)} %copy-done.56), channel_id=1, source_target_pairs={{0,4},{4,0},{8,12},{12,8},{16,20},{20,16},{24,28},{28,24},{1,5},{5... | collective-permute-start | bytes 196616 | tf_op jit(solution)/shard_map/ppermute | solution.py:43
  603.3 93.1 %collective-permute-start.42 = (bf16[1024,2048]{1,0:T(8,128)(2,1)}, bf16[1024,2048]{1,0:T(8,128)(2,1)S(1)}, u32[]{:S(2)}, u32[]{:S(2)}) collective-permute-start(bf16[1024,2048]{1,0:T(8,128)(2,1)} %pad_maximum_fusion.3.x_ref), channel_id=1, source_target_pairs={{0,4},{4,0},{8,12},{12,8},{16,20},{20,16},{24,28},{28,24},{1,5},{5... | collective-permute-start | bytes 12582920 | tf_op jit(solution)/shard_map/ppermute | solution.py:43
  859.4 81.0 %collective-permute-start.52 = (bf16[1024,2048]{1,0:T(8,128)(2,1)}, bf16[1024,2048]{1,0:T(8,128)(2,1)S(1)}, u32[]{:S(2)}, u32[]{:S(2)}) collective-permute-start(bf16[1024,2048]{1,0:T(8,128)(2,1)} %mix.7), channel_id=1, source_target_pairs={{0,4},{4,0},{8,12},{12,8},{16,20},{20,16},{24,28},{28,24},{1,5},{5... | collective-permute-start | bytes 12582920 | tf_op jit(solution)/shard_map/ppermute | solution.py:43
  866.4 84.5 %collective-permute-start.45 = (bf16[1024,2048]{1,0:T(8,128)(2,1)}, bf16[1024,2048]{1,0:T(8,128)(2,1)S(1)}, u32[]{:S(2)}, u32[]{:S(2)}) collective-permute-start(bf16[1024,2048]{1,0:T(8,128)(2,1)} %mix.5), channel_id=1, source_target_pairs={{0,4},{4,0},{8,12},{12,8},{16,20},{20,16},{24,28},{28,24},{1,5},{5... | collective-permute-start | bytes 12582920 | tf_op jit(solution)/shard_map/ppermute | solution.py:43
  917.7 75.2 %collective-permute-start.101 = (bf16[512,1024]{1,0:T(8,128)(2,1)}, bf16[512,1024]{1,0:T(8,128)(2,1)}, u32[]{:S(2)}, u32[]{:S(2)}) collective-permute-start(bf16[512,1024]{1,0:T(8,128)(2,1)} %fusion.145), channel_id=1, source_target_pairs={{0,16},{4,20},{8,24},{12,28},{16,0},{20,4},{24,8},{28,12},{1,17},{... | collective-permute-start | bytes 3145736 | tf_op jit(solution)/shard_map/ppermute | solution.py:48
  1165.9 74.5 %collective-permute-start.107 = (bf16[3,256,8,256]{1,3,2,0:T(8,128)(2,1)S(1)}, bf16[3,256,8,256]{1,3,2,0:T(8,128)(2,1)}, u32[]{:S(2)}, u32[]{:S(2)}) collective-permute-start(bf16[3,256,8,256]{1,3,2,0:T(8,128)(2,1)S(1)} %fusion.10), channel_id=1, source_target_pairs={{0,4},{4,0},{8,12},{12,8},{16,20},{20,16},{24,28},{28,24},{1,5},{5... | collective-permute-start | bytes 9437192 | tf_op jit(solution)/shard_map/ppermute | solution.py:43
  1448.4 86.3 %collective-permute-start.75 = (bf16[1024,1536]{1,0:T(8,128)(2,1)}, bf16[1024,1536]{1,0:T(8,128)(2,1)}, u32[]{:S(2)}, u32[]{:S(2)}) collective-permute-start(bf16[1024,1536]{1,0:T(8,128)(2,1)} %convolution_convert_fusion), channel_id=1, source_target_pairs={{0,4},{4,0},{8,12},{12,8},{16,20},{20,16},{24,28},{28,24},{1,5},{5... | collective-permute-start | bytes 9437192 | tf_op jit(solution)/shard_map/ppermute | solution.py:43
  1490.6 70.0 %reduce-scatter.5.cloned.1.call-start = ((), (), s32[]{:S(2)}) async-start(), calls=%async_computation.2 | async-start | bytes 221184 | tf_op jit(solution)/shard_map/reduce_scatter | solution.py:702
  1530.7 88.8 %collective-permute-start.71 = (bf16[256,2048]{1,0:T(8,128)(2,1)}, bf16[256,2048]{1,0:T(8,128)(2,1)S(1)}, u32[]{:S(2)}, u32[]{:S(2)}) collective-permute-start(bf16[256,2048]{1,0:T(8,128)(2,1)} %get-tuple-element.171), channel_id=1, source_target_pairs={{0,1},{1,2},{2,3},{4,5},{5,6},{6,7},{8,9},{9,10},{10,11},{12,13},{... | collective-permute-start | bytes 3145736 | tf_op jit(solution)/shard_map/ppermute | solution.py:89
  1545.8 73.7 %collective-permute-start.74 = (bf16[256,2048]{1,0:T(8,128)(2,1)}, bf16[256,2048]{1,0:T(8,128)(2,1)S(1)}, u32[]{:S(2)}, u32[]{:S(2)}) collective-permute-start(bf16[256,2048]{1,0:T(8,128)(2,1)} %add_convert_fusion.8), channel_id=1, source_target_pairs={{1,0},{2,1},{3,2},{5,4},{6,5},{7,6},{9,8},{10,9},{11,10},{13,12},{... | collective-permute-start | bytes 3145736 | tf_op jit(solution)/shard_map/ppermute | solution.py:90
  (230 other events, 6080.0 us)
Sparse Core Ops, SparseCore 0:
  1490.7 32.2 reduce-scatter.6
  1526.4 33.5 reduce-scatter.4

commit v2 on v1

--- a/solution.py
+++ b/solution.py
@@ -34,97 +34,118 @@
     return pl.CostEstimate(flops=int(flops), bytes_accessed=int(nbytes), transcendentals=int(trans))
 
 
-def across(value, axis, pairs):
-    return lax.ppermute(value, axis, pairs)
-
-
 def swap_core(value):
     count = lax.axis_size("fsdp")
     return lax.ppermute(value, "fsdp", [(i, i ^ 1) for i in range(count)])
 
 
-def swap_chip(value, bit):
+def chip_groups():
     count = lax.axis_size("fsdp")
-    return lax.ppermute(value, "fsdp", [(i, i ^ (2 * bit)) for i in range(count)])
-
-
-def chip_bits():
-    chips = lax.axis_size("fsdp") // 2
-    return [1 << b for b in range(chips.bit_length() - 1)]
-
-
-def spread(piece, bits):
-    held = {0: piece}
-    for bit in bits:
-        held.update({r ^ bit: swap_chip(v, bit) for r, v in list(held.items())})
-    return [held[r] for r in range(len(held))]
-
-
-def collect(parts, bits):
-    held = dict(enumerate(parts))
-    for bit in bits:
-        for r in [r for r in held if r & bit]:
-            got = swap_chip(held.pop(r).astype(BF), bit)
-            held[r ^ bit] = held[r ^ bit].astype(F32) + got.astype(F32)
-    return held[0]
-
-
-def line_gather(value):
+    return [list(range(c, count, 2)) for c in range(2)]
+
+
+def after(value, *others):
+    return lax.optimization_barrier((value,) + others)[0]
+
+
+def line_gather(value, halves=2, gates=None):
     count = lax.axis_size("tp")
-    place = lax.axis_index("tp")
-    up, down = [value], [value]
+    gates = gates or {}
+    rows = value.shape[0] // halves
+    ups = [[value[h * rows : (h + 1) * rows]] for h in range(halves)]
+    downs = [[u[0]] for u in ups]
     for s in range(1, count):
-        up.append(lax.ppermute(up[-1], "tp", [(i, i + 1) for i in range(s - 1, count - 1)]))
-        down.append(lax.ppermute(down[-1], "tp", [(i + 1, i) for i in range(count - s)]))
-    return [value] + [jnp.where(place + d < count, down[d], up[count - d]) for d in range(1, count)]
-
-
-def line_scatter(parts):
+        for up, down in zip(ups, downs):
+            ahead, behind = up[-1], down[-1]
+            if s > 1 or s in gates:
+                ahead, behind = lax.optimization_barrier((ahead, behind, *gates.get(s, ())))[:2]
+            up.append(lax.ppermute(ahead, "tp", [(i, i + 1) for i in range(s - 1, count - 1)]))
+            down.append(lax.ppermute(behind, "tp", [(i + 1, i) for i in range(count - s)]))
+    arrivals = [[t[s] for t in ups + downs] for s in range(count)]
+    return assemble(ups, downs), arrivals
+
+
+def assemble_kernel(count, halves, place_ref, *refs):
+    out, sems = refs[-2], refs[-1]
+    place = place_ref[0]
+    rows = out.shape[0] // (count * halves)
+    stride = 2 * count - 1
+
+    def each(action):
+        for h in range(halves):
+            mine = refs[h * stride : (h + 1) * stride]
+            for j in range(count):
+                target = out.at[pl.ds((j * halves + h) * rows, rows), :]
+                for s in range(-(count - 1), count):
+                    source = mine[s + count - 1]
+
+                    @pl.when(place - j == s)
+                    def _(source=source, target=target, h=h, j=j):
+                        action(pltpu.make_async_copy(source, target, sems.at[h * count + j]))
+
+    each(lambda copy: copy.start())
+    each(lambda copy: copy.wait())
+
+
+def assemble(ups, downs):
+    count, halves = len(ups[0]), len(ups)
+    rows, dim = ups[0][0].shape
+    flat = []
+    for up, down in zip(ups, downs):
+        flat += down[:0:-1] + up
+    anywhere = pl.BlockSpec(memory_space=pl.ANY)
+    return pl.pallas_call(
+        functools.partial(assemble_kernel, count, halves),
+        in_specs=[pl.BlockSpec(memory_space=pltpu.SMEM)] + [anywhere] * len(flat),
+        out_specs=pl.BlockSpec(memory_space=pltpu.VMEM),
+        out_shape=jax.ShapeDtypeStruct((count * halves * rows, dim), ups[0][0].dtype),
+        scratch_shapes=[pltpu.SemaphoreType.DMA((count * halves,))],
+        cost_estimate=cost(1, 4 * count * halves * rows * dim),
+        name="assemble",
+    )(lax.axis_index("tp").astype(jnp.int32).reshape(1), *flat)
+
+
+def line_scatter(parts, gates=None):
     count = lax.axis_size("tp")
+    gates = gates or {}
     up = down = None
+    arrivals, sends = [()], [()]
     for s in range(count - 1, 0, -1):
         send_up, send_down = parts[s].astype(F32), parts[count - s].astype(F32)
         if up is not None:
             send_up, send_down = send_up + up.astype(F32), send_down + down.astype(F32)
-        up = lax.ppermute(send_up.astype(BF), "tp", [(i, i + 1) for i in range(count - s)])
-        down = lax.ppermute(send_down.astype(BF), "tp", [(i + 1, i) for i in range(s - 1, count - 1)])
-    return parts[0].astype(F32) + up.astype(F32) + down.astype(F32)
+        step = count - s
+        send_up, send_down = send_up.astype(BF), send_down.astype(BF)
+        send_up, send_down = lax.optimization_barrier((send_up, send_down, *gates.get(step, ())))[:2]
+        sends.append((send_up, send_down))
+        up = lax.ppermute(send_up, "tp", [(i, i + 1) for i in range(count - s)])
+        down = lax.ppermute(send_down, "tp", [(i + 1, i) for i in range(s - 1, count - 1)])
+        arrivals.append((up, down))
+    return parts[0].astype(F32) + up.astype(F32) + down.astype(F32), arrivals, sends
+
+
+def total_fsdp(value):
+    count = lax.axis_size("fsdp")
+    bit = 1
+    while bit < count:
+        value = value + lax.ppermute(value, "fsdp", [(i, i ^ bit) for i in range(count)])
+        bit *= 2
+    return value
 
 
 def total_tp(value):
     count = lax.axis_size("tp")
-    out = value
+    out = flat = lax.optimization_barrier(value.reshape(-1, 128))
     for s in range(1, count):
-        out = out + lax.ppermute(value, "tp", [(i, (i + s) % count) for i in range(count)])
-    return out
-
-
-def to_rel(value, axis):
-    chips = lax.axis_size("fsdp") // 2
-    own = lax.axis_index("fsdp") // 2
-    width = value.shape[axis] // chips
-    return jnp.concatenate(
-        [lax.dynamic_slice_in_dim(value, (own ^ r) * width, width, axis) for r in range(chips)], axis
-    )
-
-
-def rows_abs(pieces):
-    count = len(pieces)
-    place = lax.axis_index("tp")
-    rows = pieces[0].shape[0]
-    out = jnp.zeros((count * rows,) + pieces[0].shape[1:], pieces[0].dtype)
-    for d, piece in enumerate(pieces):
-        out = lax.dynamic_update_slice_in_dim(out, piece, ((place + d) % count) * rows, 0)
-    return out
-
-
-def rows_rel(value):
+        out = out + lax.ppermute(flat, "tp", [(i, (i + s) % count) for i in range(count)])
+    return lax.optimization_barrier(out).reshape(value.shape)
+
+
+def shares(value):
     count = lax.axis_size("tp")
     place = lax.axis_index("tp")
     rows = value.shape[0] // count
-    return jnp.concatenate(
-        [lax.dynamic_slice_in_dim(value, ((place + d) % count) * rows, rows, 0) for d in range(count)], 0
-    )
+    return [lax.dynamic_slice_in_dim(value, ((place + d) % count) * rows, rows, 0) for d in range(count)]
 
 
 def keep_kernel(pos_ref, keep_ref):
@@ -155,12 +176,11 @@
     )(pos)
 
 
-def turn_kernel(q_ref, k_ref, v_ref, norm_ref, cos_ref, sin_ref, gain_ref, q_out, k_out, v_out):
+def turn_kernel(q_ref, k_ref, norm_ref, cos_ref, sin_ref, gain_ref, q_out, k_out):
     cos, sin = cos_ref[...], sin_ref[...]
     for slot, (raw, out) in enumerate(((q_ref, q_out), (k_ref, k_out))):
         x = raw[...] * norm_ref[:, slot : slot + 1] * gain_ref[slot]
         out[...] = (x * cos + pltpu.roll(x, HEAD_DIM // 2, 1) * sin).astype(BF)
-    v_out[...] = v_ref[...].astype(BF)
 
 
 def turn(raw, norms, cos, sin, gains):
@@ -174,18 +194,17 @@
         in_specs=[
             part(0),
             part(1),
-            part(2),
             whole(norms.shape),
             whole(cos.shape),
             whole(sin.shape),
             pl.BlockSpec((2, 1, HEAD_DIM), lambda h: (0, 0, h)),
         ],
-        out_specs=[part(0)] * 3,
-        out_shape=[jax.ShapeDtypeStruct((rows, heads * HEAD_DIM), BF)] * 3,
+        out_specs=[part(0)] * 2,
+        out_shape=[jax.ShapeDtypeStruct((rows, heads * HEAD_DIM), BF)] * 2,
         compiler_params=params(),
         cost_estimate=cost(10 * raw.size, 6 * raw.size),
         name="turn",
-    )(raw, raw, raw, norms, cos, sin, gains)
+    )(raw, raw, norms, cos, sin, gains)
 
 
 def turn_back_kernel(
@@ -399,25 +418,29 @@
     s_out[...] = jnp.where(lane == expert, s, s_out[...])
 
 
-def hidden(x, c, wg, wu, wd, weight):
+def hidden(x, c, mats, low_mat, weight, block, held=None):
     rows, dim = x.shape
     experts = weight.shape[1]
-    span = wg.shape[1] // experts
+    span = low_mat.shape[1] // experts
     full = pl.BlockSpec((rows, dim), lambda e: (0, 0))
-    mat = pl.BlockSpec((dim, span), lambda e: (0, e))
-    out = pl.BlockSpec((rows, span), lambda e: (0, e))
-    small = pl.BlockSpec((rows, experts), lambda e: (0, 0))
-    wide = jax.ShapeDtypeStruct((rows, experts * span), BF)
-    return pl.pallas_call(
-        hidden_kernel,
+    mat = lambda j: pl.BlockSpec((dim, span), lambda e: (0, j * experts + e))
+    out = pl.BlockSpec((rows, span), lambda e: (block, e))
+    wide = jax.ShapeDtypeStruct((2 * rows, experts * span), BF)
+    wider = jax.ShapeDtypeStruct((2 * rows, experts * span + 128), BF)
+    held = [] if held is None else list(held)
+    kernel = hidden_kernel if not held else lambda *refs: hidden_kernel(*refs[:6], *refs[9:])
+    return pl.pallas_call(
+        kernel,
         grid=(experts,),
-        in_specs=[full, full, mat, mat, mat, small],
-        out_specs=[out, out, out, small],
-        out_shape=[wide, wide, wide, jax.ShapeDtypeStruct((rows, experts), F32)],
+        in_specs=[full, full, mat(0), mat(1), mat(0), pl.BlockSpec((rows, experts), lambda e: (0, 0))]
+        + [pl.BlockSpec(memory_space=pl.ANY)] * len(held),
+        out_specs=[out, out, out, pl.BlockSpec((rows, experts), lambda e: (0, 0))],
+        out_shape=[wide, wider, wide, jax.ShapeDtypeStruct((rows, experts), F32)],
+        input_output_aliases={6: 0, 7: 1, 8: 2} if held else {},
         compiler_params=params(),
         cost_estimate=cost(6 * rows * dim * experts * span, 2 * (2 * rows * dim + 6 * dim * experts * span)),
         name="hidden",
-    )(x, c, wg, wu, wd, weight)
+    )(x, c, mats, mats, low_mat, weight, *held)
 
 
 def mix_kernel(*refs):
@@ -429,24 +452,125 @@
     refs[-1][...] = total.astype(refs[-1].dtype)
 
 
-def mix(pairs, dtype, tile=512):
-    rows, cols = pairs[0][0].shape[0], pairs[0][1].shape[0]
+def mix(pairs, dtype, rows, tile=512):
+    cols = pairs[0][1].shape[0]
     specs, flat, flops, nbytes = [], [], 0, 0
-    for a, b in pairs:
-        specs += [pl.BlockSpec(a.shape, lambda j: (0, 0)), pl.BlockSpec((tile, b.shape[1]), lambda j: (j, 0))]
+    for a, b, j, k in pairs:
+        deep = min(a.shape[1], b.shape[1], b.shape[0])
+        specs += [
+            pl.BlockSpec((rows, deep), lambda i, k=k: (k, 0)),
+            pl.BlockSpec((tile, deep), lambda i, j=j: (i, j)),
+        ]
         flat += [a, b]
-        flops += 2 * rows * cols * a.shape[1]
-        nbytes += 2 * (a.size + b.size)
+        flops += 2 * rows * cols * deep
+        nbytes += 2 * deep * (rows + cols)
     return pl.pallas_call(
         mix_kernel,
         grid=(cols // tile,),
         in_specs=specs,
-        out_specs=pl.BlockSpec((rows, tile), lambda j: (0, j)),
+        out_specs=pl.BlockSpec((rows, tile), lambda i: (0, i)),
         out_shape=jax.ShapeDtypeStruct((rows, cols), dtype),
         compiler_params=params(),
         cost_estimate=cost(flops, nbytes + 4 * rows * cols),
         name="mix",
     )(*flat)
+
+
+def attn_pack_kernel(experts, q_ref, k_ref, v_ref, o_ref, r_ref, gain_ref, out_ref):
+    cols = q_ref.shape[1]
+    for j, ref in enumerate((q_ref, k_ref, v_ref)):
+        out_ref[:, j * cols : (j + 1) * cols] = (ref[...].astype(F32) * gain_ref[:, 0:1]).astype(BF)
+    out_ref[:, 3 * cols : 4 * cols] = o_ref[...].astype(F32).T.astype(BF)
+    rest = r_ref[...].astype(F32)
+    lane = lax.broadcasted_iota(jnp.int32, rest.shape, 1)
+    out_ref[:, 4 * cols :] = jnp.where(lane < experts, rest * gain_ref[:, 1:2], rest).astype(BF)
+
+
+def attn_pack(q, k, v, o, r, gains, experts):
+    return pl.pallas_call(
+        functools.partial(attn_pack_kernel, experts),
+        out_shape=jax.ShapeDtypeStruct((q.shape[0], 4 * q.shape[1] + r.shape[1]), BF),
+        cost_estimate=cost(1, 4 << 20),
+        name="attn_pack",
+    )(q, k, v, o, r, gains)
+
+
+PACK = 4
+
+
+def moe_pack_kernel(core_ref, g_ref, u_ref, d_ref, gain_ref, g_out, u_out, d_out):
+    gain = gain_ref[:, 1:2]
+    span = g_ref.shape[2]
+    for i in range(PACK):
+        here = slice(i * span, (i + 1) * span)
+        g_out[0, :, here] = (g_ref[i].astype(F32) * gain).astype(BF)
+        u_out[0, :, here] = (u_ref[i].astype(F32) * gain).astype(BF)
+        d_out[0, :, here] = d_ref[i].astype(F32).T.astype(BF)
+
+
+def moe_pack(core, gate, up, down, gains):
+    experts, piece, span = gate.shape
+    local = experts // 2
+    steps = local // PACK
+    block = pl.BlockSpec((PACK, piece, span), lambda e, c: (e, 0, 0))
+    out = pl.BlockSpec((1, piece, PACK * span), lambda e, c: ((e // steps) ^ c[0], 0, e % steps))
+    return pl.pallas_call(
+        moe_pack_kernel,
+        grid_spec=pltpu.PrefetchScalarGridSpec(
+            num_scalar_prefetch=1,
+            grid=(experts // PACK,),
+            in_specs=[
+                block,
+                block,
+                pl.BlockSpec((PACK, span, piece), lambda e, c: (e, 0, 0)),
+                pl.BlockSpec(gains.shape, lambda e, c: (0, 0)),
+            ],
+            out_specs=[out] * 3,
+        ),
+        out_shape=[jax.ShapeDtypeStruct((2, piece, local * span), BF)] * 3,
+        compiler_params=params(),
+        cost_estimate=cost(1, 12 * gate.size),
+        name="moe_pack",
+    )(core, gate, up, down, gains)
+
+
+def moe_unpack_kernel(core_ref, *refs):
+    mine, theirs, gain_ref, outs = refs[:3], refs[3:6], refs[6], refs[7:]
+    steps = pl.num_programs(0) // 2
+    here = pl.program_id(0) // steps == core_ref[0]
+    gain = gain_ref[:, 1:2]
+    span = outs[0].shape[2]
+    for i in range(PACK):
+        part = slice(i * span, (i + 1) * span)
+        g, u, d = (jnp.where(here, a[:, part], b[:, part]).astype(F32) for a, b in zip(mine, theirs))
+        outs[0][i] = g * gain
+        outs[1][i] = u * gain
+        outs[2][i] = d.T
+
+
+def moe_unpack(core, mine, theirs, gains, experts, local):
+    piece = mine[0].shape[0]
+    span = mine[1].shape[1] // local
+    steps = local // PACK
+    block = pl.BlockSpec((piece, PACK * span), lambda e, c: (0, e % steps))
+    wide = pl.BlockSpec((PACK, piece, span), lambda e, c: (e, 0, 0))
+    return pl.pallas_call(
+        moe_unpack_kernel,
+        grid_spec=pltpu.PrefetchScalarGridSpec(
+            num_scalar_prefetch=1,
+            grid=(experts // PACK,),
+            in_specs=[block] * 6 + [pl.BlockSpec(gains.shape, lambda e, c: (0, 0))],
+            out_specs=[wide, wide, pl.BlockSpec((PACK, span, piece), lambda e, c: (e, 0, 0))],
+        ),
+        out_shape=[
+            jax.ShapeDtypeStruct((experts, piece, span), F32),
+            jax.ShapeDtypeStruct((experts, piece, span), F32),
+            jax.ShapeDtypeStruct((experts, span, piece), F32),
+        ],
+        compiler_params=params(),
+        cost_estimate=cost(1, 24 * experts * piece * span),
+        name="moe_unpack",
+    )(core, *mine, *theirs, gains)
 
 
 def angles(seg_block):
@@ -492,179 +616,161 @@
     fsdp, tp = lax.axis_size("fsdp"), lax.axis_size("tp")
     place = lax.axis_index("fsdp")
     core = place % 2
+    core_arg = core.astype(jnp.int32).reshape(1)
     dim = residual.shape[1]
     piece = dim // fsdp
     tokens = seg_ids.shape[0]
+    share = tokens // tp
     experts, _, span = gate_weight.shape
     local = experts // 2
     cols = query_weight.shape[1]
-    bits = chip_bits()
-    back_bits = bits[::-1]
-    cut = piece // 2
-
-    a_gain = attn_gain.astype(F32)[:, None]
-    m_gain = mlp_gain.astype(F32)[:, None]
-
-    stream = to_rel(residual, 1).astype(F32)
+    heads = cols // HEAD_DIM
+    groups = chip_groups()
+
+    norm_gains = jnp.stack([attn_gain, mlp_gain], axis=1).astype(F32)
+
+    stream = residual.astype(F32)
     norm_first = inverse_norm(stream)
     hat_one = stream * norm_first
-    normed = rows_abs(line_gather(hat_one.astype(BF)))
-
-    attn_pack = jnp.concatenate(
-        [
-            (query_weight.astype(F32) * a_gain).astype(BF),
-            (key_weight.astype(F32) * a_gain).astype(BF),
-            (value_weight.astype(F32) * a_gain).astype(BF),
-            out_weight.T,
-            jnp.pad((router_weight.astype(F32) * m_gain).astype(BF), ((0, 0), (0, 128 - experts))),
-        ],
-        axis=1,
-    )
-    first_half = spread(attn_pack[:cut], bits)
-    second_half = spread(attn_pack[cut:], back_bits)
-    mine = jnp.stack([jnp.stack([a, b]) for a, b in zip(first_half, second_half)])
-    theirs = swap_core(mine)
-    pair = jnp.where(core == 0, jnp.stack([mine, theirs], 1), jnp.stack([theirs, mine], 1))
-    attn_mat = pair.reshape(dim, -1)
+    hat_low = hat_one.astype(BF)
+    normed, steps_one = line_gather(hat_low)
+
+    narrow = HEAD_DIM // fsdp
+    gain_col = jnp.stack([query_gain, key_gain]).reshape(-1, 1)
+    gain_col = jnp.pad(gain_col, ((0, piece - gain_col.shape[0]), (0, 127 - experts)))
+    attn_mat = lax.all_gather(
+        attn_pack(
+            after(query_weight, hat_low),
+            key_weight,
+            value_weight,
+            out_weight,
+            jnp.concatenate([router_weight, gain_col], axis=1),
+            norm_gains,
+            experts,
+        ),
+        "fsdp",
+        axis=0,
+        tiled=True,
+    )
     qkv_mat = attn_mat[:, : 3 * cols]
     out_mat = attn_mat[:, 3 * cols : 4 * cols]
     router_mat = attn_mat[:, 4 * cols :]
-    gains = lax.all_gather(jnp.stack([query_gain, key_gain]), "fsdp", axis=2, tiled=True)
-    gains = gains.astype(F32).reshape(2, 1, cols)
-
-    def by_rows(weight):
-        return weight.transpose(1, 0, 2).reshape(piece, experts, span)
-
-    moe_pack = jnp.stack(
-        [
-            by_rows((gate_weight.astype(F32) * m_gain[None]).astype(BF)),
-            by_rows((up_weight.astype(F32) * m_gain[None]).astype(BF)),
-            down_weight.transpose(2, 0, 1),
-        ]
-    )
-    keep_half = lax.dynamic_slice_in_dim(moe_pack, core * local, local, 2).reshape(3, piece, local * span)
-    give_half = lax.dynamic_slice_in_dim(moe_pack, (1 - core) * local, local, 2).reshape(3, piece, local * span)
-    got_half = swap_core(give_half)
-    rows_low = jnp.where(core == 0, keep_half, got_half)
-    rows_high = jnp.where(core == 0, got_half, keep_half)
+    gains = router_mat[:, experts].astype(F32).reshape(fsdp, piece)[:, : 2 * heads * narrow]
+    gains = gains.reshape(fsdp, 2, heads, narrow).transpose(1, 2, 0, 3).reshape(2, 1, cols)
+    lane = jnp.arange(128, dtype=jnp.int32)[None, :]
+    router_mat = jnp.where(lane < experts, router_mat, 0)
+
+    packs = moe_pack(core_arg, after(gate_weight, hat_low), up_weight, down_weight, norm_gains)
+
+    def both_rows(kept, given):
+        got = swap_core(given)
+        return jnp.concatenate([jnp.where(core == 0, kept, got), jnp.where(core == 0, got, kept)], axis=0)
+
+    def over_chips(value):
+        return lax.all_gather(value, "fsdp", axis=0, tiled=True, axis_index_groups=groups)
+
+    low_rows = both_rows(packs[2][0], packs[2][1])
+    low_mat = over_chips(after(low_rows, attn_mat, *steps_one[2]))
+    rows = both_rows(*[jnp.concatenate([packs[0][h], packs[1][h]], axis=1) for h in range(2)])
 
     raw = dot(normed, qkv_mat)
-    totals = total_tp(
-        jnp.stack([jnp.sum(raw[:, :cols] ** 2, axis=1), jnp.sum(raw[:, cols : 2 * cols] ** 2, axis=1)])
-    )
+    half = fsdp // 2
+    forth = [(i, i + half) for i in range(half)]
+    value_low = raw[:, 2 * cols :].astype(BF)
+    value_far = lax.ppermute(value_low, "fsdp", forth)
+    upstream, steps_up = line_gather(cotangent, gates={1: steps_one[3]})
+    query_key = after(raw, value_low)
+    totals = jnp.stack(
+        [jnp.sum(query_key[:, :cols] ** 2, axis=1), jnp.sum(query_key[:, cols : 2 * cols] ** 2, axis=1)]
+    )
+    totals = total_tp(after(totals, *steps_up[1]))
     norms = lax.rsqrt(totals / dim + EPS).T
     cos, sin = angles(seg_ids)
-    query_rot, key_rot, value_low = turn(raw, norms, cos, sin, gains)
-    half = fsdp // 2
-    remote = lax.ppermute(jnp.stack([key_rot, value_low]), "fsdp", [(i, i + half) for i in range(half)])
+    query_rot, key_rot = turn(raw, after(norms, value_far, *steps_up[2]), cos, sin, gains)
+    key_far = lax.ppermute(key_rot, "fsdp", forth)
     cont = (place >= half).astype(jnp.int32).reshape(1)
     seg_col, seg_row = seg_ids[:, None], seg_ids[None, :]
-
-    low_parts = spread(rows_low, bits)
-    high_parts = spread(rows_high, back_bits)
-    mats = []
-    for j in range(3):
-        mats.append(jnp.concatenate([p[j] for lo, hi in zip(low_parts, high_parts) for p in (lo, hi)], axis=0))
-    gate_mat, up_mat, down_mat = mats
-
-    attended = attend(cont, query_rot, key_rot, value_low, remote[0], remote[1], seg_col, seg_row)
-    attn_part = dot(attended, out_mat, NT)
-    share = tokens // tp
-    parts = rows_rel(attn_part)
-    after_attn = stream + line_scatter([parts[d * share : (d + 1) * share] for d in range(tp)])
+    mats = over_chips(after(rows, key_far, value_far))
+
+    upstream_far = swap_core(upstream)
+
+    attended = attend(
+        cont, after(query_rot, *steps_up[3]), key_rot, value_low, key_far, value_far, seg_col, seg_row
+    )
+    attn_part = dot(attended, out_mat, NT).astype(BF)
+    attn_out, _, _ = line_scatter(shares(attn_part))
+    after_attn = stream + attn_out
     norm_second = inverse_norm(after_attn)
     hat_two = after_attn * norm_second
 
-    up_rel = to_rel(cotangent, 1)
-    upstream = jnp.concatenate(line_gather(up_rel), axis=0)
-    upstream_far = swap_core(upstream)
-    mlp_own = jnp.concatenate(line_gather(hat_two.astype(BF)), axis=0)
+    keep = kept_pairs(routes, route_order[0], experts)
+    keep_far = swap_core(keep)
+    wide_c = jnp.concatenate([upstream, upstream_far], axis=0)
+    mlp_own, _ = line_gather(hat_two.astype(BF), gates={2: [keep_far], 3: [wide_c]})
     mlp_far = swap_core(mlp_own)
-    keep = rows_rel(kept_pairs(routes, route_order[0], experts))
-    keep_far = swap_core(keep)
 
     def routed(x, kept):
         logits = dot(x, router_mat)[:, :experts]
-        peak = jnp.max(logits, axis=-1, keepdims=True)
-        grown = jnp.exp(logits - peak)
+        grown = jnp.exp(logits - jnp.max(logits, axis=-1, keepdims=True))
         probs = grown / jnp.sum(grown, axis=-1, keepdims=True)
-        weight = lax.dynamic_slice_in_dim(probs * kept, core * local, local, 1)
-        return probs, weight
-
-    probs_far, weight_far = routed(mlp_far, keep_far)
-    probs_own, weight_own = routed(mlp_own, keep)
-    act_far, dg_far, du_far, s_far = hidden(mlp_far, upstream_far, gate_mat, up_mat, down_mat, weight_far)
-    act_own, dg_own, du_own, s_own = hidden(mlp_own, upstream, gate_mat, up_mat, down_mat, weight_own)
+        return probs, lax.dynamic_slice_in_dim(probs * kept, core * local, local, 1)
 
     def logits_back(s, kept, probs):
         zero = jnp.zeros_like(s)
-        wide = jnp.where(core == 0, jnp.concatenate([s, zero], 1), jnp.concatenate([zero, s], 1)) * kept
-        grad = probs * (wide - jnp.sum(probs * wide, axis=-1, keepdims=True))
+        pair = kept * jnp.where(core == 0, jnp.concatenate([s, zero], 1), jnp.concatenate([zero, s], 1))
+        grad = probs * (pair - jnp.sum(probs * pair, axis=-1, keepdims=True))
         return jnp.pad(grad, ((0, 0), (0, 128 - experts))).astype(BF)
 
+    probs_own, weight_own = routed(mlp_own, keep)
+    *held, s_own = hidden(mlp_own, upstream, mats, low_mat, weight_own, 0)
+    probs_far, weight_far = routed(mlp_far, keep_far)
+    act, dg, du, s_far = hidden(mlp_far, upstream_far, mats, low_mat, weight_far, 1, held)
+    gl_own = logits_back(s_own, keep, probs_own)
     gl_far = logits_back(s_far, keep_far, probs_far)
-    gl_own = logits_back(s_own, keep, probs_own)
-    back_far = mix([(dg_far, gate_mat), (du_far, up_mat), (gl_far, router_mat)], BF)
+
+    def both_cores(own, got):
+        return [a.astype(F32) + b.astype(F32) for a, b in zip(shares(own), shares(got))]
+
+    back_far = mix([(dg, mats, 0, 1), (du, mats, 1, 1), (gl_far, router_mat, 0, 0)], BF, tokens)
     back_got = swap_core(back_far)
-    back_own = mix([(dg_own, gate_mat), (du_own, up_mat), (gl_own, router_mat)], F32)
-    back_sum = back_own + back_got.astype(F32)
-    grad_scaled = line_scatter([back_sum[d * share : (d + 1) * share] for d in range(tp)])
-
-    out_far = mix([(act_far, down_mat)], BF)
+    back_own = mix([(dg, mats, 0, 0), (du, mats, 1, 0), (gl_own, router_mat, 0, 0)], BF, tokens)
+    grad_scaled, _, back_sends = line_scatter(both_cores(back_own, back_got))
+
+    def scattered(value):
+        return lax.psum_scatter(value, "fsdp", scatter_dimension=0, tiled=True, axis_index_groups=groups)
+
+    dg = lax.dynamic_update_slice(
+        after(dg, back_own, back_got), jnp.concatenate([gl_own, gl_far], axis=0), (0, local * span)
+    )
+    wide_x = jnp.concatenate([after(mlp_own, back_own), mlp_far], axis=0)
+    terms = [
+        dot(left, after(right, *gate), TN).astype(BF)
+        for left, right, gate in zip((wide_c, wide_x, wide_x), (act, dg, du), back_sends[1:])
+    ]
+    terms = [terms[1], terms[2], terms[0]]
+    sums = [scattered(t) for t in terms]
+    out_far = mix([(act, low_mat, 0, 1)], BF, tokens)
+    out_own = mix([(act, low_mat, 0, 0)], BF, tokens)
     out_got = swap_core(out_far)
-    out_own = mix([(act_own, down_mat)], F32)
-    out_sum = out_own + out_got.astype(F32)
-
-    wide_x = jnp.concatenate([mlp_own, mlp_far], axis=0)
-    wide_c = jnp.concatenate([upstream, upstream_far], axis=0)
-    act = jnp.concatenate([act_own, act_far], axis=0)
-    dg = jnp.concatenate([dg_own, dg_far], axis=0)
-    du = jnp.concatenate([du_own, du_far], axis=0)
-    chips = fsdp // 2
-    width = dim // chips
-    half_cols = local * span // 2
-    terms = []
-    for left, right in ((wide_x, dg), (wide_x, du), (wide_c, act)):
-        sums = []
-        for h, order in ((0, back_bits), (1, bits)):
-            pieces = [
-                dot(
-                    left[:, r * width : (r + 1) * width],
-                    right[:, h * half_cols : (h + 1) * half_cols],
-                    TN,
-                ).astype(BF)
-                for r in range(chips)
-            ]
-            sums.append(collect(pieces, order))
-        terms.append(jnp.concatenate(sums, axis=1))
-    moe_grad = jnp.stack(terms).reshape(3, 2, piece, local, span)
-    mine = lax.dynamic_index_in_dim(moe_grad, core, 1, keepdims=False)
-    others = swap_core(lax.dynamic_index_in_dim(moe_grad, 1 - core, 1, keepdims=False).astype(BF)).astype(F32)
-    moe_grad = jnp.where(
-        core == 0, jnp.concatenate([mine, others], 2), jnp.concatenate([others, mine], 2)
-    )
-    grad_gate = moe_grad[0].transpose(1, 0, 2) * m_gain[None]
-    grad_up = moe_grad[1].transpose(1, 0, 2) * m_gain[None]
-    grad_down = moe_grad[2].transpose(1, 2, 0)
-
-    router_term = dot(wide_x, jnp.concatenate([gl_own, gl_far], axis=0), TN)[:, :experts]
-    mlp_gain_part = jnp.sum(grad_scaled * hat_two, axis=0)
-    grad_after = up_rel.astype(F32) + norm_second * (
+
+    grad_after = cotangent.astype(F32) + norm_second * (
         grad_scaled - hat_two * jnp.mean(grad_scaled * hat_two, axis=-1, keepdims=True)
     )
-    grad_attn = rows_abs(line_gather(grad_after.astype(BF)))
-
-    block_rel = after_attn + line_scatter([out_sum[d * share : (d + 1) * share] for d in range(tp)])
-    block_out = to_rel(block_rel, 1)
-
-    grad_attended = dot(grad_attn, out_mat).astype(BF)
+    grad_attn, _ = line_gather(after(grad_after.astype(BF), *terms))
+
+    grad_attended = after(dot(grad_attn, out_mat).astype(BF), out_far, out_own)
     dq, dk, dv, dk_far, dv_far = attend_back(
-        cont, query_rot, key_rot, value_low, remote[0], remote[1], grad_attended, seg_col, seg_row
-    )
-    returned = lax.ppermute(jnp.stack([dk_far, dv_far]), "fsdp", [(i + half, i) for i in range(half)])
-    grad_value = (dv + returned[1].astype(F32)).astype(BF)
-    u_query, u_key, dots, gain_parts = turn_back(dq, dk, returned[0], raw, norms, cos, sin, gains)
+        cont, query_rot, key_rot, value_low, key_far, value_far, grad_attended, seg_col, seg_row
+    )
+    out_total, out_steps, _ = line_scatter(both_cores(out_own, out_got), {1: [grad_attended], 2: [dk_far]})
+    block_out = after_attn + out_total
+    back_pairs = [(i + half, i) for i in range(half)]
+    dk_got, dv_got = lax.ppermute(dk_far, "fsdp", back_pairs), lax.ppermute(dv_far, "fsdp", back_pairs)
+    u_query, u_key, dots, gain_parts = turn_back(
+        dq, after(dk, *out_steps[1], sums[2]), dk_got, raw, norms, cos, sin, gains
+    )
     dots = total_tp(dots.T).T
+    grad_value = (dv + dv_got.astype(F32)).astype(BF)
 
     def raw_back(u, x, j):
         n = norms[:, j : j + 1]
@@ -673,49 +779,47 @@
     grad_raw = jnp.concatenate(
         [raw_back(u_query, raw[:, :cols], 0), raw_back(u_key, raw[:, cols : 2 * cols], 1), grad_value], axis=1
     )
-    normed_part = dot(grad_raw, qkv_mat, NT)
-    parts = rows_rel(normed_part)
-    grad_hat = line_scatter([parts[d * share : (d + 1) * share] for d in range(tp)])
-    attn_gain_part = jnp.sum(normed_part * normed.astype(F32), axis=0)
-    grad_input = to_rel(
-        grad_after + norm_first * (grad_hat - hat_one * jnp.mean(grad_hat * hat_one, axis=-1, keepdims=True)), 1
-    )
-
-    def by_core(x, which):
-        return lax.dynamic_index_in_dim(x.reshape(x.shape[0], chips, 2, piece), which, 2, keepdims=False).reshape(
-            x.shape[0], -1
-        )
-
-    def weight_back(left, right):
-        away = swap_core(dot(by_core(left, 1 - core), right, TN).astype(BF))
-        both = (dot(by_core(left, core), right, TN) + away.astype(F32)).astype(BF)
-        middle = right.shape[1] // 2
-        rows = [both[r * piece : (r + 1) * piece] for r in range(chips)]
-        return jnp.concatenate(
-            [collect([r[:, :middle] for r in rows], back_bits), collect([r[:, middle:] for r in rows], bits)], axis=1
-        )
-
-    grad_out_proj = weight_back(grad_attn, attended).T
-    grad_qkv = weight_back(normed, grad_raw) * a_gain
-
-    small = to_rel(jnp.concatenate([mlp_gain_part[:, None], router_term], axis=1), 0)
-    small = lax.psum(lax.psum_scatter(small, "fsdp", scatter_dimension=0, tiled=True), "tp")
-    grad_mlp_gain = small[:, 0] / m_gain[:, 0]
-    grad_router = small[:, 1:] * m_gain
-    last = lax.psum_scatter(to_rel(attn_gain_part, 0), "fsdp", scatter_dimension=0, tiled=True)
-    grad_attn_gain = lax.psum(last, "tp") / a_gain[:, 0]
-    gain_grads = lax.psum_scatter(
-        gain_parts.reshape(2, cols // HEAD_DIM, HEAD_DIM), "fsdp", scatter_dimension=2, tiled=True
-    )
+    normed_part = dot(after(grad_raw, block_out, sums[0]), qkv_mat, NT).astype(BF)
+    small = gain_parts.reshape(2, heads, fsdp, narrow).transpose(2, 0, 1, 3).reshape(fsdp, -1)
+    grad_raw_later = after(grad_raw, normed_part)
+    qkv_term = dot(normed, grad_raw_later, TN).astype(BF)
+    late = []
+    grad_hat, _, last_sends = line_scatter(shares(normed_part), {3: late})
+
+    sums = [after(t, *last_sends[1]) for t in sums]
+    mine = [lax.dynamic_slice_in_dim(t, core * piece, piece, 0) for t in sums]
+    theirs = [swap_core(lax.dynamic_slice_in_dim(t, (1 - core) * piece, piece, 0)) for t in sums]
+    grad_gate, grad_up, grad_down = moe_unpack(core_arg, mine, theirs, norm_gains, experts, local)
+    router_hat = total_tp(sum(t[0][:, local * span :].astype(F32) for t in (mine, theirs)))[:, :experts]
+    grad_router = router_hat * norm_gains[:, 1:2]
+    gate_term = jnp.sum(gate_weight.astype(F32) * grad_gate + up_weight.astype(F32) * grad_up, axis=(0, 2))
+    small = total_fsdp(after(small, *last_sends[1]))
+
+    def summed(value):
+        return lax.psum_scatter(value, "fsdp", scatter_dimension=0, tiled=True).astype(F32)
+
+    grad_out_proj = summed(dot(grad_attn, after(attended, dk_far), TN).astype(BF)).T
+    attn_sum = summed(qkv_term)
+    qkv_hat = [attn_sum[:, j * cols : (j + 1) * cols] for j in range(3)]
+    qkv_grad = [norm_gains[:, 0:1] * t for t in qkv_hat]
+    small = lax.dynamic_index_in_dim(small, place, 0, keepdims=False)
+    small = small.reshape(2, heads, narrow)
+
+    attn_dots = sum(jnp.sum(w.astype(F32) * t, axis=1) for w, t in zip((query_weight, key_weight, value_weight), qkv_hat))
+    both_dots = total_tp(jnp.stack([attn_dots, gate_term / norm_gains[:, 1]]))
+    grad_attn_gain = both_dots[0]
+    grad_mlp_gain = both_dots[1] + jnp.sum(router_weight.astype(F32) * router_hat, axis=1)
+    grad_hat = after(grad_hat, both_dots, grad_out_proj, *qkv_grad)
+    grad_input = grad_after + norm_first * (grad_hat - hat_one * jnp.mean(grad_hat * hat_one, axis=-1, keepdims=True))
     return (
         block_out,
         grad_input,
-        grad_qkv[:, :cols],
-        grad_qkv[:, cols : 2 * cols],
-        grad_qkv[:, 2 * cols :],
+        qkv_grad[0],
+        qkv_grad[1],
+        qkv_grad[2],
         grad_out_proj,
-        gain_grads[0],
-        gain_grads[1],
+        small[0],
+        small[1],
         grad_attn_gain,
         grad_mlp_gain,
         grad_router,

time: 1650 us -> 1090 us (0.66)
  local copies, waits for them, and re-layouts: 267 us -> 44.1 us
  waiting for transfers between devices: 540 us -> 372 us
  other arithmetic: 214 us -> 103 us
  blocking collectives: 57.4 us -> 0 us
  Pallas kernels: 199 us -> 234 us
  matrix products: 153 us -> 125 us
    ppermute x98 -> x91, waiting for transfers between devices: 512 us -> 371 us  [the longest x24 171 us: line_gather(): lax.ppermute(behind, 'tp', [(i + 1, i) for i in range(count - s)])]
    unnamed x319 -> x184, local copies, waits for them, and re-layouts: 134 us -> 12.8 us
    pallas_call x3 -> x10, Pallas kernels: 77.1 us -> 113 us  [the longest x2 70.7 us: hidden(): pl.pallas_call(kernel, grid=(experts,), in_specs=[full, full, mat(0), mat...]
    psum x1 -> x0, blocking collectives: 35.5 us -> none  [on_device(): grad_attn_gain = lax.psum(last, 'tp') / a_gain[:, 0]]
    another operation x14 -> x6, other arithmetic: 32.7 us -> 2.5 us  [the longest x1 10.6 us: on_device(): moe_grad = jnp.stack(terms).reshape(3, 2, piece, local, span)]
    dot_general x37 -> x13, matrix products: 153 us -> 125 us  [dot(): return lax.dot_general(a, b, dims, preferred_element_type=F32)]
    unnamed x3 -> x8, waiting for transfers between devices: 28.2 us -> 0.13 us
    reshape x4 -> x11, local copies, waits for them, and re-layouts: 23.2 us -> 1.31 us  [the longest x3 0.77 us: on_device(): gains.reshape(fsdp, 2, heads, narrow).transpose(1, 2, 0, 3)]
  transfers between devices with their start and end apart: 110 -> 109, of which waited for: 40 -> 48; matrix products, arithmetic and copies ran while one was open for 29% -> 21% of each run, Pallas kernels for 6% -> 12%
where the time goes in v2:
time: 1090 us; the launch traced here: 1080 us
  waiting for transfers between devices  372 us (34%)
  Pallas kernels  234 us (21%)
  starting transfers between devices  188 us (17%)
  matrix products  125 us (11%)
  other arithmetic  103 us (9%)
  local copies, waits for them, and re-layouts  44.1 us (4%)
  between operations  16.5 us (2%)
    ppermute x24, waiting for transfers between devices, line_gather(): lax.ppermute(behind, 'tp', [(i + 1, i) for i in range(count - s)])  171 us
    dot_general x13, matrix products, dot(): return lax.dot_general(a, b, dims, preferred_element_type=F32)  125 us
    ppermute x12, waiting for transfers between devices, line_scatter(): up = lax.ppermute(send_up, 'tp', [(i, i + 1) for i in range(count - s)])  116 us
    pallas_call x4, Pallas kernels, mix(): pl.pallas_call(mix_kernel, grid=(cols // tile,), in_specs=specs, out_spec...  78.6 us
    pallas_call x2, Pallas kernels, hidden(): pl.pallas_call(kernel, grid=(experts,), in_specs=[full, full, mat(0), mat...  70.7 us
    ppermute x12, starting transfers between devices, line_scatter(): up = lax.ppermute(send_up, 'tp', [(i, i + 1) for i in range(count - s)])  55.2 us
    ppermute x24, starting transfers between devices, line_gather(): lax.ppermute(ahead, 'tp', [(i, i + 1) for i in range(s - 1, count - 1)])  47.8 us
    convert_element_type x12, other arithmetic, line_scatter(): send_up, send_down = (send_up.astype(BF), send_down.astype(BF))  38 us
  transfers between devices with their start and end apart: 109, of which 48 were waited for; matrix products, arithmetic and copies ran while one was open for 21% of the time, Pallas kernels for 12%

profile of v2, /device:TPU:0, one launch (start us, length us, event | category | flops | bytes accessed | tf_op | source)
XLA Modules:
  0.0 1082.1 jit_solution(8752814846356850586)
XLA Ops:
  88.6 12.6 %collective-permute-done.10.refs_7_ = bf16[128,2048]{1,0:T(8,128)(2,1)S(1)} collective-permute-done((bf16[128,2048]{1,0:T(8,128)(2,1)}, bf16[128,2048]{1,0:T(8,128)(2,1)S(1)}, u32[]{:S(2)}, u32[]{:S(2)}) %collective-permute-start.10) | collective-permute-done | bytes 524320 | tf_op jit(solution)/shard_map/ppermute | solution.py:63
  101.2 10.8 %collective-permute-done.4.refs_0_ = bf16[128,2048]{1,0:T(8,128)(2,1)S(1)} collective-permute-done((bf16[128,2048]{1,0:T(8,128)(2,1)}, bf16[128,2048]{1,0:T(8,128)(2,1)S(1)}, u32[]{:S(2)}, u32[]{:S(2)}) %collective-permute-start.4) | collective-permute-done | bytes 524320 | tf_op jit(solution)/shard_map/ppermute | solution.py:63
  167.8 11.2 %collective-permute-done.23.refs_8_ = bf16[128,2048]{1,0:T(8,128)(2,1)} collective-permute-done((bf16[128,2048]{1,0:T(8,128)(2,1)}, bf16[128,2048]{1,0:T(8,128)(2,1)}, u32[]{:S(2)}, u32[]{:S(2)}) %collective-permute-start.23) | collective-permute-done | bytes 524320 | tf_op jit(solution)/shard_map/ppermute | solution.py:63
  202.5 17.0 %collective-permute-done.28.kr_ref = bf16[1024,512]{1,0:T(8,128)(2,1)S(1)} collective-permute-done((bf16[1024,512]{1,0:T(8,128)(2,1)}, bf16[1024,512]{1,0:T(8,128)(2,1)S(1)}, u32[]{:S(2)}, u32[]{:S(2)}) %collective-permute-start.28) | collective-permute-done | bytes 1048608 | tf_op jit(solution)/shard_map/ppermute | solution.py:690
  225.8 12.6 %collective-permute-done.27.refs_7_ = bf16[128,2048]{1,0:T(8,128)(2,1)S(1)} collective-permute-done((bf16[128,2048]{1,0:T(8,128)(2,1)}, bf16[128,2048]{1,0:T(8,128)(2,1)S(1)}, u32[]{:S(2)}, u32[]{:S(2)}) %collective-permute-start.27) | collective-permute-done | bytes 524320 | tf_op jit(solution)/shard_map/ppermute | solution.py:63
  247.0 12.0 %attend.1 = bf16[1024,512]{1,0:T(8,128)(2,1)} custom-call(s32[1]{0:T(128)} %bitcast.cont_ref, bf16[1024,512]{1,0:T(8,128)(2,1)} %get-tuple-element.148.q_ref, bf16[1024,512]{1,0:T(8,128)(2,1)} %get-tuple-element.149.k_ref, bf16[1024,512]{1,0:T(8,128)(2,1)} %copy-done.34, bf16[1024,512]{1,0:T(8,128)(2,1)} %copy-done.83, ...), custom_call_target="tpu_custom_call" | custom-call | flops 3221225472 | bytes 6291456 | tf_op jit(solution)/shard_map/attend/pallas_call | solution.py:321
  268.7 18.5 %collective-permute-done.29 = bf16[256,2048]{1,0:T(8,128)(2,1)S(1)} collective-permute-done((bf16[256,2048]{1,0:T(8,128)(2,1)S(1)}, bf16[256,2048]{1,0:T(8,128)(2,1)S(1)}, u32[]{:S(2)}, u32[]{:S(2)}) %collective-permute-start.29) | collective-permute-done | bytes 1048608 | tf_op jit(solution)/shard_map/ppermute | solution.py:121
  304.0 12.1 %collective-permute-done.31 = bf16[256,2048]{1,0:T(8,128)(2,1)} collective-permute-done((bf16[256,2048]{1,0:T(8,128)(2,1)}, bf16[256,2048]{1,0:T(8,128)(2,1)}, u32[]{:S(2)}, u32[]{:S(2)}) %collective-permute-start.31) | collective-permute-done | bytes 1048608 | tf_op jit(solution)/shard_map/ppermute | solution.py:121
  438.6 35.4 %hidden.2 = (bf16[2048,2048]{1,0:T(8,128)(2,1)}, bf16[2048,2176]{1,0:T(8,128)(2,1)}, bf16[2048,2048]{1,0:T(8,128)(2,1)}, f32[1024,8]{1,0:T(8,128)}) custom-call(bf16[1024,2048]{1,0:T(8,128)(2,1)} %assemble.6.x_ref, bf16[1024,2048]{1,0:T(8,128)(2,1)} %assemble.5.c_ref, bf16[2048,4096]{1,0:T(8,128)(2,1)} %all-gather.6.cloned.1.call-done.g_ref.u_ref.refs_2_.refs_3_.refs_1_, ...), custom_call_target="tpu_custom_call" | custom-call | flops 25769803776 | bytes 58720256 | tf_op jit(solution)/shard_map/hidden/pallas_call | solution.py:432
  474.0 35.3 %hidden.3 = (bf16[2048,2048]{1,0:T(8,128)(2,1)}, bf16[2048,2176]{1,0:T(8,128)(2,1)}, bf16[2048,2048]{1,0:T(8,128)(2,1)}, f32[1024,8]{1,0:T(8,128)}) custom-call(bf16[1024,2048]{1,0:T(8,128)(2,1)} %collective-permute-done.49.refs_0_, bf16[1024,2048]{1,0:T(8,128)(2,1)} %collective-permute-done.40.refs_1_, ...), custom_call_target="tpu_custom_call", output_to_operand_aliasing={{0}: (6, {}), {1}: (7, {}), {2}: (8, {})} | custom-call | flops 25769803776 | bytes 58720256 | tf_op jit(solution)/shard_map/hidden/pallas_call | solution.py:432
  513.8 25.7 %mix.7 = bf16[1024,2048]{1,0:T(8,128)(2,1)} custom-call(bf16[2048,2176]{1,0:T(8,128)(2,1)} %get-tuple-element.185.refs_0_, bf16[2048,4096]{1,0:T(8,128)(2,1)} %all-gather.6.cloned.1.call-done.g_ref.u_ref.refs_2_.refs_3_.refs_1_, bf16[2048,2048]{1,0:T(8,128)(2,1)} %get-tuple-element.187.refs_2_, ...), custom_call_target="tpu_custom_call" | custom-call | flops 17716740096 | bytes 34340864 | tf_op jit(solution)/shard_map/mix/pallas_call | solution.py:467
  541.7 25.8 %mix.6 = bf16[1024,2048]{1,0:T(8,128)(2,1)} custom-call(bf16[2048,2176]{1,0:T(8,128)(2,1)} %get-tuple-element.185.refs_0_, bf16[2048,4096]{1,0:T(8,128)(2,1)} %all-gather.6.cloned.1.call-done.g_ref.u_ref.refs_2_.refs_3_.refs_1_, bf16[2048,2048]{1,0:T(8,128)(2,1)} %get-tuple-element.187.refs_2_, ...), custom_call_target="tpu_custom_call" | custom-call | flops 17716740096 | bytes 34340864 | tf_op jit(solution)/shard_map/mix/pallas_call | solution.py:467
  571.8 22.8 %convolution_convert_fusion.2 = bf16[2048,2048]{1,0:T(8,128)(2,1)} fusion(bf16[2048,2048]{1,0:T(8,128)(2,1)} %get-tuple-element.188.refs_0_, bf16[1024,2048]{1,0:T(8,128)(2,1)} %collective-permute-done.40.refs_1_, bf16[1024,2048]{1,0:T(8,128)(2,1)S(1)} %copy-done.17), kind=kOutput, calls=%fused_computation.3 | convolution fusion | flops 17200840704 | bytes 25165824 | tf_op jit(solution)/shard_map/dot_general | solution.py:24
  603.4 15.8 %collective-permute-done.54 = bf16[256,2048]{1,0:T(8,128)(2,1)S(1)} collective-permute-done((bf16[256,2048]{1,0:T(8,128)(2,1)S(1)}, bf16[256,2048]{1,0:T(8,128)(2,1)S(1)}, u32[]{:S(2)}, u32[]{:S(2)}) %collective-permute-start.54) | collective-permute-done | bytes 1048608 | tf_op jit(solution)/shard_map/ppermute | solution.py:121
  621.6 23.5 %convolution_convert_fusion = bf16[2048,2176]{1,0:T(8,128)(2,1)} fusion(bf16[2048,2048]{1,0:T(8,128)(2,1)S(1)} %constant_dynamic-update-slice_fusion, bf16[2048,2176]{1,0:T(8,128)(2,1)S(1)} %maximum_dynamic-update-slice_fusion), kind=kOutput, calls=%fused_computation | convolution fusion | flops 18258067456 | bytes 26214400 | tf_op jit(solution)/shard_map/dot_general | solution.py:24
  650.5 21.5 %collective-permute-done.56 = bf16[256,2048]{1,0:T(8,128)(2,1)S(1)} collective-permute-done((bf16[256,2048]{1,0:T(8,128)(2,1)S(1)}, bf16[256,2048]{1,0:T(8,128)(2,1)S(1)}, u32[]{:S(2)}, u32[]{:S(2)}) %collective-permute-start.56) | collective-permute-done | bytes 1048608 | tf_op jit(solution)/shard_map/ppermute | solution.py:121
  677.0 23.9 %convolution_convert_fusion.3 = bf16[2048,2048]{1,0:T(8,128)(2,1)} fusion(bf16[2048,2048]{1,0:T(8,128)(2,1)} %copy-done.23, bf16[2048,2048]{1,0:T(8,128)(2,1)} %get-tuple-element.187.refs_2_), kind=kOutput, calls=%fused_computation.4 | convolution fusion | flops 17184063488 | bytes 25165824 | tf_op jit(solution)/shard_map/dot_general | solution.py:24
  708.9 13.7 %mix.5 = bf16[1024,2048]{1,0:T(8,128)(2,1)} custom-call(bf16[2048,2048]{1,0:T(8,128)(2,1)} %get-tuple-element.188.refs_0_, bf16[2048,2048]{1,0:T(8,128)(2,1)} %all-gather.8.cloned.1.call-done.d_ref.refs_4_.refs_1_), custom_call_target="tpu_custom_call" | custom-call | flops 8589934592 | bytes 20971520 | tf_op jit(solution)/shard_map/mix/pallas_call | solution.py:467
  796.0 13.3 %mix.4 = bf16[1024,2048]{1,0:T(8,128)(2,1)} custom-call(bf16[2048,2048]{1,0:T(8,128)(2,1)} %get-tuple-element.188.refs_0_, bf16[2048,2048]{1,0:T(8,128)(2,1)} %all-gather.8.cloned.1.call-done.d_ref.refs_4_.refs_1_), custom_call_target="tpu_custom_call" | custom-call | flops 8589934592 | bytes 20971520 | tf_op jit(solution)/shard_map/mix/pallas_call | solution.py:467
  833.1 18.0 %attend_back.1 = (f32[1024,512]{1,0:T(8,128)}, f32[1024,512]{1,0:T(8,128)}, f32[1024,512]{1,0:T(8,128)}, bf16[1024,512]{1,0:T(8,128)(2,1)}, bf16[1024,512]{1,0:T(8,128)(2,1)}) custom-call(s32[1]{0:T(128)} %bitcast.cont_ref, bf16[1024,512]{1,0:T(8,128)(2,1)} %get-tuple-element.148.q_ref, bf16[1024,512]{1,0:T(8,128)(2,1)} %get-tuple-element.149.k_ref, ...), custom_call_target="tpu_custom_call" | custom-call | flops 8053063680 | bytes 15728640 | tf_op jit(solution)/shard_map/attend_back/pallas_call | solution.py:382
  858.8 12.2 %collective-permute-done.74 = bf16[256,2048]{1,0:T(8,128)(2,1)S(1)} collective-permute-done((bf16[256,2048]{1,0:T(8,128)(2,1)S(1)}, bf16[256,2048]{1,0:T(8,128)(2,1)S(1)}, u32[]{:S(2)}, u32[]{:S(2)}) %collective-permute-start.74) | collective-permute-done | bytes 1048608 | tf_op jit(solution)/shard_map/ppermute | solution.py:121
  887.8 27.3 %collective-permute-done.82 = bf16[1024,512]{1,0:T(8,128)(2,1)S(1)} collective-permute-done((bf16[1024,512]{1,0:T(8,128)(2,1)}, bf16[1024,512]{1,0:T(8,128)(2,1)S(1)}, u32[]{:S(2)}, u32[]{:S(2)}) %collective-permute-start.82) | collective-permute-done | bytes 1048608 | tf_op jit(solution)/shard_map/ppermute | solution.py:768
  943.5 11.2 %fusion.6 = bf16[1024,2048]{1,0:T(8,128)(2,1)} fusion(bf16[1024,1536]{1,0:T(8,128)(2,1)S(1)} %pad_maximum_fusion.2, bf16[2048,2176]{1,0:T(8,128)(2,1)} %all-gather.4.cloned.1.call-done), kind=kOutput, calls=%fused_computation.14 | convolution fusion | flops 6444548096 | bytes 13631488 | tf_op jit(solution)/shard_map/dot_general | solution.py:24
  1043.7 11.3 %collective-permute-done.87 = bf16[256,2048]{1,0:T(8,128)(2,1)S(1)} collective-permute-done((bf16[256,2048]{1,0:T(8,128)(2,1)S(1)}, bf16[256,2048]{1,0:T(8,128)(2,1)S(1)}, u32[]{:S(2)}, u32[]{:S(2)}) %collective-permute-start.87) | collective-permute-done | bytes 1048608 | tf_op jit(solution)/shard_map/ppermute | solution.py:121
  (550 shorter events, 622.0 us)
Async XLA Ops:
  7.2 72.7 %all-gather.4.cloned.1.call-start = ((), (), s32[]{:S(2)}) async-start(), calls=%async_computation.5 | async-start | bytes 10027008 | tf_op jit(solution)/shard_map/all_gather | solution.py:641
  14.7 423.9 %all-gather.8.cloned.1.call-start = ((), (), s32[]{:S(2)}) async-start(), calls=%async_computation.7 | async-start | bytes 10485760 | tf_op jit(solution)/shard_map/all_gather | solution.py:670
  23.9 37.0 %collective-permute-start.51 = (bf16[256,2048]{1,0:T(8,128)(2,1)}, bf16[256,2048]{1,0:T(8,128)(2,1)}, u32[]{:S(2)}, u32[]{:S(2)}) collective-permute-start(bf16[256,2048]{1,0:T(8,128)(2,1)} %slice_bitcast_fusion), channel_id=1, source_target_pairs={{0,4},{4,0},{8,12},{12,8},{16,20},{20,16},{24,28},{28,24},{1,5},{5... | collective-permute-start | bytes 3145736 | tf_op jit(solution)/shard_map/ppermute | solution.py:39
  79.9 358.7 %all-gather.6.cloned.1.call-start = ((), (), s32[]{:S(2)}) async-start(), calls=%async_computation.6 | async-start | bytes 20971520 | tf_op jit(solution)/shard_map/all_gather | solution.py:670
  84.2 113.2 %collective-permute-start.50 = (bf16[256,4096]{1,0:T(8,128)(2,1)}, bf16[256,4096]{1,0:T(8,128)(2,1)}, u32[]{:S(2)}, u32[]{:S(2)}) collective-permute-start(bf16[256,4096]{1,0:T(8,128)(2,1)} %pad_maximum_fusion.4), channel_id=1, source_target_pairs={{0,4},{4,0},{8,12},{12,8},{16,20},{20,16},{24,28},{28,24},{1,5},{5... | collective-permute-start | bytes 6291464 | tf_op jit(solution)/shard_map/ppermute | solution.py:39
  151.4 35.6 %collective-permute-start.19 = (bf16[1024,512]{1,0:T(8,128)(2,1)S(1)}, bf16[1024,512]{1,0:T(8,128)(2,1)}, u32[]{:S(2)}, u32[]{:S(2)}) collective-permute-start(bf16[1024,512]{1,0:T(8,128)(2,1)S(1)} %slice.264.v_ref), channel_id=1, source_target_pairs={{0,16},{4,20},{8,24},{12,28},{1,17},{5,21},{9,25},{13,29},{2,18},{... | collective-permute-start | bytes 3145736 | tf_op jit(solution)/shard_map/ppermute | solution.py:680
  220.5 697.5 %reduce-scatter.6.cloned.1.call-start = ((), (), s32[]{:S(2)}) async-start(), calls=%async_computation.8 | async-start | bytes 10485760 | tf_op jit(solution)/shard_map/reduce_scatter | solution.py:740
  302.3 82.4 %collective-permute-start.40 = (bf16[1024,2048]{1,0:T(8,128)(2,1)}, bf16[1024,2048]{1,0:T(8,128)(2,1)}, u32[]{:S(2)}, u32[]{:S(2)}) collective-permute-start(bf16[1024,2048]{1,0:T(8,128)(2,1)} %assemble.5.c_ref), channel_id=1, source_target_pairs={{0,4},{4,0},{8,12},{12,8},{16,20},{20,16},{24,28},{28,24},{1,5},{5... | collective-permute-start | bytes 12582920 | tf_op jit(solution)/shard_map/ppermute | solution.py:39
  594.6 348.9 %reduce-scatter.8.cloned.1.call-start = ((), (), s32[]{:S(2)}) async-start(), calls=%async_computation.9 | async-start | bytes 11141120 | tf_op jit(solution)/shard_map/reduce_scatter | solution.py:740
  645.1 328.8 %reduce-scatter.14.cloned.1.call-start = ((), (), s32[]{:S(2)}) async-start(), calls=%async_computation.12 | async-start | bytes 10485760 | tf_op jit(solution)/shard_map/reduce_scatter | solution.py:740
  700.9 302.7 %reduce-scatter.10.cloned.1.call-start = ((), (), s32[]{:S(2)}) async-start(), calls=%async_computation.10 | async-start | bytes 2359296 | tf_op jit(solution)/shard_map/reduce_scatter | solution.py:799
  722.6 86.8 %collective-permute-start.52 = (bf16[1024,2048]{1,0:T(8,128)(2,1)}, bf16[1024,2048]{1,0:T(8,128)(2,1)}, u32[]{:S(2)}, u32[]{:S(2)}) collective-permute-start(bf16[1024,2048]{1,0:T(8,128)(2,1)} %mix.5), channel_id=1, source_target_pairs={{0,4},{4,0},{8,12},{12,8},{16,20},{20,16},{24,28},{28,24},{1,5},{5... | collective-permute-start | bytes 12582920 | tf_op jit(solution)/shard_map/ppermute | solution.py:39
  782.0 32.1 %collective-permute-start.70 = (bf16[128,2048]{1,0:T(8,128)(2,1)S(1)}, bf16[128,2048]{1,0:T(8,128)(2,1)S(1)}, u32[]{:S(2)}, u32[]{:S(2)}) collective-permute-start(bf16[128,2048]{1,0:T(8,128)(2,1)S(1)} %collective-permute-done.69.refs_8_), channel_id=1, source_target_pairs={{1,0},{5,4},{9,8},{13,12},{17,16},{21,20},{25,24},{29,28}} | collective-permute-start | bytes 1572872 | tf_op jit(solution)/shard_map/ppermute | solution.py:63
  855.8 62.3 %collective-permute-start.78 = (bf16[1024,512]{1,0:T(8,128)(2,1)}, bf16[1024,512]{1,0:T(8,128)(2,1)}, u32[]{:S(2)}, u32[]{:S(2)}) collective-permute-start(bf16[1024,512]{1,0:T(8,128)(2,1)} %get-tuple-element.201), channel_id=1, source_target_pairs={{16,0},{20,4},{24,8},{28,12},{17,1},{21,5},{25,9},{29,13},{18,2},{... | collective-permute-start | bytes 3145736 | tf_op jit(solution)/shard_map/ppermute | solution.py:768
  857.1 58.0 %collective-permute-start.82 = (bf16[1024,512]{1,0:T(8,128)(2,1)}, bf16[1024,512]{1,0:T(8,128)(2,1)S(1)}, u32[]{:S(2)}, u32[]{:S(2)}) collective-permute-start(bf16[1024,512]{1,0:T(8,128)(2,1)} %get-tuple-element.213), channel_id=1, source_target_pairs={{16,0},{20,4},{24,8},{28,12},{17,1},{21,5},{25,9},{29,13},{18,2},{... | collective-permute-start | bytes 3145736 | tf_op jit(solution)/shard_map/ppermute | solution.py:768
  875.4 58.2 %collective-permute-start.76 = (bf16[256,2048]{1,0:T(8,128)(2,1)}, bf16[256,2048]{1,0:T(8,128)(2,1)}, u32[]{:S(2)}, u32[]{:S(2)}) collective-permute-start(bf16[256,2048]{1,0:T(8,128)(2,1)} %get-tuple-element.204), channel_id=1, source_target_pairs={{0,1},{1,2},{2,3},{4,5},{5,6},{6,7},{8,9},{9,10},{10,11},{12,13},{... | collective-permute-start | bytes 3145736 | tf_op jit(solution)/shard_map/ppermute | solution.py:121
  882.7 50.8 %collective-permute-start.77 = (bf16[256,2048]{1,0:T(8,128)(2,1)}, bf16[256,2048]{1,0:T(8,128)(2,1)}, u32[]{:S(2)}, u32[]{:S(2)}) collective-permute-start(bf16[256,2048]{1,0:T(8,128)(2,1)} %get-tuple-element.205), channel_id=1, source_target_pairs={{1,0},{2,1},{3,2},{5,4},{6,5},{7,6},{9,8},{10,9},{11,10},{13,12},{... | collective-permute-start | bytes 3145736 | tf_op jit(solution)/shard_map/ppermute | solution.py:122
  887.7 171.5 %reduce-scatter.12.cloned.1.call-start = ((), (), s32[]{:S(2)}) async-start(), calls=%async_computation.11 | async-start | bytes 7077888 | tf_op jit(solution)/shard_map/reduce_scatter | solution.py:799
  971.9 35.2 %collective-permute-start.92 = (bf16[256,2176]{1,0:T(8,128)(2,1)}, bf16[256,2176]{1,0:T(8,128)(2,1)}, u32[]{:S(2)}, u32[]{:S(2)}) collective-permute-start(bf16[256,2176]{1,0:T(8,128)(2,1)} %get-tuple-element.359), channel_id=1, source_target_pairs={{0,4},{4,0},{8,12},{12,8},{16,20},{20,16},{24,28},{28,24},{1,5},{5... | collective-permute-start | bytes 3342344 | tf_op jit(solution)/shard_map/ppermute | solution.py:39
  973.3 37.4 %collective-permute-start.94 = (bf16[256,2048]{1,0:T(8,128)(2,1)}, bf16[256,2048]{1,0:T(8,128)(2,1)}, u32[]{:S(2)}, u32[]{:S(2)}) collective-permute-start(bf16[256,2048]{1,0:T(8,128)(2,1)} %get-tuple-element.361), channel_id=1, source_target_pairs={{0,4},{4,0},{8,12},{12,8},{16,20},{20,16},{24,28},{28,24},{1,5},{5... | collective-permute-start | bytes 3145736 | tf_op jit(solution)/shard_map/ppermute | solution.py:39
  977.3 33.7 %collective-permute-start.93 = (bf16[256,2048]{1,0:T(8,128)(2,1)}, bf16[256,2048]{1,0:T(8,128)(2,1)}, u32[]{:S(2)}, u32[]{:S(2)}) collective-permute-start(bf16[256,2048]{1,0:T(8,128)(2,1)} %get-tuple-element.363), channel_id=1, source_target_pairs={{0,4},{4,0},{8,12},{12,8},{16,20},{20,16},{24,28},{28,24},{1,5},{5... | collective-permute-start | bytes 3145736 | tf_op jit(solution)/shard_map/ppermute | solution.py:39
  988.2 33.5 %collective-permute-start.86 = (bf16[256,2048]{1,0:T(8,128)(2,1)}, bf16[256,2048]{1,0:T(8,128)(2,1)}, u32[]{:S(2)}, u32[]{:S(2)}) collective-permute-start(bf16[256,2048]{1,0:T(8,128)(2,1)} %get-tuple-element.218), channel_id=1, source_target_pairs={{2,1},{3,2},{6,5},{7,6},{10,9},{11,10},{14,13},{15,14},{18,17},{19... | collective-permute-start | bytes 3145736 | tf_op jit(solution)/shard_map/ppermute | solution.py:122
  1007.9 34.9 %collective-permute-start.100 = (f32[256,128]{1,0:T(8,128)S(1)}, f32[256,128]{1,0:T(8,128)S(1)}, u32[]{:S(2)}, u32[]{:S(2)}) collective-permute-start(f32[256,128]{1,0:T(8,128)S(1)} %convert_add_fusion.13), channel_id=1, source_target_pairs={{0,3},{1,0},{2,1},{3,2},{4,7},{5,4},{6,5},{7,6},{8,11},{9,8},{10,9... | collective-permute-start | bytes 393224 | tf_op jit(solution)/shard_map/ppermute | solution.py:140
  1010.8 32.1 %collective-permute-start.98 = (f32[256,128]{1,0:T(8,128)S(1)}, f32[256,128]{1,0:T(8,128)S(1)}, u32[]{:S(2)}, u32[]{:S(2)}) collective-permute-start(f32[256,128]{1,0:T(8,128)S(1)} %convert_add_fusion.13), channel_id=1, source_target_pairs={{0,1},{1,2},{2,3},{3,0},{4,5},{5,6},{6,7},{7,4},{8,9},{9,10},{10,1... | collective-permute-start | bytes 393224 | tf_op jit(solution)/shard_map/ppermute | solution.py:140
  (175 other events, 3090.6 us)
Sparse Core Ops, SparseCore 0:
  14.8 59.2 all-gather.3
  80.0 94.6 all-gather.7
  219.7 159.4 all-gather.5
  594.7 91.0 reduce-scatter.5
  689.2 90.6 reduce-scatter.7
  783.1 86.3 reduce-scatter.13
  887.9 59.0 reduce-scatter.9
  963.6 61.9 reduce-scatter.11

commit v3 on v2

--- a/solution.py
+++ b/solution.py
@@ -678,27 +678,27 @@
     forth = [(i, i + half) for i in range(half)]
     value_low = raw[:, 2 * cols :].astype(BF)
     value_far = lax.ppermute(value_low, "fsdp", forth)
-    upstream, steps_up = line_gather(cotangent, gates={1: steps_one[3]})
     query_key = after(raw, value_low)
     totals = jnp.stack(
         [jnp.sum(query_key[:, :cols] ** 2, axis=1), jnp.sum(query_key[:, cols : 2 * cols] ** 2, axis=1)]
     )
-    totals = total_tp(after(totals, *steps_up[1]))
+    totals = total_tp(totals)
     norms = lax.rsqrt(totals / dim + EPS).T
+    upstream, steps_up = line_gather(cotangent, gates={1: [norms]})
     cos, sin = angles(seg_ids)
-    query_rot, key_rot = turn(raw, after(norms, value_far, *steps_up[2]), cos, sin, gains)
+    query_rot, key_rot = turn(raw, norms, cos, sin, gains)
     key_far = lax.ppermute(key_rot, "fsdp", forth)
     cont = (place >= half).astype(jnp.int32).reshape(1)
     seg_col, seg_row = seg_ids[:, None], seg_ids[None, :]
-    mats = over_chips(after(rows, key_far, value_far))
+    mats = over_chips(after(rows, key_far, value_far, *steps_up[3]))
 
     upstream_far = swap_core(upstream)
 
     attended = attend(
-        cont, after(query_rot, *steps_up[3]), key_rot, value_low, key_far, value_far, seg_col, seg_row
+        cont, after(query_rot, *steps_up[1]), key_rot, value_low, key_far, value_far, seg_col, seg_row
     )
     attn_part = dot(attended, out_mat, NT).astype(BF)
-    attn_out, _, _ = line_scatter(shares(attn_part))
+    attn_out, _, _ = line_scatter(shares(attn_part), {1: steps_up[3]})
     after_attn = stream + attn_out
     norm_second = inverse_norm(after_attn)
     hat_two = after_attn * norm_second
@@ -731,43 +731,56 @@
     def both_cores(own, got):
         return [a.astype(F32) + b.astype(F32) for a, b in zip(shares(own), shares(got))]
 
+    def scattered(value):
+        return lax.psum_scatter(value, "fsdp", scatter_dimension=0, tiled=True, axis_index_groups=groups)
+
+    dg = lax.dynamic_update_slice(dg, jnp.concatenate([gl_own, gl_far], axis=0), (0, local * span))
+    wide_x = jnp.concatenate([mlp_own, mlp_far], axis=0)
+    down_term = dot(wide_c, act, TN).astype(BF)
+    down_sum = scattered(down_term)
+
+    gl_far = after(gl_far, down_term)
     back_far = mix([(dg, mats, 0, 1), (du, mats, 1, 1), (gl_far, router_mat, 0, 0)], BF, tokens)
     back_got = swap_core(back_far)
+    gl_own = after(gl_own, back_far)
     back_own = mix([(dg, mats, 0, 0), (du, mats, 1, 0), (gl_own, router_mat, 0, 0)], BF, tokens)
-    grad_scaled, _, back_sends = line_scatter(both_cores(back_own, back_got))
-
-    def scattered(value):
-        return lax.psum_scatter(value, "fsdp", scatter_dimension=0, tiled=True, axis_index_groups=groups)
-
-    dg = lax.dynamic_update_slice(
-        after(dg, back_own, back_got), jnp.concatenate([gl_own, gl_far], axis=0), (0, local * span)
-    )
-    wide_x = jnp.concatenate([after(mlp_own, back_own), mlp_far], axis=0)
-    terms = [
-        dot(left, after(right, *gate), TN).astype(BF)
-        for left, right, gate in zip((wide_c, wide_x, wide_x), (act, dg, du), back_sends[1:])
-    ]
-    terms = [terms[1], terms[2], terms[0]]
-    sums = [scattered(t) for t in terms]
-    out_far = mix([(act, low_mat, 0, 1)], BF, tokens)
-    out_own = mix([(act, low_mat, 0, 0)], BF, tokens)
-    out_got = swap_core(out_far)
+    grad_scaled, _, back_sends = line_scatter(both_cores(back_own, back_got), {2: [down_sum]})
+    gate_term = dot(wide_x, after(dg, back_own, back_got), TN).astype(BF)
+    gate_sum = scattered(gate_term)
+    up_term = dot(wide_x, after(du, gate_term, *back_sends[2]), TN).astype(BF)
+    up_sum = scattered(up_term)
+    sums = [gate_sum, up_sum, down_sum]
 
     grad_after = cotangent.astype(F32) + norm_second * (
         grad_scaled - hat_two * jnp.mean(grad_scaled * hat_two, axis=-1, keepdims=True)
     )
-    grad_attn, _ = line_gather(after(grad_after.astype(BF), *terms))
-
-    grad_attended = after(dot(grad_attn, out_mat).astype(BF), out_far, out_own)
+    grad_after_low = after(grad_after.astype(BF), up_term)
+    grad_attn, _ = line_gather(grad_after_low, gates={2: [gate_sum]})
+
+    act = after(act, back_own, *back_sends[1])
+    out_far = mix([(act, low_mat, 0, 1)], BF, tokens)
+    out_got = swap_core(out_far)
+    out_own = mix([(act, low_mat, 0, 0)], BF, tokens)
+    out_low = (out_own.astype(F32) + out_got.astype(F32)).astype(BF)
+    out_total = lax.psum_scatter(after(out_low, up_sum, grad_attn), "tp", scatter_dimension=0, tiled=True)
+    block_out = after_attn + out_total.astype(F32)
+
+    grad_attended = after(dot(grad_attn, out_mat).astype(BF), out_low)
     dq, dk, dv, dk_far, dv_far = attend_back(
         cont, query_rot, key_rot, value_low, key_far, value_far, grad_attended, seg_col, seg_row
     )
-    out_total, out_steps, _ = line_scatter(both_cores(out_own, out_got), {1: [grad_attended], 2: [dk_far]})
-    block_out = after_attn + out_total
     back_pairs = [(i + half, i) for i in range(half)]
     dk_got, dv_got = lax.ppermute(dk_far, "fsdp", back_pairs), lax.ppermute(dv_far, "fsdp", back_pairs)
+
+    sums = [after(t, dk_far) for t in sums]
+    mine = [lax.dynamic_slice_in_dim(t, core * piece, piece, 0) for t in sums]
+    theirs = [swap_core(lax.dynamic_slice_in_dim(t, (1 - core) * piece, piece, 0)) for t in sums]
+    grad_gate, grad_up, grad_down = moe_unpack(core_arg, mine, theirs, norm_gains, experts, local)
+    router_hat = total_tp(sum(t[0][:, local * span : local * span + experts].astype(F32) for t in (mine, theirs)))
+    grad_router = router_hat * norm_gains[:, 1:2]
+    gain_term = jnp.sum(gate_weight.astype(F32) * grad_gate + up_weight.astype(F32) * grad_up, axis=(0, 2))
     u_query, u_key, dots, gain_parts = turn_back(
-        dq, after(dk, *out_steps[1], sums[2]), dk_got, raw, norms, cos, sin, gains
+        dq, after(dk, sums[1], grad_gate, grad_up, grad_down), dk_got, raw, norms, cos, sin, gains
     )
     dots = total_tp(dots.T).T
     grad_value = (dv + dv_got.astype(F32)).astype(BF)
@@ -779,21 +792,13 @@
     grad_raw = jnp.concatenate(
         [raw_back(u_query, raw[:, :cols], 0), raw_back(u_key, raw[:, cols : 2 * cols], 1), grad_value], axis=1
     )
-    normed_part = dot(after(grad_raw, block_out, sums[0]), qkv_mat, NT).astype(BF)
+    normed_part = dot(after(grad_raw, out_total), qkv_mat, NT).astype(BF)
     small = gain_parts.reshape(2, heads, fsdp, narrow).transpose(2, 0, 1, 3).reshape(fsdp, -1)
+    small = total_fsdp(small)
     grad_raw_later = after(grad_raw, normed_part)
     qkv_term = dot(normed, grad_raw_later, TN).astype(BF)
-    late = []
-    grad_hat, _, last_sends = line_scatter(shares(normed_part), {3: late})
-
-    sums = [after(t, *last_sends[1]) for t in sums]
-    mine = [lax.dynamic_slice_in_dim(t, core * piece, piece, 0) for t in sums]
-    theirs = [swap_core(lax.dynamic_slice_in_dim(t, (1 - core) * piece, piece, 0)) for t in sums]
-    grad_gate, grad_up, grad_down = moe_unpack(core_arg, mine, theirs, norm_gains, experts, local)
-    router_hat = total_tp(sum(t[0][:, local * span :].astype(F32) for t in (mine, theirs)))[:, :experts]
-    grad_router = router_hat * norm_gains[:, 1:2]
-    gate_term = jnp.sum(gate_weight.astype(F32) * grad_gate + up_weight.astype(F32) * grad_up, axis=(0, 2))
-    small = total_fsdp(after(small, *last_sends[1]))
+    grad_hat, _, last_sends = line_scatter(shares(normed_part), {3: [router_hat, gain_term, small]})
+
 
     def summed(value):
         return lax.psum_scatter(value, "fsdp", scatter_dimension=0, tiled=True).astype(F32)
@@ -806,7 +811,7 @@
     small = small.reshape(2, heads, narrow)
 
     attn_dots = sum(jnp.sum(w.astype(F32) * t, axis=1) for w, t in zip((query_weight, key_weight, value_weight), qkv_hat))
-    both_dots = total_tp(jnp.stack([attn_dots, gate_term / norm_gains[:, 1]]))
+    both_dots = total_tp(jnp.stack([attn_dots, gain_term / norm_gains[:, 1]]))
     grad_attn_gain = both_dots[0]
     grad_mlp_gain = both_dots[1] + jnp.sum(router_weight.astype(F32) * router_hat, axis=1)
     grad_hat = after(grad_hat, both_dots, grad_out_proj, *qkv_grad)

time: 1090 us -> 1040 us (0.954)
  waiting for transfers between devices: 372 us -> 340 us
  starting transfers between devices: 188 us -> 171 us
    ppermute x1, waiting for transfers between devices: 0.01 us -> 27.3 us  [on_device(): lax.ppermute(dk_far, 'fsdp', back_pairs)]
    ppermute x24, waiting for transfers between devices: 171 us -> 146 us  [line_gather(): lax.ppermute(behind, 'tp', [(i + 1, i) for i in range(count - s)])]
    ppermute x1, waiting for transfers between devices: 27.3 us -> 7.88 us  [on_device(): lax.ppermute(dv_far, 'fsdp', back_pairs)]
    ppermute x1, waiting for transfers between devices: 17 us -> 1.01 us  [on_device(): key_far = lax.ppermute(key_rot, 'fsdp', forth)]
    convert_element_type x12 -> x9, other arithmetic: 38 us -> 26.2 us  [line_scatter(): send_up, send_down = (send_up.astype(BF), send_down.astype(BF))]
    ppermute x12 -> x9, starting transfers between devices: 55.2 us -> 45 us  [line_scatter(): up = lax.ppermute(send_up, 'tp', [(i, i + 1) for i in range(count - s)])]
    ppermute x12 -> x9, waiting for transfers between devices: 116 us -> 117 us  [line_scatter(): up = lax.ppermute(send_up, 'tp', [(i, i + 1) for i in range(count - s)])]
  transfers between devices with their start and end apart: 109 -> 104, of which waited for: 48 -> 47; matrix products, arithmetic and copies ran while one was open for 21% -> 22% of each run, Pallas kernels for 12% -> 16%
where the time goes in v3:
time: 1040 us; the launch traced here: 1020 us
  waiting for transfers between devices  340 us (33%)
  Pallas kernels  234 us (22%)
  starting transfers between devices  171 us (16%)
  matrix products  127 us (12%)
  other arithmetic  98.6 us (9%)
  local copies, waits for them, and re-layouts  38.7 us (4%)
  between operations  15.9 us (2%)
    ppermute x24, waiting for transfers between devices, line_gather(): lax.ppermute(behind, 'tp', [(i + 1, i) for i in range(count - s)])  146 us
    dot_general x13, matrix products, dot(): return lax.dot_general(a, b, dims, preferred_element_type=F32)  127 us
    ppermute x9, waiting for transfers between devices, line_scatter(): up = lax.ppermute(send_up, 'tp', [(i, i + 1) for i in range(count - s)])  117 us
    pallas_call x4, Pallas kernels, mix(): pl.pallas_call(mix_kernel, grid=(cols // tile,), in_specs=specs, out_spec...  79 us
    pallas_call x2, Pallas kernels, hidden(): pl.pallas_call(kernel, grid=(experts,), in_specs=[full, full, mat(0), mat...  71 us
    ppermute x24, starting transfers between devices, line_gather(): lax.ppermute(ahead, 'tp', [(i, i + 1) for i in range(s - 1, count - 1)])  52.9 us
    ppermute x9, starting transfers between devices, line_scatter(): up = lax.ppermute(send_up, 'tp', [(i, i + 1) for i in range(count - s)])  45 us
    ppermute x24, starting transfers between devices, line_gather(): lax.ppermute(behind, 'tp', [(i + 1, i) for i in range(count - s)])  30.8 us
  transfers between devices with their start and end apart: 104, of which 47 were waited for; matrix products, arithmetic and copies ran while one was open for 22% of the time, Pallas kernels for 16%

profile of v3, /device:TPU:0, one launch (start us, length us, event | category | flops | bytes accessed | tf_op | source)
XLA Modules:
  0.0 1024.2 jit_solution(10540175914000035655)
XLA Ops:
  69.4 10.5 %collective-permute-done.3.refs_1_ = bf16[128,2048]{1,0:T(8,128)(2,1)} collective-permute-done((bf16[128,2048]{1,0:T(8,128)(2,1)}, bf16[128,2048]{1,0:T(8,128)(2,1)}, u32[]{:S(2)}, u32[]{:S(2)}) %collective-permute-start.3) | collective-permute-done | bytes 524320 | tf_op jit(solution)/shard_map/ppermute | solution.py:63
  99.7 9.6 collective-permute-done.4.refs_0_
  113.6 10.1 fusion.2.q_ref.k_ref
  181.6 10.9 %collective-permute-done.25.refs_8_ = bf16[128,2048]{1,0:T(8,128)(2,1)S(1)} collective-permute-done((bf16[128,2048]{1,0:T(8,128)(2,1)S(1)}, bf16[128,2048]{1,0:T(8,128)(2,1)S(1)}, u32[]{:S(2)}, u32[]{:S(2)}) %collective-permute-start.25) | collective-permute-done | bytes 524320 | tf_op jit(solution)/shard_map/ppermute | solution.py:63
  219.1 11.9 %attend.1 = bf16[1024,512]{1,0:T(8,128)(2,1)} custom-call(s32[1]{0:T(128)} %bitcast.cont_ref, bf16[1024,512]{1,0:T(8,128)(2,1)} %get-tuple-element.130.q_ref, bf16[1024,512]{1,0:T(8,128)(2,1)} %get-tuple-element.131.k_ref, bf16[1024,512]{1,0:T(8,128)(2,1)} %slice.257.v_ref, bf16[1024,512]{1,0:T(8,128)(2,1)} %collective-permute-done.19.kr_ref, ...), custom_call_target="tpu_custom_call" | custom-call | flops 3221225472 | bytes 6291456 | tf_op jit(solution)/shard_map/attend/pallas_call | solution.py:321
  241.2 12.8 %collective-permute-done.29 = bf16[256,2048]{1,0:T(8,128)(2,1)S(1)} collective-permute-done((bf16[256,2048]{1,0:T(8,128)(2,1)S(1)}, bf16[256,2048]{1,0:T(8,128)(2,1)S(1)}, u32[]{:S(2)}, u32[]{:S(2)}) %collective-permute-start.29) | collective-permute-done | bytes 1048608 | tf_op jit(solution)/shard_map/ppermute | solution.py:121
  279.8 11.9 %collective-permute-start.33 = (bf16[256,2048]{1,0:T(8,128)(2,1)}, bf16[256,2048]{1,0:T(8,128)(2,1)}, u32[]{:S(2)}, u32[]{:S(2)}) collective-permute-start(bf16[256,2048]{1,0:T(8,128)(2,1)} %add_convert_fusion.9), channel_id=1, source_target_pairs={{0,1},{1,2},{2,3},{4,5},{5,6},{6,7},{8,9},{9,10},{10,11},{12,13},{... | collective-permute-start | bytes 3145736 | tf_op jit(solution)/shard_map/ppermute | solution.py:121
  403.8 35.4 %hidden.2 = (bf16[2048,2048]{1,0:T(8,128)(2,1)}, bf16[2048,2176]{1,0:T(8,128)(2,1)}, bf16[2048,2048]{1,0:T(8,128)(2,1)}, f32[1024,8]{1,0:T(8,128)}) custom-call(bf16[1024,2048]{1,0:T(8,128)(2,1)} %assemble.6.x_ref, bf16[1024,2048]{1,0:T(8,128)(2,1)} %assemble.5.c_ref, bf16[2048,4096]{1,0:T(8,128)(2,1)} %all-gather.6.cloned.1.call-done.g_ref.u_ref.refs_2_.refs_3_.refs_1_, ...), custom_call_target="tpu_custom_call" | custom-call | flops 25769803776 | bytes 58720256 | tf_op jit(solution)/shard_map/hidden/pallas_call | solution.py:432
  439.3 35.5 %hidden.3 = (bf16[2048,2048]{1,0:T(8,128)(2,1)}, bf16[2048,2176]{1,0:T(8,128)(2,1)}, bf16[2048,2048]{1,0:T(8,128)(2,1)}, f32[1024,8]{1,0:T(8,128)}) custom-call(bf16[1024,2048]{1,0:T(8,128)(2,1)} %collective-permute-done.49.refs_0_, bf16[1024,2048]{1,0:T(8,128)(2,1)} %collective-permute-done.40.refs_1_, ...), custom_call_target="tpu_custom_call", output_to_operand_aliasing={{0}: (6, {}), {1}: (7, {}), {2}: (8, {})} | custom-call | flops 25769803776 | bytes 58720256 | tf_op jit(solution)/shard_map/hidden/pallas_call | solution.py:432
  474.8 22.6 %convolution_convert_fusion.3 = bf16[2048,2048]{1,0:T(8,128)(2,1)} fusion(bf16[2048,2048]{1,0:T(8,128)(2,1)} %get-tuple-element.172.refs_0_, bf16[1024,2048]{1,0:T(8,128)(2,1)} %collective-permute-done.40.refs_1_, bf16[1024,2048]{1,0:T(8,128)(2,1)S(1)} %copy-done.13), kind=kOutput, calls=%fused_computation.6 | convolution fusion | flops 17200840704 | bytes 25165824 | tf_op jit(solution)/shard_map/dot_general | solution.py:24
  502.1 25.7 %mix.4 = bf16[1024,2048]{1,0:T(8,128)(2,1)} custom-call(bf16[2048,2176]{1,0:T(8,128)(2,1)} %maximum_dynamic-update-slice_fusion.refs_0_, bf16[2048,4096]{1,0:T(8,128)(2,1)} %all-gather.6.cloned.1.call-done.g_ref.u_ref.refs_2_.refs_3_.refs_1_, bf16[2048,2048]{1,0:T(8,128)(2,1)} %get-tuple-element.176.refs_2_, ...), custom_call_target="tpu_custom_call" | custom-call | flops 17716740096 | bytes 34340864 | tf_op jit(solution)/shard_map/mix/pallas_call | solution.py:467
  528.0 26.1 %mix.5 = bf16[1024,2048]{1,0:T(8,128)(2,1)} custom-call(bf16[2048,2176]{1,0:T(8,128)(2,1)} %maximum_dynamic-update-slice_fusion.refs_0_, bf16[2048,4096]{1,0:T(8,128)(2,1)} %all-gather.6.cloned.1.call-done.g_ref.u_ref.refs_2_.refs_3_.refs_1_, bf16[2048,2048]{1,0:T(8,128)(2,1)} %get-tuple-element.176.refs_2_, ...), custom_call_target="tpu_custom_call" | custom-call | flops 17716740096 | bytes 34340864 | tf_op jit(solution)/shard_map/mix/pallas_call | solution.py:467
  554.1 26.0 %convolution_convert_fusion = bf16[2048,2176]{1,0:T(8,128)(2,1)} fusion(bf16[2048,2176]{1,0:T(8,128)(2,1)} %maximum_dynamic-update-slice_fusion.refs_0_, bf16[1024,2048]{1,0:T(8,128)(2,1)} %collective-permute-done.49.refs_0_, bf16[1024,2048]{1,0:T(8,128)(2,1)S(1)} %copy-done.14), kind=kOutput, calls=%fused_computation | convolution fusion | flops 18274844672 | bytes 26214400 | tf_op jit(solution)/shard_map/dot_general | solution.py:24
  585.7 22.4 %collective-permute-done.54 = bf16[256,2048]{1,0:T(8,128)(2,1)S(1)} collective-permute-done((bf16[256,2048]{1,0:T(8,128)(2,1)S(1)}, bf16[256,2048]{1,0:T(8,128)(2,1)S(1)}, u32[]{:S(2)}, u32[]{:S(2)}) %collective-permute-start.54) | collective-permute-done | bytes 1048608 | tf_op jit(solution)/shard_map/ppermute | solution.py:121
  611.4 24.1 %convolution_convert_fusion.2 = bf16[2048,2048]{1,0:T(8,128)(2,1)} fusion(bf16[2048,2048]{1,0:T(8,128)(2,1)} %get-tuple-element.176.refs_2_, bf16[1024,2048]{1,0:T(8,128)(2,1)} %collective-permute-done.49.refs_0_, bf16[1024,2048]{1,0:T(8,128)(2,1)} %assemble.6.x_ref), kind=kOutput, calls=%fused_computation.5 | convolution fusion | flops 17200840704 | bytes 25165824 | tf_op jit(solution)/shard_map/dot_general | solution.py:24
  643.2 13.3 %mix.7 = bf16[1024,2048]{1,0:T(8,128)(2,1)} custom-call(bf16[2048,2048]{1,0:T(8,128)(2,1)} %get-tuple-element.172.refs_0_, bf16[2048,2048]{1,0:T(8,128)(2,1)} %all-gather.8.cloned.1.call-done.d_ref.refs_4_.refs_1_), custom_call_target="tpu_custom_call" | custom-call | flops 8589934592 | bytes 20971520 | tf_op jit(solution)/shard_map/mix/pallas_call | solution.py:467
  674.8 20.3 %collective-permute-done.58 = bf16[256,2048]{1,0:T(8,128)(2,1)S(1)} collective-permute-done((bf16[256,2048]{1,0:T(8,128)(2,1)S(1)}, bf16[256,2048]{1,0:T(8,128)(2,1)S(1)}, u32[]{:S(2)}, u32[]{:S(2)}) %collective-permute-start.58) | collective-permute-done | bytes 1048608 | tf_op jit(solution)/shard_map/ppermute | solution.py:121
  738.5 13.9 %mix.6 = bf16[1024,2048]{1,0:T(8,128)(2,1)} custom-call(bf16[2048,2048]{1,0:T(8,128)(2,1)} %get-tuple-element.172.refs_0_, bf16[2048,2048]{1,0:T(8,128)(2,1)} %all-gather.8.cloned.1.call-done.d_ref.refs_4_.refs_1_), custom_call_target="tpu_custom_call" | custom-call | flops 8589934592 | bytes 20971520 | tf_op jit(solution)/shard_map/mix/pallas_call | solution.py:467
  788.0 17.7 %attend_back.1 = (f32[1024,512]{1,0:T(8,128)}, f32[1024,512]{1,0:T(8,128)}, f32[1024,512]{1,0:T(8,128)}, bf16[1024,512]{1,0:T(8,128)(2,1)}, bf16[1024,512]{1,0:T(8,128)(2,1)}) custom-call(s32[1]{0:T(128)} %bitcast.cont_ref, bf16[1024,512]{1,0:T(8,128)(2,1)} %get-tuple-element.130.q_ref, bf16[1024,512]{1,0:T(8,128)(2,1)} %get-tuple-element.131.k_ref, ...), custom_call_target="tpu_custom_call" | custom-call | flops 8053063680 | bytes 15728640 | tf_op jit(solution)/shard_map/attend_back/pallas_call | solution.py:382
  828.9 27.3 %collective-permute-done.75.dkr_ref = bf16[1024,512]{1,0:T(8,128)(2,1)} collective-permute-done((bf16[1024,512]{1,0:T(8,128)(2,1)}, bf16[1024,512]{1,0:T(8,128)(2,1)}, u32[]{:S(2)}, u32[]{:S(2)}) %collective-permute-start.75) | collective-permute-done | bytes 1048608 | tf_op jit(solution)/shard_map/ppermute | solution.py:773
  888.2 11.2 %fusion.6 = bf16[1024,2048]{1,0:T(8,128)(2,1)} fusion(bf16[1024,1536]{1,0:T(8,128)(2,1)} %pad_maximum_fusion.5, bf16[2048,2176]{1,0:T(8,128)(2,1)} %all-gather.4.cloned.1.call-done), kind=kOutput, calls=%fused_computation.16 | convolution fusion | flops 6444548096 | bytes 13631488 | tf_op jit(solution)/shard_map/dot_general | solution.py:24
  921.2 14.5 %collective-permute-done.80 = bf16[256,2048]{1,0:T(8,128)(2,1)} collective-permute-done((bf16[256,2048]{1,0:T(8,128)(2,1)}, bf16[256,2048]{1,0:T(8,128)(2,1)}, u32[]{:S(2)}, u32[]{:S(2)}) %collective-permute-start.80) | collective-permute-done | bytes 1048608 | tf_op jit(solution)/shard_map/ppermute | solution.py:121
  958.9 13.7 %collective-permute-done.82 = bf16[256,2048]{1,0:T(8,128)(2,1)S(1)} collective-permute-done((bf16[256,2048]{1,0:T(8,128)(2,1)}, bf16[256,2048]{1,0:T(8,128)(2,1)S(1)}, u32[]{:S(2)}, u32[]{:S(2)}) %collective-permute-start.82) | collective-permute-done | bytes 1048608 | tf_op jit(solution)/shard_map/ppermute | solution.py:121
  986.8 13.1 %collective-permute-done.90 = bf16[256,2048]{1,0:T(8,128)(2,1)} collective-permute-done((bf16[256,2048]{1,0:T(8,128)(2,1)}, bf16[256,2048]{1,0:T(8,128)(2,1)}, u32[]{:S(2)}, u32[]{:S(2)}) %collective-permute-start.90) | collective-permute-done | bytes 1048608 | tf_op jit(solution)/shard_map/ppermute | solution.py:121
  (514 shorter events, 567.8 us)
Async XLA Ops:
  7.2 72.7 %all-gather.4.cloned.1.call-start = ((), (), s32[]{:S(2)}) async-start(), calls=%async_computation.6 | async-start | bytes 10027008 | tf_op jit(solution)/shard_map/all_gather | solution.py:641
  14.7 389.1 %all-gather.8.cloned.1.call-start = ((), (), s32[]{:S(2)}) async-start(), calls=%async_computation.8 | async-start | bytes 10485760 | tf_op jit(solution)/shard_map/all_gather | solution.py:670
  23.9 37.0 %collective-permute-start.51 = (bf16[256,2048]{1,0:T(8,128)(2,1)}, bf16[256,2048]{1,0:T(8,128)(2,1)}, u32[]{:S(2)}, u32[]{:S(2)}) collective-permute-start(bf16[256,2048]{1,0:T(8,128)(2,1)} %slice_bitcast_fusion), channel_id=1, source_target_pairs={{0,4},{4,0},{8,12},{12,8},{16,20},{20,16},{24,28},{28,24},{1,5},{5... | collective-permute-start | bytes 3145736 | tf_op jit(solution)/shard_map/ppermute | solution.py:39
  79.9 323.9 %all-gather.6.cloned.1.call-start = ((), (), s32[]{:S(2)}) async-start(), calls=%async_computation.7 | async-start | bytes 20971520 | tf_op jit(solution)/shard_map/all_gather | solution.py:670
  89.7 86.5 %collective-permute-start.50 = (bf16[256,4096]{1,0:T(8,128)(2,1)}, bf16[256,4096]{1,0:T(8,128)(2,1)}, u32[]{:S(2)}, u32[]{:S(2)}) collective-permute-start(bf16[256,4096]{1,0:T(8,128)(2,1)} %pad_maximum_fusion.7), channel_id=1, source_target_pairs={{0,4},{4,0},{8,12},{12,8},{16,20},{20,16},{24,28},{28,24},{1,5},{5... | collective-permute-start | bytes 6291464 | tf_op jit(solution)/shard_map/ppermute | solution.py:39
  140.2 32.4 %collective-permute-start.15 = (bf16[128,2048]{1,0:T(8,128)(2,1)S(1)}, bf16[128,2048]{1,0:T(8,128)(2,1)}, u32[]{:S(2)}, u32[]{:S(2)}) collective-permute-start(bf16[128,2048]{1,0:T(8,128)(2,1)S(1)} %copy-done.25), channel_id=1, source_target_pairs={{0,1},{1,2},{2,3},{4,5},{5,6},{6,7},{8,9},{9,10},{10,11},{12,13},{... | collective-permute-start | bytes 1572872 | tf_op jit(solution)/shard_map/ppermute | solution.py:62
  145.6 29.3 %collective-permute-start.17 = (bf16[128,2048]{1,0:T(8,128)(2,1)S(1)}, bf16[128,2048]{1,0:T(8,128)(2,1)}, u32[]{:S(2)}, u32[]{:S(2)}) collective-permute-start(bf16[128,2048]{1,0:T(8,128)(2,1)S(1)} %copy-done.25), channel_id=1, source_target_pairs={{1,0},{2,1},{3,2},{5,4},{6,5},{7,6},{9,8},{10,9},{11,10},{13,12},{... | collective-permute-start | bytes 1572872 | tf_op jit(solution)/shard_map/ppermute | solution.py:63
  160.0 44.7 %collective-permute-start.20 = (bf16[1024,512]{1,0:T(8,128)(2,1)}, bf16[1024,512]{1,0:T(8,128)(2,1)}, u32[]{:S(2)}, u32[]{:S(2)}) collective-permute-start(bf16[1024,512]{1,0:T(8,128)(2,1)} %slice.257.v_ref), channel_id=1, source_target_pairs={{0,16},{4,20},{8,24},{12,28},{1,17},{5,21},{9,25},{13,29},{2,18},{... | collective-permute-start | bytes 3145736 | tf_op jit(solution)/shard_map/ppermute | solution.py:680
  172.6 36.9 %collective-permute-start.19 = (bf16[1024,512]{1,0:T(8,128)(2,1)}, bf16[1024,512]{1,0:T(8,128)(2,1)}, u32[]{:S(2)}, u32[]{:S(2)}) collective-permute-start(bf16[1024,512]{1,0:T(8,128)(2,1)} %get-tuple-element.131.k_ref), channel_id=1, source_target_pairs={{0,16},{4,20},{8,24},{12,28},{1,17},{5,21},{9,25},{13,29},{2,18},{... | collective-permute-start | bytes 3145736 | tf_op jit(solution)/shard_map/ppermute | solution.py:690
  218.0 393.4 %reduce-scatter.7.cloned.1.call-start = ((), (), s32[]{:S(2)}) async-start(), calls=%async_computation.9 | async-start | bytes 10485760 | tf_op jit(solution)/shard_map/reduce_scatter | solution.py:735
  268.5 81.6 %collective-permute-start.40 = (bf16[1024,2048]{1,0:T(8,128)(2,1)}, bf16[1024,2048]{1,0:T(8,128)(2,1)}, u32[]{:S(2)}, u32[]{:S(2)}) collective-permute-start(bf16[1024,2048]{1,0:T(8,128)(2,1)} %assemble.5.c_ref), channel_id=1, source_target_pairs={{0,4},{4,0},{8,12},{12,8},{16,20},{20,16},{24,28},{28,24},{1,5},{5... | collective-permute-start | bytes 12582920 | tf_op jit(solution)/shard_map/ppermute | solution.py:39
  279.8 28.7 %collective-permute-start.33 = (bf16[256,2048]{1,0:T(8,128)(2,1)}, bf16[256,2048]{1,0:T(8,128)(2,1)}, u32[]{:S(2)}, u32[]{:S(2)}) collective-permute-start(bf16[256,2048]{1,0:T(8,128)(2,1)} %add_convert_fusion.9), channel_id=1, source_target_pairs={{0,1},{1,2},{2,3},{4,5},{5,6},{6,7},{8,9},{9,10},{10,11},{12,13},{... | collective-permute-start | bytes 3145736 | tf_op jit(solution)/shard_map/ppermute | solution.py:121
  497.4 227.1 %reduce-scatter.11.cloned.1.call-start = ((), (), s32[]{:S(2)}) async-start(), calls=%async_computation.11 | async-start | bytes 11141120 | tf_op jit(solution)/shard_map/reduce_scatter | solution.py:735
  580.2 201.6 %reduce-scatter.9.cloned.1.call-start = ((), (), s32[]{:S(2)}) async-start(), calls=%async_computation.10 | async-start | bytes 10485760 | tf_op jit(solution)/shard_map/reduce_scatter | solution.py:735
  635.6 252.6 %reduce-scatter.13.cloned.1.call-start = ((), (), s32[]{:S(2)}) async-start(), calls=%async_computation.12 | async-start | bytes 5242880 | tf_op jit(solution)/shard_map/reduce_scatter | solution.py:765
  635.6 27.8 %collective-permute-start.56 = (bf16[256,2048]{1,0:T(8,128)(2,1)}, bf16[256,2048]{1,0:T(8,128)(2,1)}, u32[]{:S(2)}, u32[]{:S(2)}) collective-permute-start(bf16[256,2048]{1,0:T(8,128)(2,1)} %get-tuple-element.174), channel_id=1, source_target_pairs={{0,1},{1,2},{4,5},{5,6},{8,9},{9,10},{12,13},{13,14},{16,17},{17,1... | collective-permute-start | bytes 3145736 | tf_op jit(solution)/shard_map/ppermute | solution.py:121
  656.5 104.5 %collective-permute-start.53 = (bf16[1024,2048]{1,0:T(8,128)(2,1)}, bf16[1024,2048]{1,0:T(8,128)(2,1)}, u32[]{:S(2)}, u32[]{:S(2)}) collective-permute-start(bf16[1024,2048]{1,0:T(8,128)(2,1)} %mix.7), channel_id=1, source_target_pairs={{0,4},{4,0},{8,12},{12,8},{16,20},{20,16},{24,28},{28,24},{1,5},{5... | collective-permute-start | bytes 12582920 | tf_op jit(solution)/shard_map/ppermute | solution.py:39
  667.1 28.0 %collective-permute-start.58 = (bf16[256,2048]{1,0:T(8,128)(2,1)S(1)}, bf16[256,2048]{1,0:T(8,128)(2,1)S(1)}, u32[]{:S(2)}, u32[]{:S(2)}) collective-permute-start(bf16[256,2048]{1,0:T(8,128)(2,1)S(1)} %get-tuple-element.177), channel_id=1, source_target_pairs={{0,1},{1,2},{2,3},{4,5},{5,6},{6,7},{8,9},{9,10},{10,11},{12,13},{... | collective-permute-start | bytes 3145736 | tf_op jit(solution)/shard_map/ppermute | solution.py:121
  724.5 27.9 %collective-permute-start.68 = (bf16[128,2048]{1,0:T(8,128)(2,1)}, bf16[128,2048]{1,0:T(8,128)(2,1)}, u32[]{:S(2)}, u32[]{:S(2)}) collective-permute-start(bf16[128,2048]{1,0:T(8,128)(2,1)} %copy-done.48), channel_id=1, source_target_pairs={{1,2},{2,3},{5,6},{6,7},{9,10},{10,11},{13,14},{14,15},{17,18},{18... | collective-permute-start | bytes 1572872 | tf_op jit(solution)/shard_map/ppermute | solution.py:62
  725.9 26.4 %collective-permute-start.69 = (bf16[128,2048]{1,0:T(8,128)(2,1)}, bf16[128,2048]{1,0:T(8,128)(2,1)}, u32[]{:S(2)}, u32[]{:S(2)}) collective-permute-start(bf16[128,2048]{1,0:T(8,128)(2,1)} %collective-permute-done.67.refs_9_), channel_id=1, source_target_pairs={{1,0},{2,1},{5,4},{6,5},{9,8},{10,9},{13,12},{14,13},{17,16},{18,1... | collective-permute-start | bytes 1572872 | tf_op jit(solution)/shard_map/ppermute | solution.py:63
  781.8 198.7 %reduce-scatter.15.cloned.1.call-start = ((), (), s32[]{:S(2)}) async-start(), calls=%async_computation.13 | async-start | bytes 2359296 | tf_op jit(solution)/shard_map/reduce_scatter | solution.py:804
  811.7 44.4 %collective-permute-start.75 = (bf16[1024,512]{1,0:T(8,128)(2,1)}, bf16[1024,512]{1,0:T(8,128)(2,1)}, u32[]{:S(2)}, u32[]{:S(2)}) collective-permute-start(bf16[1024,512]{1,0:T(8,128)(2,1)} %get-tuple-element.192), channel_id=1, source_target_pairs={{16,0},{20,4},{24,8},{28,12},{17,1},{21,5},{25,9},{29,13},{18,2},{... | collective-permute-start | bytes 3145736 | tf_op jit(solution)/shard_map/ppermute | solution.py:773
  813.1 64.7 %collective-permute-start.79 = (bf16[1024,512]{1,0:T(8,128)(2,1)}, bf16[1024,512]{1,0:T(8,128)(2,1)}, u32[]{:S(2)}, u32[]{:S(2)}) collective-permute-start(bf16[1024,512]{1,0:T(8,128)(2,1)} %get-tuple-element.204), channel_id=1, source_target_pairs={{16,0},{20,4},{24,8},{28,12},{17,1},{21,5},{25,9},{29,13},{18,2},{... | collective-permute-start | bytes 3145736 | tf_op jit(solution)/shard_map/ppermute | solution.py:773
  818.4 188.9 %reduce-scatter.17.cloned.1.call-start = ((), (), s32[]{:S(2)}) async-start(), calls=%async_computation.14 | async-start | bytes 7077888 | tf_op jit(solution)/shard_map/reduce_scatter | solution.py:804
  (158 other events, 2471.2 us)
Sparse Core Ops, SparseCore 0:
  14.8 59.2 all-gather.3
  80.0 90.3 all-gather.7
  217.4 154.6 all-gather.5
  497.5 90.1 reduce-scatter.6
  591.1 90.7 reduce-scatter.10
  685.0 86.3 reduce-scatter.8
  781.9 80.0 reduce-scatter.12
  865.6 41.7 reduce-scatter.14
  910.7 61.8 reduce-scatter.16

commit v4 on v3

--- a/solution.py
+++ b/solution.py
@@ -755,7 +755,7 @@
         grad_scaled - hat_two * jnp.mean(grad_scaled * hat_two, axis=-1, keepdims=True)
     )
     grad_after_low = after(grad_after.astype(BF), up_term)
-    grad_attn, _ = line_gather(grad_after_low, gates={2: [gate_sum]})
+    grad_attn, _ = line_gather(grad_after_low)
 
     act = after(act, back_own, *back_sends[1])
     out_far = mix([(act, low_mat, 0, 1)], BF, tokens)
@@ -792,12 +792,12 @@
     grad_raw = jnp.concatenate(
         [raw_back(u_query, raw[:, :cols], 0), raw_back(u_key, raw[:, cols : 2 * cols], 1), grad_value], axis=1
     )
-    normed_part = dot(after(grad_raw, out_total), qkv_mat, NT).astype(BF)
+    normed_part = dot(grad_raw, qkv_mat, NT).astype(BF)
     small = gain_parts.reshape(2, heads, fsdp, narrow).transpose(2, 0, 1, 3).reshape(fsdp, -1)
     small = total_fsdp(small)
     grad_raw_later = after(grad_raw, normed_part)
     qkv_term = dot(normed, grad_raw_later, TN).astype(BF)
-    grad_hat, _, last_sends = line_scatter(shares(normed_part), {3: [router_hat, gain_term, small]})
+    grad_hat, _, last_sends = line_scatter(shares(normed_part), {1: [out_total], 3: [router_hat, gain_term, small]})
 
 
     def summed(value):

time: 1040 us -> 1020 us (0.981)
  waiting for transfers between devices: 340 us -> 323 us
    ppermute x9, waiting for transfers between devices: 117 us -> 59.7 us  [line_scatter(): up = lax.ppermute(send_up, 'tp', [(i, i + 1) for i in range(count - s)])]
    reduce_scatter x2, waiting for transfers between devices: 0.04 us -> 24.8 us  [summed(): lax.psum_scatter(value, 'fsdp', scatter_dimension=0, tiled=True).astype(F32)]
    ppermute x12, waiting for transfers between devices: 2.48 us -> 21.8 us  [total_tp(): lax.ppermute(flat, 'tp', [(i, (i + s) % count) for i in range(count)])]
    reduce_scatter x3, waiting for transfers between devices: 0.02 us -> 18.9 us  [scattered(): lax.psum_scatter(value, 'fsdp', scatter_dimension=0, tiled=True, axis_ind...]
    ppermute x1, waiting for transfers between devices: 27.3 us -> 11.4 us  [on_device(): lax.ppermute(dk_far, 'fsdp', back_pairs)]
  transfers between devices with their start and end apart: 104 -> 104, of which waited for: 47 -> 48; matrix products, arithmetic and copies ran while one was open for 22% -> 20% of each run, Pallas kernels for 16% -> 16%
where the time goes in v4:
time: 1020 us; the launch traced here: 1010 us
  waiting for transfers between devices  323 us (32%)
  Pallas kernels  234 us (23%)
  starting transfers between devices  174 us (17%)
  matrix products  126 us (12%)
  other arithmetic  101 us (10%)
  local copies, waits for them, and re-layouts  40.1 us (4%)
  between operations  16.1 us (2%)
    ppermute x24, waiting for transfers between devices, line_gather(): lax.ppermute(behind, 'tp', [(i + 1, i) for i in range(count - s)])  147 us
    dot_general x13, matrix products, dot(): return lax.dot_general(a, b, dims, preferred_element_type=F32)  126 us
    pallas_call x4, Pallas kernels, mix(): pl.pallas_call(mix_kernel, grid=(cols // tile,), in_specs=specs, out_spec...  78.5 us
    pallas_call x2, Pallas kernels, hidden(): pl.pallas_call(kernel, grid=(experts,), in_specs=[full, full, mat(0), mat...  71.2 us
    ppermute x9, waiting for transfers between devices, line_scatter(): up = lax.ppermute(send_up, 'tp', [(i, i + 1) for i in range(count - s)])  59.7 us
    ppermute x24, starting transfers between devices, line_gather(): lax.ppermute(ahead, 'tp', [(i, i + 1) for i in range(s - 1, count - 1)])  51.8 us
    ppermute x9, starting transfers between devices, line_scatter(): up = lax.ppermute(send_up, 'tp', [(i, i + 1) for i in range(count - s)])  45.6 us
    ppermute x24, starting transfers between devices, line_gather(): lax.ppermute(behind, 'tp', [(i + 1, i) for i in range(count - s)])  31 us
  transfers between devices with their start and end apart: 104, of which 48 were waited for; matrix products, arithmetic and copies ran while one was open for 20% of the time, Pallas kernels for 16%

profile of v4, /device:TPU:0, one launch (start us, length us, event | category | flops | bytes accessed | tf_op | source)
XLA Modules:
  0.0 1013.8 jit_solution(17000340362744215409)
XLA Ops:
  69.4 10.5 %collective-permute-done.3.refs_1_ = bf16[128,2048]{1,0:T(8,128)(2,1)} collective-permute-done((bf16[128,2048]{1,0:T(8,128)(2,1)}, bf16[128,2048]{1,0:T(8,128)(2,1)}, u32[]{:S(2)}, u32[]{:S(2)}) %collective-permute-start.3) | collective-permute-done | bytes 524320 | tf_op jit(solution)/shard_map/ppermute | solution.py:63
  99.8 9.6 collective-permute-done.4.refs_0_
  113.8 10.0 fusion.2.q_ref.k_ref
  181.6 10.9 %collective-permute-done.25.refs_8_ = bf16[128,2048]{1,0:T(8,128)(2,1)S(1)} collective-permute-done((bf16[128,2048]{1,0:T(8,128)(2,1)S(1)}, bf16[128,2048]{1,0:T(8,128)(2,1)S(1)}, u32[]{:S(2)}, u32[]{:S(2)}) %collective-permute-start.25) | collective-permute-done | bytes 524320 | tf_op jit(solution)/shard_map/ppermute | solution.py:63
  194.5 9.3 collective-permute-done.22.refs_1_
  218.5 11.8 %attend.1 = bf16[1024,512]{1,0:T(8,128)(2,1)} custom-call(s32[1]{0:T(128)} %bitcast.cont_ref, bf16[1024,512]{1,0:T(8,128)(2,1)} %get-tuple-element.129.q_ref, bf16[1024,512]{1,0:T(8,128)(2,1)} %get-tuple-element.130.k_ref, bf16[1024,512]{1,0:T(8,128)(2,1)} %slice.257.v_ref, bf16[1024,512]{1,0:T(8,128)(2,1)} %collective-permute-done.19.kr_ref, ...), custom_call_target="tpu_custom_call" | custom-call | flops 3221225472 | bytes 6291456 | tf_op jit(solution)/shard_map/attend/pallas_call | solution.py:321
  240.7 12.0 %collective-permute-done.29 = bf16[256,2048]{1,0:T(8,128)(2,1)S(1)} collective-permute-done((bf16[256,2048]{1,0:T(8,128)(2,1)S(1)}, bf16[256,2048]{1,0:T(8,128)(2,1)S(1)}, u32[]{:S(2)}, u32[]{:S(2)}) %collective-permute-start.29) | collective-permute-done | bytes 1048608 | tf_op jit(solution)/shard_map/ppermute | solution.py:121
  277.9 11.8 %collective-permute-start.33 = (bf16[256,2048]{1,0:T(8,128)(2,1)}, bf16[256,2048]{1,0:T(8,128)(2,1)}, u32[]{:S(2)}, u32[]{:S(2)}) collective-permute-start(bf16[256,2048]{1,0:T(8,128)(2,1)} %add_convert_fusion.9), channel_id=1, source_target_pairs={{0,1},{1,2},{2,3},{4,5},{5,6},{6,7},{8,9},{9,10},{10,11},{12,13},{... | collective-permute-start | bytes 3145736 | tf_op jit(solution)/shard_map/ppermute | solution.py:121
  399.7 35.6 %hidden.2 = (bf16[2048,2048]{1,0:T(8,128)(2,1)}, bf16[2048,2176]{1,0:T(8,128)(2,1)}, bf16[2048,2048]{1,0:T(8,128)(2,1)}, f32[1024,8]{1,0:T(8,128)}) custom-call(bf16[1024,2048]{1,0:T(8,128)(2,1)} %assemble.6.x_ref, bf16[1024,2048]{1,0:T(8,128)(2,1)} %assemble.5.c_ref, bf16[2048,4096]{1,0:T(8,128)(2,1)} %all-gather.6.cloned.1.call-done.g_ref.u_ref.refs_2_.refs_3_.refs_1_, ...), custom_call_target="tpu_custom_call" | custom-call | flops 25769803776 | bytes 58720256 | tf_op jit(solution)/shard_map/hidden/pallas_call | solution.py:432
  435.3 35.5 %hidden.3 = (bf16[2048,2048]{1,0:T(8,128)(2,1)}, bf16[2048,2176]{1,0:T(8,128)(2,1)}, bf16[2048,2048]{1,0:T(8,128)(2,1)}, f32[1024,8]{1,0:T(8,128)}) custom-call(bf16[1024,2048]{1,0:T(8,128)(2,1)} %collective-permute-done.49.refs_0_, bf16[1024,2048]{1,0:T(8,128)(2,1)} %collective-permute-done.40.refs_1_, ...), custom_call_target="tpu_custom_call", output_to_operand_aliasing={{0}: (6, {}), {1}: (7, {}), {2}: (8, {})} | custom-call | flops 25769803776 | bytes 58720256 | tf_op jit(solution)/shard_map/hidden/pallas_call | solution.py:432
  470.9 22.6 %convolution_convert_fusion.3 = bf16[2048,2048]{1,0:T(8,128)(2,1)} fusion(bf16[2048,2048]{1,0:T(8,128)(2,1)} %get-tuple-element.171.refs_0_, bf16[1024,2048]{1,0:T(8,128)(2,1)} %collective-permute-done.40.refs_1_, bf16[1024,2048]{1,0:T(8,128)(2,1)S(1)} %copy-done.15), kind=kOutput, calls=%fused_computation.6 | convolution fusion | flops 17200840704 | bytes 25165824 | tf_op jit(solution)/shard_map/dot_general | solution.py:24
  498.1 25.8 %mix.4 = bf16[1024,2048]{1,0:T(8,128)(2,1)} custom-call(bf16[2048,2176]{1,0:T(8,128)(2,1)} %maximum_dynamic-update-slice_fusion.refs_0_, bf16[2048,4096]{1,0:T(8,128)(2,1)} %all-gather.6.cloned.1.call-done.g_ref.u_ref.refs_2_.refs_3_.refs_1_, bf16[2048,2048]{1,0:T(8,128)(2,1)} %get-tuple-element.175.refs_2_, ...), custom_call_target="tpu_custom_call" | custom-call | flops 17716740096 | bytes 34340864 | tf_op jit(solution)/shard_map/mix/pallas_call | solution.py:467
  524.1 26.1 %mix.5 = bf16[1024,2048]{1,0:T(8,128)(2,1)} custom-call(bf16[2048,2176]{1,0:T(8,128)(2,1)} %maximum_dynamic-update-slice_fusion.refs_0_, bf16[2048,4096]{1,0:T(8,128)(2,1)} %all-gather.6.cloned.1.call-done.g_ref.u_ref.refs_2_.refs_3_.refs_1_, bf16[2048,2048]{1,0:T(8,128)(2,1)} %get-tuple-element.175.refs_2_, ...), custom_call_target="tpu_custom_call" | custom-call | flops 17716740096 | bytes 34340864 | tf_op jit(solution)/shard_map/mix/pallas_call | solution.py:467
  557.4 25.7 %convolution_convert_fusion = bf16[2048,2176]{1,0:T(8,128)(2,1)} fusion(bf16[2048,2176]{1,0:T(8,128)(2,1)} %maximum_dynamic-update-slice_fusion.refs_0_, bf16[1024,2048]{1,0:T(8,128)(2,1)} %collective-permute-done.49.refs_0_, bf16[1024,2048]{1,0:T(8,128)(2,1)S(1)} %copy-done.16), kind=kOutput, calls=%fused_computation | convolution fusion | flops 18274844672 | bytes 26214400 | tf_op jit(solution)/shard_map/dot_general | solution.py:24
  587.1 23.7 %convolution_convert_fusion.2 = bf16[2048,2048]{1,0:T(8,128)(2,1)} fusion(bf16[2048,2048]{1,0:T(8,128)(2,1)} %get-tuple-element.175.refs_2_, bf16[1024,2048]{1,0:T(8,128)(2,1)} %collective-permute-done.49.refs_0_, bf16[1024,2048]{1,0:T(8,128)(2,1)} %assemble.6.x_ref), kind=kOutput, calls=%fused_computation.5 | convolution fusion | flops 17200840704 | bytes 25165824 | tf_op jit(solution)/shard_map/dot_general | solution.py:24
  617.7 13.3 %mix.7 = bf16[1024,2048]{1,0:T(8,128)(2,1)} custom-call(bf16[2048,2048]{1,0:T(8,128)(2,1)} %get-tuple-element.171.refs_0_, bf16[2048,2048]{1,0:T(8,128)(2,1)} %all-gather.8.cloned.1.call-done.d_ref.refs_4_.refs_1_), custom_call_target="tpu_custom_call" | custom-call | flops 8589934592 | bytes 20971520 | tf_op jit(solution)/shard_map/mix/pallas_call | solution.py:467
  650.3 19.8 %collective-permute-done.58 = bf16[256,2048]{1,0:T(8,128)(2,1)S(1)} collective-permute-done((bf16[256,2048]{1,0:T(8,128)(2,1)S(1)}, bf16[256,2048]{1,0:T(8,128)(2,1)S(1)}, u32[]{:S(2)}, u32[]{:S(2)}) %collective-permute-start.58) | collective-permute-done | bytes 1048608 | tf_op jit(solution)/shard_map/ppermute | solution.py:121
  710.9 13.3 %mix.6 = bf16[1024,2048]{1,0:T(8,128)(2,1)} custom-call(bf16[2048,2048]{1,0:T(8,128)(2,1)} %get-tuple-element.171.refs_0_, bf16[2048,2048]{1,0:T(8,128)(2,1)} %all-gather.8.cloned.1.call-done.d_ref.refs_4_.refs_1_), custom_call_target="tpu_custom_call" | custom-call | flops 8589934592 | bytes 20971520 | tf_op jit(solution)/shard_map/mix/pallas_call | solution.py:467
  760.7 17.7 %attend_back.1 = (f32[1024,512]{1,0:T(8,128)}, f32[1024,512]{1,0:T(8,128)}, f32[1024,512]{1,0:T(8,128)}, bf16[1024,512]{1,0:T(8,128)(2,1)}, bf16[1024,512]{1,0:T(8,128)(2,1)}) custom-call(s32[1]{0:T(128)} %bitcast.cont_ref, bf16[1024,512]{1,0:T(8,128)(2,1)} %get-tuple-element.129.q_ref, bf16[1024,512]{1,0:T(8,128)(2,1)} %get-tuple-element.130.k_ref, ...), custom_call_target="tpu_custom_call" | custom-call | flops 8053063680 | bytes 15728640 | tf_op jit(solution)/shard_map/attend_back/pallas_call | solution.py:382
  780.0 18.3 %reduce-scatter.13.cloned.1.call-done = bf16[512,2176]{1,0:T(8,128)(2,1)} async-done(((bf16[2048,2176]{1,0:T(8,128)(2,1)}), bf16[512,2176]{1,0:T(8,128)(2,1)}) %reduce-scatter.13.cloned.1.call-update) | async-done | bytes 2228240 | tf_op jit(solution)/shard_map/reduce_scatter | solution.py:735
  820.7 11.4 %collective-permute-done.75.dkr_ref = bf16[1024,512]{1,0:T(8,128)(2,1)} collective-permute-done((bf16[1024,512]{1,0:T(8,128)(2,1)}, bf16[1024,512]{1,0:T(8,128)(2,1)}, u32[]{:S(2)}, u32[]{:S(2)}) %collective-permute-start.75) | collective-permute-done | bytes 1048608 | tf_op jit(solution)/shard_map/ppermute | solution.py:773
  863.2 11.2 %fusion.6 = bf16[1024,2048]{1,0:T(8,128)(2,1)} fusion(bf16[2048,2176]{1,0:T(8,128)(2,1)} %all-gather.4.cloned.1.call-done, bf16[1024,512]{1,0:T(8,128)(2,1)S(1)} %copy-done.19, bf16[1024,512]{1,0:T(8,128)(2,1)S(1)} %get-tuple-element.322, bf16[1024,512]{1,0:T(8,128)(2,1)S(1)} %get-tuple-element.321), kind=kOutput, calls=%fused_computation.16 | convolution fusion | flops 6453985280 | bytes 13631488 | tf_op jit(solution)/shard_map/dot_general | solution.py:24
  896.1 18.7 %collective-permute-done.84 = f32[32,128]{1,0:T(8,128)S(1)} collective-permute-done((f32[32,128]{1,0:T(8,128)S(1)}, f32[32,128]{1,0:T(8,128)S(1)}, u32[]{:S(2)}, u32[]{:S(2)}) %collective-permute-start.84) | collective-permute-done | bytes 16416 | tf_op jit(solution)/shard_map/ppermute | solution.py:140
  963.6 24.8 %reduce-scatter.17.cloned.1.call-done = bf16[256,1536]{1,0:T(8,128)(2,1)} async-done(((bf16[2048,1536]{1,0:T(8,128)(2,1)}), bf16[256,1536]{1,0:T(8,128)(2,1)}) %reduce-scatter.17.cloned.1.call-update) | async-done | bytes 786448 | tf_op jit(solution)/shard_map/reduce_scatter | solution.py:804
  (520 shorter events, 568.2 us)
Async XLA Ops:
  7.2 72.7 %all-gather.4.cloned.1.call-start = ((), (), s32[]{:S(2)}) async-start(), calls=%async_computation.6 | async-start | bytes 10027008 | tf_op jit(solution)/shard_map/all_gather | solution.py:641
  14.7 385.0 %all-gather.8.cloned.1.call-start = ((), (), s32[]{:S(2)}) async-start(), calls=%async_computation.8 | async-start | bytes 10485760 | tf_op jit(solution)/shard_map/all_gather | solution.py:670
  23.9 37.0 %collective-permute-start.51 = (bf16[256,2048]{1,0:T(8,128)(2,1)}, bf16[256,2048]{1,0:T(8,128)(2,1)}, u32[]{:S(2)}, u32[]{:S(2)}) collective-permute-start(bf16[256,2048]{1,0:T(8,128)(2,1)} %slice_bitcast_fusion), channel_id=1, source_target_pairs={{0,4},{4,0},{8,12},{12,8},{16,20},{20,16},{24,28},{28,24},{1,5},{5... | collective-permute-start | bytes 3145736 | tf_op jit(solution)/shard_map/ppermute | solution.py:39
  80.0 319.7 %all-gather.6.cloned.1.call-start = ((), (), s32[]{:S(2)}) async-start(), calls=%async_computation.7 | async-start | bytes 20971520 | tf_op jit(solution)/shard_map/all_gather | solution.py:670
  89.8 86.4 %collective-permute-start.50 = (bf16[256,4096]{1,0:T(8,128)(2,1)}, bf16[256,4096]{1,0:T(8,128)(2,1)}, u32[]{:S(2)}, u32[]{:S(2)}) collective-permute-start(bf16[256,4096]{1,0:T(8,128)(2,1)} %pad_maximum_fusion.7), channel_id=1, source_target_pairs={{0,4},{4,0},{8,12},{12,8},{16,20},{20,16},{24,28},{28,24},{1,5},{5... | collective-permute-start | bytes 6291464 | tf_op jit(solution)/shard_map/ppermute | solution.py:39
  140.3 32.4 %collective-permute-start.15 = (bf16[128,2048]{1,0:T(8,128)(2,1)S(1)}, bf16[128,2048]{1,0:T(8,128)(2,1)}, u32[]{:S(2)}, u32[]{:S(2)}) collective-permute-start(bf16[128,2048]{1,0:T(8,128)(2,1)S(1)} %copy-done.25), channel_id=1, source_target_pairs={{0,1},{1,2},{2,3},{4,5},{5,6},{6,7},{8,9},{9,10},{10,11},{12,13},{... | collective-permute-start | bytes 1572872 | tf_op jit(solution)/shard_map/ppermute | solution.py:62
  145.6 29.3 %collective-permute-start.17 = (bf16[128,2048]{1,0:T(8,128)(2,1)S(1)}, bf16[128,2048]{1,0:T(8,128)(2,1)}, u32[]{:S(2)}, u32[]{:S(2)}) collective-permute-start(bf16[128,2048]{1,0:T(8,128)(2,1)S(1)} %copy-done.25), channel_id=1, source_target_pairs={{1,0},{2,1},{3,2},{5,4},{6,5},{7,6},{9,8},{10,9},{11,10},{13,12},{... | collective-permute-start | bytes 1572872 | tf_op jit(solution)/shard_map/ppermute | solution.py:63
  160.0 44.7 %collective-permute-start.20 = (bf16[1024,512]{1,0:T(8,128)(2,1)}, bf16[1024,512]{1,0:T(8,128)(2,1)}, u32[]{:S(2)}, u32[]{:S(2)}) collective-permute-start(bf16[1024,512]{1,0:T(8,128)(2,1)} %slice.257.v_ref), channel_id=1, source_target_pairs={{0,16},{4,20},{8,24},{12,28},{1,17},{5,21},{9,25},{13,29},{2,18},{... | collective-permute-start | bytes 3145736 | tf_op jit(solution)/shard_map/ppermute | solution.py:680
  172.7 36.8 %collective-permute-start.19 = (bf16[1024,512]{1,0:T(8,128)(2,1)}, bf16[1024,512]{1,0:T(8,128)(2,1)}, u32[]{:S(2)}, u32[]{:S(2)}) collective-permute-start(bf16[1024,512]{1,0:T(8,128)(2,1)} %get-tuple-element.130.k_ref), channel_id=1, source_target_pairs={{0,16},{4,20},{8,24},{12,28},{1,17},{5,21},{9,25},{13,29},{2,18},{... | collective-permute-start | bytes 3145736 | tf_op jit(solution)/shard_map/ppermute | solution.py:690
  217.4 369.7 %reduce-scatter.7.cloned.1.call-start = ((), (), s32[]{:S(2)}) async-start(), calls=%async_computation.9 | async-start | bytes 10485760 | tf_op jit(solution)/shard_map/reduce_scatter | solution.py:735
  267.3 79.8 %collective-permute-start.40 = (bf16[1024,2048]{1,0:T(8,128)(2,1)}, bf16[1024,2048]{1,0:T(8,128)(2,1)}, u32[]{:S(2)}, u32[]{:S(2)}) collective-permute-start(bf16[1024,2048]{1,0:T(8,128)(2,1)} %assemble.5.c_ref), channel_id=1, source_target_pairs={{0,4},{4,0},{8,12},{12,8},{16,20},{20,16},{24,28},{28,24},{1,5},{5... | collective-permute-start | bytes 12582920 | tf_op jit(solution)/shard_map/ppermute | solution.py:39
  493.5 260.6 %reduce-scatter.9.cloned.1.call-start = ((), (), s32[]{:S(2)}) async-start(), calls=%async_computation.10 | async-start | bytes 10485760 | tf_op jit(solution)/shard_map/reduce_scatter | solution.py:735
  610.8 187.4 %reduce-scatter.13.cloned.1.call-start = ((), (), s32[]{:S(2)}) async-start(), calls=%async_computation.12 | async-start | bytes 11141120 | tf_op jit(solution)/shard_map/reduce_scatter | solution.py:735
  611.4 274.4 %reduce-scatter.11.cloned.1.call-start = ((), (), s32[]{:S(2)}) async-start(), calls=%async_computation.11 | async-start | bytes 5242880 | tf_op jit(solution)/shard_map/reduce_scatter | solution.py:765
  631.1 102.3 %collective-permute-start.53 = (bf16[1024,2048]{1,0:T(8,128)(2,1)}, bf16[1024,2048]{1,0:T(8,128)(2,1)}, u32[]{:S(2)}, u32[]{:S(2)}) collective-permute-start(bf16[1024,2048]{1,0:T(8,128)(2,1)} %mix.7), channel_id=1, source_target_pairs={{0,4},{4,0},{8,12},{12,8},{16,20},{20,16},{24,28},{28,24},{1,5},{5... | collective-permute-start | bytes 12582920 | tf_op jit(solution)/shard_map/ppermute | solution.py:39
  641.4 28.7 %collective-permute-start.58 = (bf16[256,2048]{1,0:T(8,128)(2,1)S(1)}, bf16[256,2048]{1,0:T(8,128)(2,1)S(1)}, u32[]{:S(2)}, u32[]{:S(2)}) collective-permute-start(bf16[256,2048]{1,0:T(8,128)(2,1)S(1)} %get-tuple-element.176), channel_id=1, source_target_pairs={{0,1},{1,2},{2,3},{4,5},{5,6},{6,7},{8,9},{9,10},{10,11},{12,13},{... | collective-permute-start | bytes 3145736 | tf_op jit(solution)/shard_map/ppermute | solution.py:121
  754.2 169.9 %reduce-scatter.15.cloned.1.call-start = ((), (), s32[]{:S(2)}) async-start(), calls=%async_computation.13 | async-start | bytes 2359296 | tf_op jit(solution)/shard_map/reduce_scatter | solution.py:804
  780.0 30.4 %collective-permute-start.74 = (bf16[256,2048]{1,0:T(8,128)(2,1)}, bf16[256,2048]{1,0:T(8,128)(2,1)}, u32[]{:S(2)}, u32[]{:S(2)}) collective-permute-start(bf16[256,2048]{1,0:T(8,128)(2,1)} %get-tuple-element.337), channel_id=1, source_target_pairs={{0,4},{4,0},{8,12},{12,8},{16,20},{20,16},{24,28},{28,24},{1,5},{5... | collective-permute-start | bytes 3145736 | tf_op jit(solution)/shard_map/ppermute | solution.py:39
  804.9 49.4 %collective-permute-start.79 = (bf16[1024,512]{1,0:T(8,128)(2,1)}, bf16[1024,512]{1,0:T(8,128)(2,1)}, u32[]{:S(2)}, u32[]{:S(2)}) collective-permute-start(bf16[1024,512]{1,0:T(8,128)(2,1)} %get-tuple-element.203), channel_id=1, source_target_pairs={{16,0},{20,4},{24,8},{28,12},{17,1},{21,5},{25,9},{29,13},{18,2},{... | collective-permute-start | bytes 3145736 | tf_op jit(solution)/shard_map/ppermute | solution.py:773
  810.3 178.2 %reduce-scatter.17.cloned.1.call-start = ((), (), s32[]{:S(2)}) async-start(), calls=%async_computation.14 | async-start | bytes 7077888 | tf_op jit(solution)/shard_map/reduce_scatter | solution.py:804
  885.8 32.7 %collective-permute-start.80 = (bf16[256,2048]{1,0:T(8,128)(2,1)}, bf16[256,2048]{1,0:T(8,128)(2,1)}, u32[]{:S(2)}, u32[]{:S(2)}) collective-permute-start(bf16[256,2048]{1,0:T(8,128)(2,1)} %get-tuple-element.204), channel_id=1, source_target_pairs={{0,1},{4,5},{8,9},{12,13},{16,17},{20,21},{24,25},{28,29}} | collective-permute-start | bytes 3145736 | tf_op jit(solution)/shard_map/ppermute | solution.py:121
  889.0 29.5 %collective-permute-start.81 = (bf16[256,2048]{1,0:T(8,128)(2,1)S(1)}, bf16[256,2048]{1,0:T(8,128)(2,1)}, u32[]{:S(2)}, u32[]{:S(2)}) collective-permute-start(bf16[256,2048]{1,0:T(8,128)(2,1)S(1)} %get-tuple-element.205), channel_id=1, source_target_pairs={{3,2},{7,6},{11,10},{15,14},{19,18},{23,22},{27,26},{31,30}} | collective-permute-start | bytes 3145736 | tf_op jit(solution)/shard_map/ppermute | solution.py:122
  957.0 44.0 %collective-permute-start.90 = (bf16[256,2048]{1,0:T(8,128)(2,1)}, bf16[256,2048]{1,0:T(8,128)(2,1)}, u32[]{:S(2)}, u32[]{:S(2)}) collective-permute-start(bf16[256,2048]{1,0:T(8,128)(2,1)} %add_convert_fusion.2), channel_id=1, source_target_pairs={{0,1},{1,2},{2,3},{4,5},{5,6},{6,7},{8,9},{9,10},{10,11},{12,13},{... | collective-permute-start | bytes 3145736 | tf_op jit(solution)/shard_map/ppermute | solution.py:121
  962.3 38.6 %collective-permute-start.91 = (bf16[256,2048]{1,0:T(8,128)(2,1)}, bf16[256,2048]{1,0:T(8,128)(2,1)}, u32[]{:S(2)}, u32[]{:S(2)}) collective-permute-start(bf16[256,2048]{1,0:T(8,128)(2,1)} %add_convert_fusion.1), channel_id=1, source_target_pairs={{1,0},{2,1},{3,2},{5,4},{6,5},{7,6},{9,8},{10,9},{11,10},{13,12},{... | collective-permute-start | bytes 3145736 | tf_op jit(solution)/shard_map/ppermute | solution.py:122
  (161 other events, 2681.0 us)
Sparse Core Ops, SparseCore 0:
  14.8 59.2 all-gather.3
  80.1 90.3 all-gather.7
  217.5 154.6 all-gather.5
  493.6 93.4 reduce-scatter.6
  610.9 93.5 reduce-scatter.8
  707.5 90.6 reduce-scatter.12
  800.5 77.2 reduce-scatter.10
  881.5 41.8 reduce-scatter.14
  926.7 61.6 reduce-scatter.16

commit v5 on v4

--- a/solution.py
+++ b/solution.py
@@ -498,40 +498,36 @@
 PACK = 4
 
 
-def moe_pack_kernel(core_ref, g_ref, u_ref, d_ref, gain_ref, g_out, u_out, d_out):
+def moe_pack_kernel(turned, core_ref, gain_ref, *refs):
     gain = gain_ref[:, 1:2]
-    span = g_ref.shape[2]
-    for i in range(PACK):
-        here = slice(i * span, (i + 1) * span)
-        g_out[0, :, here] = (g_ref[i].astype(F32) * gain).astype(BF)
-        u_out[0, :, here] = (u_ref[i].astype(F32) * gain).astype(BF)
-        d_out[0, :, here] = d_ref[i].astype(F32).T.astype(BF)
-
-
-def moe_pack(core, gate, up, down, gains):
-    experts, piece, span = gate.shape
+    count = len(refs) // 2
+    for ref, out in zip(refs[:count], refs[count:]):
+        span = out.shape[2] // PACK
+        for i in range(PACK):
+            x = ref[i].astype(F32)
+            out[0, :, i * span : (i + 1) * span] = (x.T if turned else x * gain).astype(BF)
+
+
+def moe_pack(core, weights, gains, turned):
+    experts, rows, cols = weights[0].shape
+    piece, span = (cols, rows) if turned else (rows, cols)
     local = experts // 2
     steps = local // PACK
-    block = pl.BlockSpec((PACK, piece, span), lambda e, c: (e, 0, 0))
     out = pl.BlockSpec((1, piece, PACK * span), lambda e, c: ((e // steps) ^ c[0], 0, e % steps))
     return pl.pallas_call(
-        moe_pack_kernel,
+        functools.partial(moe_pack_kernel, turned),
         grid_spec=pltpu.PrefetchScalarGridSpec(
             num_scalar_prefetch=1,
             grid=(experts // PACK,),
-            in_specs=[
-                block,
-                block,
-                pl.BlockSpec((PACK, span, piece), lambda e, c: (e, 0, 0)),
-                pl.BlockSpec(gains.shape, lambda e, c: (0, 0)),
-            ],
-            out_specs=[out] * 3,
+            in_specs=[pl.BlockSpec(gains.shape, lambda e, c: (0, 0))]
+            + [pl.BlockSpec((PACK, rows, cols), lambda e, c: (e, 0, 0))] * len(weights),
+            out_specs=[out] * len(weights),
         ),
-        out_shape=[jax.ShapeDtypeStruct((2, piece, local * span), BF)] * 3,
+        out_shape=[jax.ShapeDtypeStruct((2, piece, local * span), BF)] * len(weights),
         compiler_params=params(),
-        cost_estimate=cost(1, 12 * gate.size),
+        cost_estimate=cost(1, 4 * len(weights) * weights[0].size),
         name="moe_pack",
-    )(core, gate, up, down, gains)
+    )(core, gains, *weights)
 
 
 def moe_unpack_kernel(core_ref, *refs):
@@ -660,7 +656,8 @@
     lane = jnp.arange(128, dtype=jnp.int32)[None, :]
     router_mat = jnp.where(lane < experts, router_mat, 0)
 
-    packs = moe_pack(core_arg, after(gate_weight, hat_low), up_weight, down_weight, norm_gains)
+    (low_pack,) = moe_pack(core_arg, [after(down_weight, hat_low)], norm_gains, True)
+    packs = moe_pack(core_arg, [after(gate_weight, *steps_one[2]), up_weight], norm_gains, False)
 
     def both_rows(kept, given):
         got = swap_core(given)
@@ -669,7 +666,7 @@
     def over_chips(value):
         return lax.all_gather(value, "fsdp", axis=0, tiled=True, axis_index_groups=groups)
 
-    low_rows = both_rows(packs[2][0], packs[2][1])
+    low_rows = both_rows(low_pack[0], low_pack[1])
     low_mat = over_chips(after(low_rows, attn_mat, *steps_one[2]))
     rows = both_rows(*[jnp.concatenate([packs[0][h], packs[1][h]], axis=1) for h in range(2)])
 

time: 1020 us -> 1020 us (level)
  transfers between devices with their start and end apart: 104 -> 104, of which waited for: 48 -> 47; matrix products, arithmetic and copies ran while one was open for 20% -> 20% of each run, Pallas kernels for 16% -> 16%
where the time goes in v5:
time: 1020 us; the launch traced here: 1010 us
  waiting for transfers between devices  323 us (32%)
  Pallas kernels  236 us (23%)
  starting transfers between devices  171 us (17%)
  matrix products  127 us (12%)
  other arithmetic  100 us (10%)
  local copies, waits for them, and re-layouts  39.1 us (4%)
  between operations  16.1 us (2%)
    ppermute x24, waiting for transfers between devices, line_gather(): lax.ppermute(behind, 'tp', [(i + 1, i) for i in range(count - s)])  140 us
    dot_general x13, matrix products, dot(): return lax.dot_general(a, b, dims, preferred_element_type=F32)  127 us
    pallas_call x4, Pallas kernels, mix(): pl.pallas_call(mix_kernel, grid=(cols // tile,), in_specs=specs, out_spec...  78.4 us
    pallas_call x2, Pallas kernels, hidden(): pl.pallas_call(kernel, grid=(experts,), in_specs=[full, full, mat(0), mat...  71.3 us
    ppermute x9, waiting for transfers between devices, line_scatter(): up = lax.ppermute(send_up, 'tp', [(i, i + 1) for i in range(count - s)])  64.6 us
    ppermute x24, starting transfers between devices, line_gather(): lax.ppermute(ahead, 'tp', [(i, i + 1) for i in range(s - 1, count - 1)])  51.8 us
    ppermute x9, starting transfers between devices, line_scatter(): up = lax.ppermute(send_up, 'tp', [(i, i + 1) for i in range(count - s)])  41.6 us
    ppermute x24, starting transfers between devices, line_gather(): lax.ppermute(behind, 'tp', [(i + 1, i) for i in range(count - s)])  31 us
  transfers between devices with their start and end apart: 104, of which 47 were waited for; matrix products, arithmetic and copies ran while one was open for 20% of the time, Pallas kernels for 16%

profile of v5, /device:TPU:0, one launch (start us, length us, event | category | flops | bytes accessed | tf_op | source)
XLA Modules:
  0.0 1012.1 jit_solution(6423222967458333116)
XLA Ops:
  66.8 10.5 %collective-permute-done.3.refs_1_ = bf16[128,2048]{1,0:T(8,128)(2,1)} collective-permute-done((bf16[128,2048]{1,0:T(8,128)(2,1)}, bf16[128,2048]{1,0:T(8,128)(2,1)}, u32[]{:S(2)}, u32[]{:S(2)}) %collective-permute-start.3) | collective-permute-done | bytes 524320 | tf_op jit(solution)/shard_map/ppermute | solution.py:63
  94.7 9.6 collective-permute-done.4.refs_0_
  108.6 10.0 fusion.2.q_ref.k_ref
  177.2 11.0 %collective-permute-done.25.refs_8_ = bf16[128,2048]{1,0:T(8,128)(2,1)S(1)} collective-permute-done((bf16[128,2048]{1,0:T(8,128)(2,1)S(1)}, bf16[128,2048]{1,0:T(8,128)(2,1)S(1)}, u32[]{:S(2)}, u32[]{:S(2)}) %collective-permute-start.25) | collective-permute-done | bytes 524320 | tf_op jit(solution)/shard_map/ppermute | solution.py:63
  190.2 9.3 collective-permute-done.22.refs_1_
  215.1 11.8 %attend.1 = bf16[1024,512]{1,0:T(8,128)(2,1)} custom-call(s32[1]{0:T(128)} %bitcast.cont_ref, bf16[1024,512]{1,0:T(8,128)(2,1)} %get-tuple-element.129.q_ref, bf16[1024,512]{1,0:T(8,128)(2,1)} %get-tuple-element.130.k_ref, bf16[1024,512]{1,0:T(8,128)(2,1)} %slice.262.v_ref, bf16[1024,512]{1,0:T(8,128)(2,1)} %collective-permute-done.19.kr_ref, ...), custom_call_target="tpu_custom_call" | custom-call | flops 3221225472 | bytes 6291456 | tf_op jit(solution)/shard_map/attend/pallas_call | solution.py:321
  237.3 13.4 %collective-permute-done.29 = bf16[256,2048]{1,0:T(8,128)(2,1)S(1)} collective-permute-done((bf16[256,2048]{1,0:T(8,128)(2,1)S(1)}, bf16[256,2048]{1,0:T(8,128)(2,1)S(1)}, u32[]{:S(2)}, u32[]{:S(2)}) %collective-permute-start.29) | collective-permute-done | bytes 1048608 | tf_op jit(solution)/shard_map/ppermute | solution.py:121
  277.2 11.3 %collective-permute-start.33 = (bf16[256,2048]{1,0:T(8,128)(2,1)}, bf16[256,2048]{1,0:T(8,128)(2,1)}, u32[]{:S(2)}, u32[]{:S(2)}) collective-permute-start(bf16[256,2048]{1,0:T(8,128)(2,1)} %add_convert_fusion.9), channel_id=1, source_target_pairs={{0,1},{1,2},{2,3},{4,5},{5,6},{6,7},{8,9},{9,10},{10,11},{12,13},{... | collective-permute-start | bytes 3145736 | tf_op jit(solution)/shard_map/ppermute | solution.py:121
  401.1 35.7 %hidden.2 = (bf16[2048,2048]{1,0:T(8,128)(2,1)}, bf16[2048,2176]{1,0:T(8,128)(2,1)}, bf16[2048,2048]{1,0:T(8,128)(2,1)}, f32[1024,8]{1,0:T(8,128)}) custom-call(bf16[1024,2048]{1,0:T(8,128)(2,1)} %assemble.6.x_ref, bf16[1024,2048]{1,0:T(8,128)(2,1)} %assemble.5.c_ref, bf16[2048,4096]{1,0:T(8,128)(2,1)} %all-gather.6.cloned.1.call-done.g_ref.u_ref.refs_2_.refs_3_.refs_1_, ...), custom_call_target="tpu_custom_call" | custom-call | flops 25769803776 | bytes 58720256 | tf_op jit(solution)/shard_map/hidden/pallas_call | solution.py:432
  436.8 35.6 %hidden.3 = (bf16[2048,2048]{1,0:T(8,128)(2,1)}, bf16[2048,2176]{1,0:T(8,128)(2,1)}, bf16[2048,2048]{1,0:T(8,128)(2,1)}, f32[1024,8]{1,0:T(8,128)}) custom-call(bf16[1024,2048]{1,0:T(8,128)(2,1)} %collective-permute-done.49.refs_0_, bf16[1024,2048]{1,0:T(8,128)(2,1)} %collective-permute-done.40.refs_1_, ...), custom_call_target="tpu_custom_call", output_to_operand_aliasing={{0}: (6, {}), {1}: (7, {}), {2}: (8, {})} | custom-call | flops 25769803776 | bytes 58720256 | tf_op jit(solution)/shard_map/hidden/pallas_call | solution.py:432
  472.4 22.6 %convolution_convert_fusion.3 = bf16[2048,2048]{1,0:T(8,128)(2,1)} fusion(bf16[2048,2048]{1,0:T(8,128)(2,1)} %get-tuple-element.171.refs_0_, bf16[1024,2048]{1,0:T(8,128)(2,1)} %collective-permute-done.40.refs_1_, bf16[1024,2048]{1,0:T(8,128)(2,1)S(1)} %copy-done.16), kind=kOutput, calls=%fused_computation.6 | convolution fusion | flops 17200840704 | bytes 25165824 | tf_op jit(solution)/shard_map/dot_general | solution.py:24
  499.6 25.7 %mix.4 = bf16[1024,2048]{1,0:T(8,128)(2,1)} custom-call(bf16[2048,2176]{1,0:T(8,128)(2,1)} %maximum_dynamic-update-slice_fusion.refs_0_, bf16[2048,4096]{1,0:T(8,128)(2,1)} %all-gather.6.cloned.1.call-done.g_ref.u_ref.refs_2_.refs_3_.refs_1_, bf16[2048,2048]{1,0:T(8,128)(2,1)} %get-tuple-element.175.refs_2_, ...), custom_call_target="tpu_custom_call" | custom-call | flops 17716740096 | bytes 34340864 | tf_op jit(solution)/shard_map/mix/pallas_call | solution.py:467
  525.4 26.0 %mix.5 = bf16[1024,2048]{1,0:T(8,128)(2,1)} custom-call(bf16[2048,2176]{1,0:T(8,128)(2,1)} %maximum_dynamic-update-slice_fusion.refs_0_, bf16[2048,4096]{1,0:T(8,128)(2,1)} %all-gather.6.cloned.1.call-done.g_ref.u_ref.refs_2_.refs_3_.refs_1_, bf16[2048,2048]{1,0:T(8,128)(2,1)} %get-tuple-element.175.refs_2_, ...), custom_call_target="tpu_custom_call" | custom-call | flops 17716740096 | bytes 34340864 | tf_op jit(solution)/shard_map/mix/pallas_call | solution.py:467
  558.7 26.3 %convolution_convert_fusion = bf16[2048,2176]{1,0:T(8,128)(2,1)} fusion(bf16[2048,2176]{1,0:T(8,128)(2,1)} %maximum_dynamic-update-slice_fusion.refs_0_, bf16[1024,2048]{1,0:T(8,128)(2,1)} %collective-permute-done.49.refs_0_, bf16[1024,2048]{1,0:T(8,128)(2,1)S(1)} %copy-done.17), kind=kOutput, calls=%fused_computation | convolution fusion | flops 18274844672 | bytes 26214400 | tf_op jit(solution)/shard_map/dot_general | solution.py:24
  588.3 23.7 %convolution_convert_fusion.2 = bf16[2048,2048]{1,0:T(8,128)(2,1)} fusion(bf16[2048,2048]{1,0:T(8,128)(2,1)} %get-tuple-element.175.refs_2_, bf16[1024,2048]{1,0:T(8,128)(2,1)} %collective-permute-done.49.refs_0_, bf16[1024,2048]{1,0:T(8,128)(2,1)} %assemble.6.x_ref), kind=kOutput, calls=%fused_computation.5 | convolution fusion | flops 17200840704 | bytes 25165824 | tf_op jit(solution)/shard_map/dot_general | solution.py:24
  616.8 13.3 %mix.7 = bf16[1024,2048]{1,0:T(8,128)(2,1)} custom-call(bf16[2048,2048]{1,0:T(8,128)(2,1)} %get-tuple-element.171.refs_0_, bf16[2048,2048]{1,0:T(8,128)(2,1)} %all-gather.8.cloned.1.call-done.d_ref.refs_4_.refs_1_), custom_call_target="tpu_custom_call" | custom-call | flops 8589934592 | bytes 20971520 | tf_op jit(solution)/shard_map/mix/pallas_call | solution.py:467
  648.7 20.1 %collective-permute-done.58 = bf16[256,2048]{1,0:T(8,128)(2,1)S(1)} collective-permute-done((bf16[256,2048]{1,0:T(8,128)(2,1)S(1)}, bf16[256,2048]{1,0:T(8,128)(2,1)S(1)}, u32[]{:S(2)}, u32[]{:S(2)}) %collective-permute-start.58) | collective-permute-done | bytes 1048608 | tf_op jit(solution)/shard_map/ppermute | solution.py:121
  709.6 13.4 %mix.6 = bf16[1024,2048]{1,0:T(8,128)(2,1)} custom-call(bf16[2048,2048]{1,0:T(8,128)(2,1)} %get-tuple-element.171.refs_0_, bf16[2048,2048]{1,0:T(8,128)(2,1)} %all-gather.8.cloned.1.call-done.d_ref.refs_4_.refs_1_), custom_call_target="tpu_custom_call" | custom-call | flops 8589934592 | bytes 20971520 | tf_op jit(solution)/shard_map/mix/pallas_call | solution.py:467
  759.6 17.8 %attend_back.1 = (f32[1024,512]{1,0:T(8,128)}, f32[1024,512]{1,0:T(8,128)}, f32[1024,512]{1,0:T(8,128)}, bf16[1024,512]{1,0:T(8,128)(2,1)}, bf16[1024,512]{1,0:T(8,128)(2,1)}) custom-call(s32[1]{0:T(128)} %bitcast.cont_ref, bf16[1024,512]{1,0:T(8,128)(2,1)} %get-tuple-element.129.q_ref, bf16[1024,512]{1,0:T(8,128)(2,1)} %get-tuple-element.130.k_ref, ...), custom_call_target="tpu_custom_call" | custom-call | flops 8053063680 | bytes 15728640 | tf_op jit(solution)/shard_map/attend_back/pallas_call | solution.py:382
  779.0 17.6 %reduce-scatter.13.cloned.1.call-done = bf16[512,2176]{1,0:T(8,128)(2,1)} async-done(((bf16[2048,2176]{1,0:T(8,128)(2,1)}), bf16[512,2176]{1,0:T(8,128)(2,1)}) %reduce-scatter.13.cloned.1.call-update) | async-done | bytes 2228240 | tf_op jit(solution)/shard_map/reduce_scatter | solution.py:732
  819.0 11.3 %collective-permute-done.75.dkr_ref = bf16[1024,512]{1,0:T(8,128)(2,1)} collective-permute-done((bf16[1024,512]{1,0:T(8,128)(2,1)}, bf16[1024,512]{1,0:T(8,128)(2,1)}, u32[]{:S(2)}, u32[]{:S(2)}) %collective-permute-start.75) | collective-permute-done | bytes 1048608 | tf_op jit(solution)/shard_map/ppermute | solution.py:770
  861.4 11.2 %fusion.6 = bf16[1024,2048]{1,0:T(8,128)(2,1)} fusion(bf16[2048,2176]{1,0:T(8,128)(2,1)} %all-gather.4.cloned.1.call-done, bf16[1024,512]{1,0:T(8,128)(2,1)S(1)} %copy-done.20, bf16[1024,512]{1,0:T(8,128)(2,1)S(1)} %get-tuple-element.322, bf16[1024,512]{1,0:T(8,128)(2,1)S(1)} %get-tuple-element.321), kind=kOutput, calls=%fused_computation.16 | convolution fusion | flops 6453985280 | bytes 13631488 | tf_op jit(solution)/shard_map/dot_general | solution.py:24
  894.3 18.7 %collective-permute-done.84 = f32[32,128]{1,0:T(8,128)S(1)} collective-permute-done((f32[32,128]{1,0:T(8,128)S(1)}, f32[32,128]{1,0:T(8,128)S(1)}, u32[]{:S(2)}, u32[]{:S(2)}) %collective-permute-start.84) | collective-permute-done | bytes 16416 | tf_op jit(solution)/shard_map/ppermute | solution.py:140
  961.9 24.9 %reduce-scatter.17.cloned.1.call-done = bf16[256,1536]{1,0:T(8,128)(2,1)} async-done(((bf16[2048,1536]{1,0:T(8,128)(2,1)}), bf16[256,1536]{1,0:T(8,128)(2,1)}) %reduce-scatter.17.cloned.1.call-update) | async-done | bytes 786448 | tf_op jit(solution)/shard_map/reduce_scatter | solution.py:801
  (519 shorter events, 565.1 us)
Async XLA Ops:
  7.2 70.1 %all-gather.4.cloned.1.call-start = ((), (), s32[]{:S(2)}) async-start(), calls=%async_computation.6 | async-start | bytes 10027008 | tf_op jit(solution)/shard_map/all_gather | solution.py:637
  14.7 386.4 %all-gather.8.cloned.1.call-start = ((), (), s32[]{:S(2)}) async-start(), calls=%async_computation.8 | async-start | bytes 10485760 | tf_op jit(solution)/shard_map/all_gather | solution.py:667
  21.4 36.9 %collective-permute-start.51 = (bf16[256,2048]{1,0:T(8,128)(2,1)}, bf16[256,2048]{1,0:T(8,128)(2,1)}, u32[]{:S(2)}, u32[]{:S(2)}) collective-permute-start(bf16[256,2048]{1,0:T(8,128)(2,1)} %slice_bitcast_fusion), channel_id=1, source_target_pairs={{0,4},{4,0},{8,12},{12,8},{16,20},{20,16},{24,28},{28,24},{1,5},{5... | collective-permute-start | bytes 3145736 | tf_op jit(solution)/shard_map/ppermute | solution.py:39
  77.4 323.7 %all-gather.6.cloned.1.call-start = ((), (), s32[]{:S(2)}) async-start(), calls=%async_computation.7 | async-start | bytes 20971520 | tf_op jit(solution)/shard_map/all_gather | solution.py:667
  92.7 79.1 %collective-permute-start.50 = (bf16[256,4096]{1,0:T(8,128)(2,1)}, bf16[256,4096]{1,0:T(8,128)(2,1)}, u32[]{:S(2)}, u32[]{:S(2)}) collective-permute-start(bf16[256,4096]{1,0:T(8,128)(2,1)} %pad_maximum_fusion.7), channel_id=1, source_target_pairs={{0,4},{4,0},{8,12},{12,8},{16,20},{20,16},{24,28},{28,24},{1,5},{5... | collective-permute-start | bytes 6291464 | tf_op jit(solution)/shard_map/ppermute | solution.py:39
  135.1 33.2 %collective-permute-start.15 = (bf16[128,2048]{1,0:T(8,128)(2,1)S(1)}, bf16[128,2048]{1,0:T(8,128)(2,1)}, u32[]{:S(2)}, u32[]{:S(2)}) collective-permute-start(bf16[128,2048]{1,0:T(8,128)(2,1)S(1)} %get-tuple-element.127.refs_3_), channel_id=1, source_target_pairs={{0,1},{1,2},{2,3},{4,5},{5,6},{6,7},{8,9},{9,10},{10,11},{12,13},{... | collective-permute-start | bytes 1572872 | tf_op jit(solution)/shard_map/ppermute | solution.py:62
  140.4 30.1 %collective-permute-start.17 = (bf16[128,2048]{1,0:T(8,128)(2,1)S(1)}, bf16[128,2048]{1,0:T(8,128)(2,1)}, u32[]{:S(2)}, u32[]{:S(2)}) collective-permute-start(bf16[128,2048]{1,0:T(8,128)(2,1)S(1)} %get-tuple-element.127.refs_3_), channel_id=1, source_target_pairs={{1,0},{2,1},{3,2},{5,4},{6,5},{7,6},{9,8},{10,9},{11,10},{13,12},{... | collective-permute-start | bytes 1572872 | tf_op jit(solution)/shard_map/ppermute | solution.py:63
  155.6 44.6 %collective-permute-start.20 = (bf16[1024,512]{1,0:T(8,128)(2,1)}, bf16[1024,512]{1,0:T(8,128)(2,1)}, u32[]{:S(2)}, u32[]{:S(2)}) collective-permute-start(bf16[1024,512]{1,0:T(8,128)(2,1)} %slice.262.v_ref), channel_id=1, source_target_pairs={{0,16},{4,20},{8,24},{12,28},{1,17},{5,21},{9,25},{13,29},{2,18},{... | collective-permute-start | bytes 3145736 | tf_op jit(solution)/shard_map/ppermute | solution.py:677
  168.2 38.7 %collective-permute-start.19 = (bf16[1024,512]{1,0:T(8,128)(2,1)}, bf16[1024,512]{1,0:T(8,128)(2,1)}, u32[]{:S(2)}, u32[]{:S(2)}) collective-permute-start(bf16[1024,512]{1,0:T(8,128)(2,1)} %get-tuple-element.130.k_ref), channel_id=1, source_target_pairs={{0,16},{4,20},{8,24},{12,28},{1,17},{5,21},{9,25},{13,29},{2,18},{... | collective-permute-start | bytes 3145736 | tf_op jit(solution)/shard_map/ppermute | solution.py:687
  214.0 374.3 %reduce-scatter.7.cloned.1.call-start = ((), (), s32[]{:S(2)}) async-start(), calls=%async_computation.9 | async-start | bytes 10485760 | tf_op jit(solution)/shard_map/reduce_scatter | solution.py:732
  265.3 81.9 %collective-permute-start.40 = (bf16[1024,2048]{1,0:T(8,128)(2,1)}, bf16[1024,2048]{1,0:T(8,128)(2,1)}, u32[]{:S(2)}, u32[]{:S(2)}) collective-permute-start(bf16[1024,2048]{1,0:T(8,128)(2,1)} %assemble.5.c_ref), channel_id=1, source_target_pairs={{0,4},{4,0},{8,12},{12,8},{16,20},{20,16},{24,28},{28,24},{1,5},{5... | collective-permute-start | bytes 12582920 | tf_op jit(solution)/shard_map/ppermute | solution.py:39
  495.0 258.1 %reduce-scatter.9.cloned.1.call-start = ((), (), s32[]{:S(2)}) async-start(), calls=%async_computation.10 | async-start | bytes 10485760 | tf_op jit(solution)/shard_map/reduce_scatter | solution.py:732
  556.4 28.6 %collective-permute-start.54 = (bf16[256,2048]{1,0:T(8,128)(2,1)}, bf16[256,2048]{1,0:T(8,128)(2,1)S(1)}, u32[]{:S(2)}, u32[]{:S(2)}) collective-permute-start(bf16[256,2048]{1,0:T(8,128)(2,1)} %get-tuple-element.169), channel_id=1, source_target_pairs={{0,1},{4,5},{8,9},{12,13},{16,17},{20,21},{24,25},{28,29}} | collective-permute-start | bytes 3145736 | tf_op jit(solution)/shard_map/ppermute | solution.py:121
  612.0 184.6 %reduce-scatter.13.cloned.1.call-start = ((), (), s32[]{:S(2)}) async-start(), calls=%async_computation.12 | async-start | bytes 11141120 | tf_op jit(solution)/shard_map/reduce_scatter | solution.py:732
  612.6 271.4 %reduce-scatter.11.cloned.1.call-start = ((), (), s32[]{:S(2)}) async-start(), calls=%async_computation.11 | async-start | bytes 5242880 | tf_op jit(solution)/shard_map/reduce_scatter | solution.py:762
  630.1 102.0 %collective-permute-start.53 = (bf16[1024,2048]{1,0:T(8,128)(2,1)}, bf16[1024,2048]{1,0:T(8,128)(2,1)}, u32[]{:S(2)}, u32[]{:S(2)}) collective-permute-start(bf16[1024,2048]{1,0:T(8,128)(2,1)} %mix.7), channel_id=1, source_target_pairs={{0,4},{4,0},{8,12},{12,8},{16,20},{20,16},{24,28},{28,24},{1,5},{5... | collective-permute-start | bytes 12582920 | tf_op jit(solution)/shard_map/ppermute | solution.py:39
  753.1 169.3 %reduce-scatter.15.cloned.1.call-start = ((), (), s32[]{:S(2)}) async-start(), calls=%async_computation.13 | async-start | bytes 2359296 | tf_op jit(solution)/shard_map/reduce_scatter | solution.py:801
  779.0 29.7 %collective-permute-start.74 = (bf16[256,2048]{1,0:T(8,128)(2,1)}, bf16[256,2048]{1,0:T(8,128)(2,1)}, u32[]{:S(2)}, u32[]{:S(2)}) collective-permute-start(bf16[256,2048]{1,0:T(8,128)(2,1)} %get-tuple-element.337), channel_id=1, source_target_pairs={{0,4},{4,0},{8,12},{12,8},{16,20},{20,16},{24,28},{28,24},{1,5},{5... | collective-permute-start | bytes 3145736 | tf_op jit(solution)/shard_map/ppermute | solution.py:39
  803.2 49.4 %collective-permute-start.79 = (bf16[1024,512]{1,0:T(8,128)(2,1)}, bf16[1024,512]{1,0:T(8,128)(2,1)}, u32[]{:S(2)}, u32[]{:S(2)}) collective-permute-start(bf16[1024,512]{1,0:T(8,128)(2,1)} %get-tuple-element.203), channel_id=1, source_target_pairs={{16,0},{20,4},{24,8},{28,12},{17,1},{21,5},{25,9},{29,13},{18,2},{... | collective-permute-start | bytes 3145736 | tf_op jit(solution)/shard_map/ppermute | solution.py:770
  808.6 178.1 %reduce-scatter.17.cloned.1.call-start = ((), (), s32[]{:S(2)}) async-start(), calls=%async_computation.14 | async-start | bytes 7077888 | tf_op jit(solution)/shard_map/reduce_scatter | solution.py:801
  884.0 32.8 %collective-permute-start.80 = (bf16[256,2048]{1,0:T(8,128)(2,1)}, bf16[256,2048]{1,0:T(8,128)(2,1)}, u32[]{:S(2)}, u32[]{:S(2)}) collective-permute-start(bf16[256,2048]{1,0:T(8,128)(2,1)} %get-tuple-element.204), channel_id=1, source_target_pairs={{0,1},{4,5},{8,9},{12,13},{16,17},{20,21},{24,25},{28,29}} | collective-permute-start | bytes 3145736 | tf_op jit(solution)/shard_map/ppermute | solution.py:121
  887.2 29.6 %collective-permute-start.81 = (bf16[256,2048]{1,0:T(8,128)(2,1)S(1)}, bf16[256,2048]{1,0:T(8,128)(2,1)}, u32[]{:S(2)}, u32[]{:S(2)}) collective-permute-start(bf16[256,2048]{1,0:T(8,128)(2,1)S(1)} %get-tuple-element.205), channel_id=1, source_target_pairs={{3,2},{7,6},{11,10},{15,14},{19,18},{23,22},{27,26},{31,30}} | collective-permute-start | bytes 3145736 | tf_op jit(solution)/shard_map/ppermute | solution.py:122
  955.2 44.0 %collective-permute-start.90 = (bf16[256,2048]{1,0:T(8,128)(2,1)}, bf16[256,2048]{1,0:T(8,128)(2,1)}, u32[]{:S(2)}, u32[]{:S(2)}) collective-permute-start(bf16[256,2048]{1,0:T(8,128)(2,1)} %add_convert_fusion.2), channel_id=1, source_target_pairs={{0,1},{1,2},{2,3},{4,5},{5,6},{6,7},{8,9},{9,10},{10,11},{12,13},{... | collective-permute-start | bytes 3145736 | tf_op jit(solution)/shard_map/ppermute | solution.py:121
  960.6 38.6 %collective-permute-start.91 = (bf16[256,2048]{1,0:T(8,128)(2,1)}, bf16[256,2048]{1,0:T(8,128)(2,1)}, u32[]{:S(2)}, u32[]{:S(2)}) collective-permute-start(bf16[256,2048]{1,0:T(8,128)(2,1)} %add_convert_fusion.1), channel_id=1, source_target_pairs={{1,0},{2,1},{3,2},{5,4},{6,5},{7,6},{9,8},{10,9},{11,10},{13,12},{... | collective-permute-start | bytes 3145736 | tf_op jit(solution)/shard_map/ppermute | solution.py:122
  (160 other events, 2801.1 us)
Sparse Core Ops, SparseCore 0:
  14.8 59.2 all-gather.3
  77.5 91.2 all-gather.7
  214.1 154.6 all-gather.5
  495.1 90.2 reduce-scatter.6
  612.1 90.6 reduce-scatter.8
  705.8 90.7 reduce-scatter.12
  798.8 77.2 reduce-scatter.10
  879.8 41.7 reduce-scatter.14
  925.0 61.7 reduce-scatter.16
